TPU v7x, 32 devices: a whole 2x2x4 slice. The times are simulated.
32 devices in a mesh: field: 2 (over y), ccd: 16 (over z, x, core).
Axes of the slice: x: 2, y: 2, z: 4, core: 2. Of those that a mesh axis runs over, the one named last changes fastest.
Arguments:
- exposures: float32 [2, 4096, 1024], P(None, ('field', 'ccd')), parts along dimension 1, may hold values from -100 to 100
- lanczos_shift: int32 [2, 32, 2], P(None, ('field', 'ccd')), parts along dimension 1, may hold values from -2 to 2
- lanczos_frac: float32 [2, 32, 2], P(None, ('field', 'ccd')), parts along dimension 1, may hold values from 0 to 1
- margin_patch: int32 [32, 32, 1], P('field'), parts along dimension 0, may hold values from 0 to 15; in each aligned block of 32 rows (0 to 31, 32 to 63, ..., all dimensions but the last counted through in order) at most 4 rows name the same one
- margin_slot: int32 [32, 32], P('field'), parts along dimension 0, may hold values from 0 to 31
Outputs:
- difference: float32 [4096, 1024], P(('field', 'ccd')), parts along dimension 0
There are 2 independent parts, one for each index of `field`. A program takes and returns all parts, laid end to end along the dimension named above; each array names one. Nothing has to cross between parts.
Inputs may be any that keep to these rules, and one draw needn't show every extreme that they name: `margin_patch`: no CCD has more than 4 of its blocks on one patch, and some CCD has exactly 4 on one patch; every patch is intersected by some block.
All inputs are finite; a program needn't handle non-finite values.
Results may differ from a plain program's by a relative error of at most 0.0003.
Values sent between devices are 32-bit elements; how exact they have to be, the bound alone decides.
No kernel may reach another device: no remote copies, remote signals or barrier semaphores. Data moves between devices by JAX's collectives and lax.ppermute only.
A program may use at most 128 MiB of HBM per device.

v0:
```python
import functools

import jax
import jax.numpy as jnp
import numpy as np
from jax import lax
from jax.experimental import pallas as pl
from jax.experimental.pallas import tpu as pltpu
from jax.sharding import PartitionSpec as P


BR = 32
BC = 128
KSIDE = 5
KB = 25
NB = 32
REACH = KSIDE // 2
SUB = 8
LANES = 128
TAP_LOW, TAP_HIGH = -4, 5
TAPS = tuple(range(TAP_LOW, TAP_HIGH + 1))
LAGS = tuple(range(-(KSIDE - 1), KSIDE))
PRODUCTS = tuple(
    (down, lag) for down in range(KSIDE) for lag in (range(KSIDE) if down == 0 else LAGS)
)
EDGE_ROWS = ((0, (0, 1)), (1, (0,)), (-2, (0, 1)), (-1, (0,)))
EDGES = tuple(
    (row, down, lag) for row, downs in EDGE_ROWS for down, lag in PRODUCTS if down in downs
)
MAX_PERMUTES = 32
UNROLL = 4
RHS_LANE = KB


HIGHEST = lax.Precision.HIGHEST
SMEM = pl.BlockSpec(memory_space=pltpu.SMEM)
VMEM = pl.BlockSpec(memory_space=pltpu.VMEM)


def mm(a, b, contract=((1,), (0,))):
    return lax.dot_general(
        a, b, (contract, ((), ())), precision=HIGHEST, preferred_element_type=jnp.float32
    )


def call(kernel, out_shape, in_specs, scratch, flops, moved, grid=()):
    many = isinstance(out_shape, (list, tuple))
    return pl.pallas_call(
        kernel,
        out_shape=out_shape,
        grid=grid,
        in_specs=in_specs,
        out_specs=[VMEM] * len(out_shape) if many else VMEM,
        scratch_shapes=scratch,
        cost_estimate=pl.CostEstimate(flops=flops, bytes_accessed=moved, transcendentals=0),
    )


def f32(*shape):
    return jax.ShapeDtypeStruct(shape, jnp.float32)


def lane_ids():
    return lax.broadcasted_iota(jnp.int32, (SUB, LANES), 1)


def shifted(parts, by, lane):
    if by == 0:
        return list(parts)
    turned = [pltpu.roll(part, by % LANES, 1) for part in parts]
    zero = jnp.zeros_like(parts[0])
    out = []
    for j in range(len(parts)):
        beside = j - 1 if by > 0 else j + 1
        other = turned[beside] if 0 <= beside < len(parts) else zero
        keep = lane >= by if by > 0 else lane < LANES + by
        out.append(jnp.where(keep, turned[j], other))
    return out


def sinc(t):
    scaled = jnp.float32(np.pi) * t
    safe = jnp.where(t == 0.0, jnp.float32(1.0), scaled)
    return jnp.where(t == 0.0, jnp.float32(1.0), jnp.sin(safe) / safe)


def tap_weights(shift, frac, lane):
    t = (lane + TAP_LOW).astype(jnp.float32) - shift.astype(jnp.float32) - frac
    w = jnp.where(jnp.abs(t) < 3.0, sinc(t) * sinc(t / 3.0), 0.0)
    return [jnp.broadcast_to(w[:, k : k + 1], (SUB, LANES)) for k in range(len(TAPS))]


def warp_kernel(
    visit, devices, cap, paired, own_ref, tgt_ref, shift_ref, frac_ref, x_ref, *refs
):
    outs, (mid, blocks, inv, cnt) = refs[:-4], refs[-4:]
    rows, columns = x_ref.shape
    slabs, tiles = columns // LANES, rows // SUB
    own = own_ref[0]
    lane = lane_ids()

    for e in range(devices * cap):
        inv[e] = 0
    for p in range(devices):
        cnt[p] = 0

    def book(b):
        p = tgt_ref[own, b]
        c = cnt[p]
        cnt[p] = c + 1
        k = jnp.bitwise_xor(p, own) if paired else p
        inv[k * cap + jnp.minimum(c, cap - 1)] = b

    col_w = tap_weights(shift_ref[visit, 0, 1], frac_ref[visit, 0, 1], lane)
    row_w = tap_weights(shift_ref[visit, 0, 0], frac_ref[visit, 0, 0], lane)
    for j in range(slabs):
        mid[j, 0:SUB, :] = jnp.zeros((SUB, LANES), jnp.float32)
        mid[j, SUB + rows :, :] = jnp.zeros((SUB, LANES), jnp.float32)

    @pl.loop(0, tiles, unroll=UNROLL)
    def _(t):
        for b in range(NB // tiles):
            book(t * (NB // tiles) + b)
        at = pl.multiple_of(t * SUB, SUB)
        parts = [x_ref[pl.ds(at, SUB), j * LANES : (j + 1) * LANES] for j in range(slabs)]
        total = [jnp.zeros((SUB, LANES), jnp.float32)] * slabs
        for n, d in enumerate(TAPS):
            moved = shifted(parts, -d, lane)
            total = [a + col_w[n] * m for a, m in zip(total, moved)]
        for j in range(slabs):
            mid[j, pl.ds(at + SUB, SUB), :] = total[j]

    @pl.loop(0, slabs)
    def _(j):
        for t in range(tiles):
            first = SUB + t * SUB
            total = jnp.zeros((SUB, LANES), jnp.float32)
            for n, d in enumerate(TAPS):
                total = total + row_w[n] * mid[j, first + d : first + d + SUB, :]
            inner = (t * SUB) % BR
            blocks[(t * SUB) // BR * slabs + j, inner : inner + SUB, :] = total

    if paired:
        for k in range(devices):
            for r in range(cap):
                outs[k][r] = blocks[inv[k * cap + r]]
    else:

        @pl.loop(0, devices * cap)
        def _(e):
            outs[0][e] = blocks[inv[e]]


def sum_blocks(devices, cap, paired, own, table_ref, ins, acc):
    acc[...] = jnp.zeros_like(acc)
    if paired:
        for k in range(devices):
            for r in range(cap):
                slot = table_ref[jnp.bitwise_xor(own, k) * cap + r]
                acc[slot] = acc[slot] + ins[k][r]
    else:

        @pl.loop(0, devices * cap)
        def _(e):
            slot = table_ref[e]
            acc[slot] = acc[slot] + ins[0][e]


def template_kernel(devices, cap, paired, own_ref, table_ref, *refs):
    ins, (out, top, bottom, acc) = refs[:-4], refs[-4:]
    slabs, _, _ = out.shape
    sum_blocks(devices, cap, paired, own_ref[0], table_ref, ins, acc)
    for s in range(NB):
        out[s % slabs, s // slabs * BR : (s // slabs + 1) * BR, :] = acc[s]
    for j in range(slabs):
        top[j] = acc[j, 0:SUB, :]
        bottom[j] = acc[NB - slabs + j, BR - SUB : BR, :]


def gram_kernel(
    ends_ref, t_ref, above_ref, below_ref, coef_ref, ext_ref, gram_ref, lagged, gen, spec
):
    slabs, rows, _ = t_ref.shape
    tiles = rows // SUB
    lane = lane_ids()
    sub = lax.broadcasted_iota(jnp.int32, (SUB, LANES), 0)

    @pl.loop(0, tiles, unroll=UNROLL)
    def _(t):
        at = pl.ds(pl.multiple_of(t * SUB, SUB), SUB)
        parts = [t_ref[j, at, :] for j in range(slabs)]
        for j in range(slabs):
            ext_ref[j, pl.ds(pl.multiple_of(t * SUB + SUB, SUB), SUB), :] = parts[j]
        for n, lag in enumerate(LAGS):
            for j, moved in enumerate(shifted(parts, lag, lane)):
                lagged[n, j, at, :] = moved

    for j in range(slabs):
        ext_ref[j, 0:SUB, :] = above_ref[j]
        ext_ref[j, SUB + rows :, :] = below_ref[j]

    gen[...] = jnp.zeros_like(gen)
    spec[...] = jnp.zeros_like(spec)

    @pl.loop(0, slabs)
    def _(j):
        def firsts(t):
            return [lagged[n, j, t * SUB : (t + 1) * SUB, :] for n in range(len(LAGS))]

        def second(t, down):
            base = SUB + t * SUB + down
            return ext_ref[j, base : base + SUB, :]

        sums = [None] * len(PRODUCTS)
        for t in range(tiles):
            first = firsts(t)
            moved = [second(t, down) for down in range(KSIDE)]
            for n, (down, lag) in enumerate(PRODUCTS):
                term = first[lag + KSIDE - 1] * moved[down]
                sums[n] = term if sums[n] is None else sums[n] + term
        edge = ((j == 0) & (lane < REACH)) | ((j == slabs - 1) & (lane >= LANES - REACH))
        for n in range(len(PRODUCTS)):
            gen[n] = gen[n] + jnp.where(edge, 0.0, sums[n])
            spec[n] = spec[n] + jnp.where(edge, sums[n], 0.0)
        for m, (row, down, lag) in enumerate(EDGES):
            n = len(PRODUCTS) + m
            t = 0 if row >= 0 else tiles - 1
            here = (sub == row % SUB) & (ends_ref[0 if row >= 0 else 1] > 0)
            term = lagged[lag + KSIDE - 1, j, t * SUB : (t + 1) * SUB, :] * second(t, down)
            term = jnp.where(here, term, 0.0)
            gen[n] = gen[n] + jnp.where(edge, 0.0, term)
            spec[n] = spec[n] + jnp.where(edge, term, 0.0)

    src = lax.broadcasted_iota(jnp.int32, (LANES, LANES), 0)
    q2 = lax.rem(lax.broadcasted_iota(jnp.int32, (LANES, LANES), 1), KSIDE)
    late = (src >= REACH) & (q2 - REACH >= src - (LANES - 1))
    inside = jnp.where(((src < REACH) & (q2 - REACH <= src)) | late, 1.0, 0.0)
    data = mm(jnp.sum(gen[...], axis=1), jnp.ones((LANES, LANES), jnp.float32))
    data = data + mm(jnp.sum(spec[...], axis=1), inside)
    gram_ref[...] = jnp.zeros_like(gram_ref)
    for i in range(KB):
        gram_ref[i : i + 1, :] = jnp.sum(coef_ref[i] * data, axis=0, keepdims=True)
    total = gram_ref[...]
    size = total.shape[0]
    below = jnp.zeros((LANES - size, LANES), jnp.float32)
    flipped = jnp.transpose(jnp.concatenate([total, below], axis=0))[:size]
    row = lax.broadcasted_iota(jnp.int32, (size, LANES), 0)
    column = lax.broadcasted_iota(jnp.int32, (size, LANES), 1)
    gram_ref[...] = total + jnp.where(row == column, 0.0, flipped)


def science_kernel(devices, cap, paired, own_ref, table_ref, ext_ref, gram_ref, *refs):
    ins, (out, fit_ref, acc, moved, sums_ref) = refs[:-5], refs[-5:]
    slabs, rows, _ = out.shape
    lane = lane_ids()
    sum_blocks(devices, cap, paired, own_ref[0], table_ref, ins, acc)

    for band in range(rows // BR):

        @pl.loop(0, BR // SUB, unroll=UNROLL)
        def _(t):
            at = pl.ds(pl.multiple_of(t * SUB, SUB), SUB)
            to = pl.ds(pl.multiple_of(band * BR + t * SUB, SUB), SUB)
            parts = [acc[band * slabs + j, at, :] for j in range(slabs)]
            for j in range(slabs):
                out[j, to, :] = parts[j]
            for q in range(KSIDE):
                for j, part in enumerate(shifted(parts, q - REACH, lane)):
                    moved[q, j, to, :] = part

    def slab(j, sums):
        sums = list(sums)
        for t in range(rows // SUB):
            base = SUB + t * SUB - REACH
            seconds = [moved[q, j, t * SUB : (t + 1) * SUB, :] for q in range(KSIDE)]
            for r in range(KSIDE):
                first = ext_ref[j, base + r : base + r + SUB, :]
                for q in range(KSIDE):
                    sums[r * KSIDE + q] = sums[r * KSIDE + q] + first * seconds[q]
        return tuple(sums)

    sums = lax.fori_loop(0, slabs, slab, (jnp.zeros((SUB, LANES), jnp.float32),) * KB)
    sums_ref[...] = jnp.zeros_like(sums_ref)
    for i in range(KB):
        sums_ref[i : i + 1, :] = jnp.sum(sums[i], axis=0, keepdims=True)
    rhs = jnp.sum(sums_ref[...], axis=1, keepdims=True)
    size = gram_ref.shape[0]
    column = lax.broadcasted_iota(jnp.int32, (size, LANES), 1)
    joined = jnp.where(column == RHS_LANE, rhs, gram_ref[...])
    packed = joined[0:SUB]
    for a in range(1, size // SUB):
        packed = packed + pltpu.roll(joined[a * SUB : (a + 1) * SUB], a * size, 1)
    for k in range(devices):
        fit_ref[k] = packed


def solved(packed, size):
    parts = [packed] + [
        pltpu.roll(packed, LANES - a * size, 1) for a in range(1, size // SUB)
    ]
    work = jnp.concatenate(parts, axis=0)
    row = lax.broadcasted_iota(jnp.int32, (size, LANES), 0)
    lane = lax.broadcasted_iota(jnp.int32, (size, LANES), 1)
    diagonal = (row == lane) & (row < KB)
    trace = jnp.sum(jnp.where(diagonal, work, 0.0), axis=(0, 1), keepdims=True)
    ridge = 0.001 * trace / KB + 1.0
    work = jnp.where(lane < size, jnp.where(diagonal, work + ridge, work), 0.0)
    for i in range(KB):
        pivot = work[i : i + 1, :] / work[i : i + 1, i : i + 1]
        work = jnp.where(row == i, pivot, work - work[:, i : i + 1] * pivot)
    return work[:, RHS_LANE : RHS_LANE + 1]


def difference_kernel(fit_ref, ext_ref, sci_ref, out_ref, rowed):
    slabs, rows, _ = sci_ref.shape
    lane = lane_ids()
    shared = fit_ref[0]
    for k in range(1, fit_ref.shape[0]):
        shared = shared + fit_ref[k]
    kernel = solved(shared, NB)
    taps = [jnp.broadcast_to(kernel[i : i + 1, :], (SUB, LANES)) for i in range(KB)]

    @pl.loop(0, slabs)
    def _(j):
        for t in range(rows // SUB):
            base = SUB + t * SUB - REACH
            sums = [None] * KSIDE
            for r in range(KSIDE):
                part = ext_ref[j, base + r : base + r + SUB, :]
                for q in range(KSIDE):
                    term = taps[r * KSIDE + q] * part
                    sums[q] = term if sums[q] is None else sums[q] + term
            for q in range(KSIDE):
                rowed[q, j, t * SUB : (t + 1) * SUB, :] = sums[q]

    @pl.loop(0, rows // SUB, unroll=UNROLL)
    def _(t):
        at = pl.ds(pl.multiple_of(t * SUB, SUB), SUB)
        total = [jnp.zeros((SUB, LANES), jnp.float32)] * slabs
        for q in range(KSIDE):
            parts = [rowed[q, j, at, :] for j in range(slabs)]
            total = [a + m for a, m in zip(total, shifted(parts, REACH - q, lane))]
        for j in range(slabs):
            out_ref[at, j * LANES : (j + 1) * LANES] = sci_ref[j, at, :] - total[j]


def by_permutes(devices):
    return devices <= MAX_PERMUTES and devices & (devices - 1) == 0


def gram_table():
    count = -(-(len(PRODUCTS) + len(EDGES)) // SUB) * SUB
    coef = np.zeros((KB, count, LANES), np.float32)
    left_out = {0: (-2, -1), 1: (-1,), 2: (), 3: (0,), 4: (0, 1)}
    for r in range(KSIDE):
        for q in range(KSIDE):
            for n, (row, down, lag) in enumerate([(None, *p) for p in PRODUCTS] + list(EDGES)):
                if r + down < KSIDE and 0 <= q + lag < KSIDE:
                    column = (r + down) * KSIDE + q + lag
                    if row is None:
                        coef[r * KSIDE + q, n, column] = 1.0
                    elif row in left_out[r]:
                        coef[r * KSIDE + q, n, column] = -1.0
    return count, coef


def body(exposures, lanczos_shift, lanczos_frac, margin_patch, margin_slot):
    rows, columns = exposures.shape[1], exposures.shape[2]
    slabs = columns // LANES
    devices = lax.axis_size("ccd")
    owner = lax.axis_index("ccd")
    cap = max(2, 2 * NB // devices)
    paired = by_permutes(devices)
    own = owner.astype(jnp.int32).reshape(1)
    targets = margin_patch[:, :, 0]

    pixels = rows * columns

    def warped(visit, paired):
        out = call(
            functools.partial(warp_kernel, visit, devices, cap, paired),
            [f32(cap, BR, BC)] * devices if paired else [f32(devices * cap, BR, BC)],
            [SMEM, SMEM, SMEM, SMEM, pl.BlockSpec((None, rows, columns), lambda i: (visit, 0, 0))],
            [
                pltpu.VMEM((slabs, rows + 2 * SUB, LANES), jnp.float32),
                pltpu.VMEM((NB, BR, BC), jnp.float32),
                pltpu.SMEM((devices * cap,), jnp.int32),
                pltpu.SMEM((devices,), jnp.int32),
            ],
            40 * pixels,
            4 * pixels * 3,
            (1,),
        )(own, targets, lanczos_shift, lanczos_frac, exposures)
        return out

    def exchanged(chunks):
        if len(chunks) == 1:
            return [lax.all_to_all(chunks[0], "ccd", split_axis=0, concat_axis=0, tiled=True)]
        moved = [chunks[0]]
        for k in range(1, devices):
            moved.append(
                lax.ppermute(chunks[k], "ccd", [(i, i ^ k) for i in range(devices)])
            )
        return moved

    template_chunks = warped(0, False)
    science_chunks = warped(1, paired)
    template_in = exchanged(template_chunks)
    science_in = exchanged(science_chunks)

    block_ids = jnp.arange(NB)
    earlier = block_ids[None, :] < block_ids[:, None]
    same = targets[:, :, None] == targets[:, None, :]
    order = jnp.sum(same & earlier[None], axis=2)
    arrives = (targets == owner)[:, None, :] & (order[:, None, :] == jnp.arange(cap)[None, :, None])
    table = jnp.where(
        jnp.any(arrives, axis=2), jnp.sum(jnp.where(arrives, margin_slot[:, None, :], 0), axis=2), NB
    ).reshape(-1).astype(jnp.int32)

    slab_shape = f32(slabs, rows, LANES)
    strip = f32(slabs, SUB, LANES)
    sums = pltpu.VMEM((NB + 1, BR, BC), jnp.float32)
    template, top, bottom = call(
        functools.partial(template_kernel, devices, cap, False),
        [slab_shape, strip, strip],
        [SMEM, SMEM, VMEM],
        [sums],
        pixels * 2,
        pixels * 12,
    )(own, table, *template_in)
    ends = devices - 1
    above = lax.ppermute(bottom, "ccd", [(i, i + 1) for i in range(ends)])
    below = lax.ppermute(top, "ccd", [(i + 1, i) for i in range(ends)])

    size = NB
    count, coef = gram_table()
    at_ends = jnp.stack([owner == 0, owner == devices - 1]).astype(jnp.int32)
    extended, gram = call(
        gram_kernel,
        [f32(slabs, rows + 2 * SUB, LANES), f32(size, LANES)],
        [SMEM] + [VMEM] * 4,
        [
            pltpu.VMEM((len(LAGS), slabs, rows, LANES), jnp.float32),
            pltpu.VMEM((count, SUB, LANES), jnp.float32),
            pltpu.VMEM((count, SUB, LANES), jnp.float32),
        ],
        pixels * 2 * len(PRODUCTS),
        pixels * 8,
    )(at_ends, template, above, below, jnp.asarray(coef))

    science, fit = call(
        functools.partial(science_kernel, devices, cap, paired),
        [slab_shape, f32(devices, SUB, LANES)],
        [SMEM, SMEM, VMEM, VMEM] + [VMEM] * len(science_in),
        [
            sums,
            pltpu.VMEM((KSIDE, slabs, rows, LANES), jnp.float32),
            pltpu.VMEM((size, LANES), jnp.float32),
        ],
        pixels * 2 * KB,
        pixels * 16,
    )(own, table, extended, gram, *science_in)
    fit = lax.all_to_all(fit, "ccd", split_axis=0, concat_axis=0, tiled=True)

    return call(
        difference_kernel,
        f32(rows, columns),
        [VMEM] * 3,
        [pltpu.VMEM((KSIDE, slabs, rows, LANES), jnp.float32)],
        pixels * 2 * KB,
        pixels * 12,
    )(fit, extended, science)


def solution(mesh):
    placed = (
        P(None, ("field", "ccd"), None),
        P(None, ("field", "ccd"), None),
        P(None, ("field", "ccd"), None),
        P("field", None, None),
        P("field", None),
    )
    return jax.shard_map(
        body, mesh=mesh, in_specs=placed, out_specs=P(("field", "ccd"), None), check_vma=False
    )
```

profile of v0, /device:TPU:0, one launch (start us, length us, event | category | flops | bytes accessed | tf_op | source)
XLA Modules:
  0.0 90.3 jit_solution(2672808236363629328)
XLA Ops:
  0.0 4.5 %shard_map.64 = f32[64,32,128]{2,1,0:T(8,128)} custom-call(s32[1]{0:T(128)} %bitcast.own_ref, s32[16,32]{1,0:T(8,128)} %bitcast.4, s32[2,1,2]{2,1,0:T(1,128)} %shift_ref.3, f32[2,1,2]{2,1,0:T(1,128)} %frac_ref.3, f32[2,128,1024]{2,1,0:T(8,128)} %x_ref.3), custom_call_target="tpu_custom_call" | custom-call | flops 5242880 | bytes 1572864 | tf_op jit(solution)/shard_map/pallas_call | solution.py:380
  4.5 7.4 %all-to-all-start = ((f32[64,32,128]{2,1,0:T(8,128)}), f32[64,32,128]{2,1,0:T(8,128)S(1)}, u32[]{:S(2)}, u32[]{:S(2)}) async-start(f32[64,32,128]{2,1,0:T(8,128)} %shard_map.64), calls=%async_computation | async-start | bytes 2097152 | tf_op jit(solution)/shard_map/all_to_all | solution.py:398
  11.9 4.2 %shard_map.67 = (f32[4,32,128]{2,1,0:T(8,128)}, f32[4,32,128]{2,1,0:T(8,128)}, f32[4,32,128]{2,1,0:T(8,128)}, f32[4,32,128]{2,1,0:T(8,128)}, f32[4,32,128]{2,1,0...) custom-call(s32[1]{0:T(128)} %bitcast.own_ref, ...), custom_call_target="tpu_custom_call" | custom-call | flops 5242880 | bytes 1572864 | tf_op jit(solution)/shard_map/pallas_call | solution.py:380
  16.1 0.4 collective-permute-start.2
  16.5 1.6 %collective-permute-start.3 = (f32[4,32,128]{2,1,0:T(8,128)}, f32[4,32,128]{2,1,0:T(8,128)S(1)}, u32[]{:S(2)}, u32[]{:S(2)}) collective-permute-start(f32[4,32,128]{2,1,0:T(8,128)} %get-tuple-element.35), channel_id=1, source_target_pairs={{0,2},{1,3},{2,0},{3,1},{4,6},{5,7},{6,4},{7,5},{8,10},{9,11},{10,... | collective-permute-start | bytes 196616 | tf_op jit(solution)/shard_map/ppermute | solution.py:402
  18.2 0.0 collective-permute-start.4
  18.2 1.7 %collective-permute-start.5 = (f32[4,32,128]{2,1,0:T(8,128)}, f32[4,32,128]{2,1,0:T(8,128)S(1)}, u32[]{:S(2)}, u32[]{:S(2)}) collective-permute-start(f32[4,32,128]{2,1,0:T(8,128)} %get-tuple-element.37), channel_id=1, source_target_pairs={{0,4},{1,5},{2,6},{3,7},{4,0},{5,1},{6,2},{7,3},{8,12},{9,13},{10,... | collective-permute-start | bytes 196616 | tf_op jit(solution)/shard_map/ppermute | solution.py:402
  19.9 0.1 collective-permute-start.6
  20.1 0.5 convert_reduce_fusion
  20.5 0.0 copy-start.19
  20.5 0.7 copy-done.19
  21.2 0.1 select_reduce_fusion
  21.4 0.2 fusion.1
  21.5 0.0 collective-permute-done.2.refs_1_
  21.5 2.6 %collective-permute-start.7 = (f32[4,32,128]{2,1,0:T(8,128)}, f32[4,32,128]{2,1,0:T(8,128)S(1)}, u32[]{:S(2)}, u32[]{:S(2)}) collective-permute-start(f32[4,32,128]{2,1,0:T(8,128)} %get-tuple-element.39), channel_id=1, source_target_pairs={{0,6},{1,7},{2,4},{3,5},{4,2},{5,3},{6,0},{7,1},{8,14},{9,15},{10,... | collective-permute-start | bytes 196616 | tf_op jit(solution)/shard_map/ppermute | solution.py:402
  24.1 0.0 collective-permute-done.3.refs_2_
  24.1 0.3 collective-permute-start.8
  24.4 0.6 collective-permute-done.4.refs_3_
  25.0 1.8 %collective-permute-start.9 = (f32[4,32,128]{2,1,0:T(8,128)}, f32[4,32,128]{2,1,0:T(8,128)S(1)}, u32[]{:S(2)}, u32[]{:S(2)}) collective-permute-start(f32[4,32,128]{2,1,0:T(8,128)} %get-tuple-element.41), channel_id=1, source_target_pairs={{0,8},{1,9},{2,10},{3,11},{4,12},{5,13},{6,14},{7,15},{8,0},{9,1},... | collective-permute-start | bytes 196616 | tf_op jit(solution)/shard_map/ppermute | solution.py:402
  26.8 4.9 %collective-permute-done.5.refs_4_ = f32[4,32,128]{2,1,0:T(8,128)S(1)} collective-permute-done((f32[4,32,128]{2,1,0:T(8,128)}, f32[4,32,128]{2,1,0:T(8,128)S(1)}, u32[]{:S(2)}, u32[]{:S(2)}) %collective-permute-start.5) | collective-permute-done | bytes 65568 | tf_op jit(solution)/shard_map/ppermute | solution.py:402
  31.7 3.2 %collective-permute-start.10 = (f32[4,32,128]{2,1,0:T(8,128)}, f32[4,32,128]{2,1,0:T(8,128)S(1)}, u32[]{:S(2)}, u32[]{:S(2)}) collective-permute-start(f32[4,32,128]{2,1,0:T(8,128)} %get-tuple-element.42), channel_id=1, source_target_pairs={{0,9},{1,8},{2,11},{3,10},{4,13},{5,12},{6,15},{7,14},{8,1},{9,0},... | collective-permute-start | bytes 196616 | tf_op jit(solution)/shard_map/ppermute | solution.py:402
  34.9 0.0 collective-permute-done.6.refs_5_
  34.9 2.6 %collective-permute-start.11 = (f32[4,32,128]{2,1,0:T(8,128)}, f32[4,32,128]{2,1,0:T(8,128)S(1)}, u32[]{:S(2)}, u32[]{:S(2)}) collective-permute-start(f32[4,32,128]{2,1,0:T(8,128)} %get-tuple-element.43), channel_id=1, source_target_pairs={{0,10},{1,11},{2,8},{3,9},{4,14},{5,15},{6,12},{7,13},{8,2},{9,3},... | collective-permute-start | bytes 196616 | tf_op jit(solution)/shard_map/ppermute | solution.py:402
  37.5 0.1 copy.7
  37.6 0.6 select_n.14.table_ref
  38.2 0.0 all-to-all-done.refs_0_
  38.2 1.0 %copy-done = f32[64,32,128]{2,1,0:T(8,128)} copy-done((f32[64,32,128]{2,1,0:T(8,128)}, f32[64,32,128]{2,1,0:T(8,128)S(1)}, u32[]{:S(2)}) %copy-start) | copy-done | bytes 1048600
  39.2 2.5 %shard_map.65 = (f32[8,128,128]{2,1,0:T(8,128)}, f32[8,8,128]{2,1,0:T(8,128)}, f32[8,8,128]{2,1,0:T(8,128)}) custom-call(s32[1]{0:T(128)} %bitcast.own_ref, s32[64]{0:T(128)} %select_n.14.table_ref, f32[64,32,128]{2,1,0:T(8,128)} %copy-done), custom_call_target="tpu_custom_call" | custom-call | flops 262144 | bytes 1572864 | tf_op jit(solution)/shard_map/pallas_call | solution.py:423
  41.7 0.0 copy-done.4
  41.7 0.0 collective-permute-done.7.refs_6_
  41.8 2.6 %collective-permute-start = (f32[8,8,128]{2,1,0:T(8,128)}, f32[8,8,128]{2,1,0:T(8,128)S(1)}, u32[]{:S(2)}, u32[]{:S(2)}) collective-permute-start(f32[8,8,128]{2,1,0:T(8,128)} %get-tuple-element.29), channel_id=1, source_target_pairs={{0,1},{1,2},{2,3},{3,4},{4,5},{5,6},{6,7},{7,8},{8,9},{9,10},{10,1... | collective-permute-start | bytes 98312 | tf_op jit(solution)/shard_map/ppermute | solution.py:432
  44.4 0.0 collective-permute-done.8.refs_7_
  44.4 0.0 copy-start.8
  44.4 1.3 %collective-permute-start.1 = (f32[8,8,128]{2,1,0:T(8,128)}, f32[8,8,128]{2,1,0:T(8,128)S(1)}, u32[]{:S(2)}, u32[]{:S(2)}) collective-permute-start(f32[8,8,128]{2,1,0:T(8,128)} %get-tuple-element.30), channel_id=1, source_target_pairs={{1,0},{2,1},{3,2},{4,3},{5,4},{6,5},{7,6},{8,7},{9,8},{10,9},{11,1... | collective-permute-start | bytes 98312 | tf_op jit(solution)/shard_map/ppermute | solution.py:433
  45.7 0.0 collective-permute-done.9.refs_8_
  45.7 0.0 copy-start.9
  45.7 0.0 copy-done.24
  45.7 2.6 %collective-permute-start.12 = (f32[4,32,128]{2,1,0:T(8,128)S(1)}, f32[4,32,128]{2,1,0:T(8,128)S(1)}, u32[]{:S(2)}, u32[]{:S(2)}) collective-permute-start(f32[4,32,128]{2,1,0:T(8,128)S(1)} %copy-done.24), channel_id=1, source_target_pairs={{0,11},{1,10},{2,9},{3,8},{4,15},{5,14},{6,13},{7,12},{8,3},{9,2},... | collective-permute-start | bytes 196616 | tf_op jit(solution)/shard_map/ppermute | solution.py:402
  48.3 0.0 collective-permute-done.10.refs_9_
  48.4 7.6 %collective-permute-start.13 = (f32[4,32,128]{2,1,0:T(8,128)S(1)}, f32[4,32,128]{2,1,0:T(8,128)S(1)}, u32[]{:S(2)}, u32[]{:S(2)}) collective-permute-start(f32[4,32,128]{2,1,0:T(8,128)S(1)} %copy-done.23), channel_id=1, source_target_pairs={{0,12},{1,13},{2,14},{3,15},{4,8},{5,9},{6,10},{7,11},{8,4},{9,5},... | collective-permute-start | bytes 196616 | tf_op jit(solution)/shard_map/ppermute | solution.py:402
  55.9 0.0 collective-permute-done.11.refs_10_
  55.9 0.1 collective-permute-start.14
  56.0 0.0 collective-permute-done.above_ref
  56.0 3.6 %collective-permute-start.15 = (f32[4,32,128]{2,1,0:T(8,128)S(1)}, f32[4,32,128]{2,1,0:T(8,128)S(1)}, u32[]{:S(2)}, u32[]{:S(2)}) collective-permute-start(f32[4,32,128]{2,1,0:T(8,128)S(1)} %copy-done.21), channel_id=1, source_target_pairs={{0,14},{1,15},{2,12},{3,13},{4,10},{5,11},{6,8},{7,9},{8,6},{9,7},... | collective-permute-start | bytes 196616 | tf_op jit(solution)/shard_map/ppermute | solution.py:402
  59.6 0.0 collective-permute-done.1.below_ref
  59.6 0.7 collective-permute-start.16
  60.3 0.6 add_convert_fusion.ends_ref
  61.0 0.0 copy-done.17
  61.0 5.9 %shard_map.66 = (f32[8,144,128]{2,1,0:T(8,128)}, f32[32,128]{1,0:T(8,128)}) custom-call(s32[2]{0:T(128)} %add_convert_fusion.ends_ref, f32[8,128,128]{2,1,0:T(8,128)} %get-tuple-element.28.t_ref, f32[8,8,128]{2,1,0:T(8,128)} %copy-done.17, f32[8,8,128]{2,1,0:T(8,128)} %copy-done.18, f32[25,80,128]{2,1,0:T(8,128)} %constant.14.clone.coef_ref), custom_call_target="tpu_custom_call" | custom-call | flops 10747904 | bytes 1048576 | tf_op jit(solution)/shard_map/pallas_call | solution.py:438
  66.9 0.0 copy-done.7
  66.9 0.0 collective-permute-done.12.refs_11_
  66.9 0.0 copy-start.12
  66.9 0.0 collective-permute-done.13.refs_12_
  66.9 0.0 collective-permute-done.14.refs_13_
  66.9 0.0 collective-permute-done.15.refs_14_
  67.0 0.0 collective-permute-done.16.refs_15_
  67.0 0.5 copy-done.12
  67.5 0.0 copy-done.13
  67.5 0.0 copy-done.14
  67.6 0.0 copy-done.15
  67.6 0.0 copy-done.16
  67.6 4.1 %shard_map.68 = (f32[8,128,128]{2,1,0:T(8,128)}, f32[16,8,128]{2,1,0:T(8,128)}) custom-call(s32[1]{0:T(128)} %bitcast.own_ref, s32[64]{0:T(128)} %select_n.14.table_ref, f32[8,144,128]{2,1,0:T(8,128)} %get-tuple-element.31.ext_ref, f32[32,128]{1,0:T(8,128)} %get-tuple-element.32.gram_ref, f32[4,32,128]{2,1,0:T(8,128)} %get-tuple-element.33.refs_0_, ...), custom_call_target="tpu_custom_call" | custom-call | flops 6553600 | bytes 2097152 | tf_op jit(solution)/shard_map/pallas_call | solution.py:451
  71.7 12.5 %all_to_all.10.fit_ref = f32[16,8,128]{2,1,0:T(8,128)} all-to-all(f32[16,8,128]{2,1,0:T(8,128)} %get-tuple-element.49), channel_id=1, replica_groups=mesh['field'=2,'ccd'=16] {'ccd'}, dimensions={0} | all-to-all | bytes 131072 | tf_op jit(solution)/shard_map/all_to_all | solution.py:463
  84.2 6.1 %shard_map.69 = f32[128,1024]{1,0:T(8,128)} custom-call(f32[16,8,128]{2,1,0:T(8,128)} %all_to_all.10.fit_ref, f32[8,144,128]{2,1,0:T(8,128)} %get-tuple-element.31.ext_ref, f32[8,128,128]{2,1,0:T(8,128)} %get-tuple-element.50.sci_ref), custom_call_target="tpu_custom_call" | custom-call | flops 6553600 | bytes 1572864 | tf_op jit(solution)/shard_map/pallas_call | solution.py:465
  (38 shorter events, 0.1 us)
Async XLA Ops:
  4.5 33.7 %all-to-all-start = ((f32[64,32,128]{2,1,0:T(8,128)}), f32[64,32,128]{2,1,0:T(8,128)S(1)}, u32[]{:S(2)}, u32[]{:S(2)}) async-start(f32[64,32,128]{2,1,0:T(8,128)} %shard_map.64), calls=%async_computation | async-start | bytes 2097152 | tf_op jit(solution)/shard_map/all_to_all | solution.py:398
  16.1 4.0 %copy-start.1 = (s32[16,32,1]{1,2,0:T(1,128)S(1)}, s32[16,32,1]{1,2,0:T(1,128)}, u32[]{:S(2)}) copy-start(s32[16,32,1]{1,2,0:T(1,128)} %param.9) | copy-start | bytes 6148
  16.1 5.4 %collective-permute-start.2 = (f32[4,32,128]{2,1,0:T(8,128)}, f32[4,32,128]{2,1,0:T(8,128)S(1)}, u32[]{:S(2)}, u32[]{:S(2)}) collective-permute-start(f32[4,32,128]{2,1,0:T(8,128)} %get-tuple-element.34), channel_id=1, source_target_pairs={{0,1},{1,0},{2,3},{3,2},{4,5},{5,4},{6,7},{7,6},{8,9},{9,8},{10,11... | collective-permute-start | bytes 196616 | tf_op jit(solution)/shard_map/ppermute | solution.py:402
  16.5 7.6 %collective-permute-start.3 = (f32[4,32,128]{2,1,0:T(8,128)}, f32[4,32,128]{2,1,0:T(8,128)S(1)}, u32[]{:S(2)}, u32[]{:S(2)}) collective-permute-start(f32[4,32,128]{2,1,0:T(8,128)} %get-tuple-element.35), channel_id=1, source_target_pairs={{0,2},{1,3},{2,0},{3,1},{4,6},{5,7},{6,4},{7,5},{8,10},{9,11},{10,... | collective-permute-start | bytes 196616 | tf_op jit(solution)/shard_map/ppermute | solution.py:402
  18.2 6.8 %collective-permute-start.4 = (f32[4,32,128]{2,1,0:T(8,128)}, f32[4,32,128]{2,1,0:T(8,128)S(1)}, u32[]{:S(2)}, u32[]{:S(2)}) collective-permute-start(f32[4,32,128]{2,1,0:T(8,128)} %get-tuple-element.36), channel_id=1, source_target_pairs={{0,3},{1,2},{2,1},{3,0},{4,7},{5,6},{6,5},{7,4},{8,11},{9,10},{10,... | collective-permute-start | bytes 196616 | tf_op jit(solution)/shard_map/ppermute | solution.py:402
  18.2 13.5 %collective-permute-start.5 = (f32[4,32,128]{2,1,0:T(8,128)}, f32[4,32,128]{2,1,0:T(8,128)S(1)}, u32[]{:S(2)}, u32[]{:S(2)}) collective-permute-start(f32[4,32,128]{2,1,0:T(8,128)} %get-tuple-element.37), channel_id=1, source_target_pairs={{0,4},{1,5},{2,6},{3,7},{4,0},{5,1},{6,2},{7,3},{8,12},{9,13},{10,... | collective-permute-start | bytes 196616 | tf_op jit(solution)/shard_map/ppermute | solution.py:402
  19.9 15.0 %collective-permute-start.6 = (f32[4,32,128]{2,1,0:T(8,128)}, f32[4,32,128]{2,1,0:T(8,128)S(1)}, u32[]{:S(2)}, u32[]{:S(2)}) collective-permute-start(f32[4,32,128]{2,1,0:T(8,128)} %get-tuple-element.38), channel_id=1, source_target_pairs={{0,5},{1,4},{2,7},{3,6},{4,1},{5,0},{6,3},{7,2},{8,13},{9,12},{10,... | collective-permute-start | bytes 196616 | tf_op jit(solution)/shard_map/ppermute | solution.py:402
  20.5 0.7 copy-start.19
  21.5 20.2 %copy-start.2 = (f32[4,32,128]{2,1,0:T(8,128)}, f32[4,32,128]{2,1,0:T(8,128)S(1)}, u32[]{:S(2)}) copy-start(f32[4,32,128]{2,1,0:T(8,128)S(1)} %collective-permute-done.2.refs_1_) | copy-start | bytes 196612
  21.5 20.2 %collective-permute-start.7 = (f32[4,32,128]{2,1,0:T(8,128)}, f32[4,32,128]{2,1,0:T(8,128)S(1)}, u32[]{:S(2)}, u32[]{:S(2)}) collective-permute-start(f32[4,32,128]{2,1,0:T(8,128)} %get-tuple-element.39), channel_id=1, source_target_pairs={{0,6},{1,7},{2,4},{3,5},{4,2},{5,3},{6,0},{7,1},{8,14},{9,15},{10,... | collective-permute-start | bytes 196616 | tf_op jit(solution)/shard_map/ppermute | solution.py:402
  24.1 17.6 %copy-start.3 = (f32[4,32,128]{2,1,0:T(8,128)}, f32[4,32,128]{2,1,0:T(8,128)S(1)}, u32[]{:S(2)}) copy-start(f32[4,32,128]{2,1,0:T(8,128)S(1)} %collective-permute-done.3.refs_2_) | copy-start | bytes 196612
  24.1 20.2 %collective-permute-start.8 = (f32[4,32,128]{2,1,0:T(8,128)}, f32[4,32,128]{2,1,0:T(8,128)S(1)}, u32[]{:S(2)}, u32[]{:S(2)}) collective-permute-start(f32[4,32,128]{2,1,0:T(8,128)} %get-tuple-element.40), channel_id=1, source_target_pairs={{0,7},{1,6},{2,5},{3,4},{4,3},{5,2},{6,1},{7,0},{8,15},{9,14},{10,... | collective-permute-start | bytes 196616 | tf_op jit(solution)/shard_map/ppermute | solution.py:402
  25.0 16.7 %copy-start.4 = (f32[4,32,128]{2,1,0:T(8,128)}, f32[4,32,128]{2,1,0:T(8,128)S(1)}, u32[]{:S(2)}) copy-start(f32[4,32,128]{2,1,0:T(8,128)S(1)} %collective-permute-done.4.refs_3_) | copy-start | bytes 196612
  25.0 20.7 %collective-permute-start.9 = (f32[4,32,128]{2,1,0:T(8,128)}, f32[4,32,128]{2,1,0:T(8,128)S(1)}, u32[]{:S(2)}, u32[]{:S(2)}) collective-permute-start(f32[4,32,128]{2,1,0:T(8,128)} %get-tuple-element.41), channel_id=1, source_target_pairs={{0,8},{1,9},{2,10},{3,11},{4,12},{5,13},{6,14},{7,15},{8,0},{9,1},... | collective-permute-start | bytes 196616 | tf_op jit(solution)/shard_map/ppermute | solution.py:402
  31.7 10.0 %copy-start.5 = (f32[4,32,128]{2,1,0:T(8,128)}, f32[4,32,128]{2,1,0:T(8,128)S(1)}, u32[]{:S(2)}) copy-start(f32[4,32,128]{2,1,0:T(8,128)S(1)} %collective-permute-done.5.refs_4_) | copy-start | bytes 196612
  31.7 16.6 %collective-permute-start.10 = (f32[4,32,128]{2,1,0:T(8,128)}, f32[4,32,128]{2,1,0:T(8,128)S(1)}, u32[]{:S(2)}, u32[]{:S(2)}) collective-permute-start(f32[4,32,128]{2,1,0:T(8,128)} %get-tuple-element.42), channel_id=1, source_target_pairs={{0,9},{1,8},{2,11},{3,10},{4,13},{5,12},{6,15},{7,14},{8,1},{9,0},... | collective-permute-start | bytes 196616 | tf_op jit(solution)/shard_map/ppermute | solution.py:402
  34.9 6.8 %copy-start.6 = (f32[4,32,128]{2,1,0:T(8,128)}, f32[4,32,128]{2,1,0:T(8,128)S(1)}, u32[]{:S(2)}) copy-start(f32[4,32,128]{2,1,0:T(8,128)S(1)} %collective-permute-done.6.refs_5_) | copy-start | bytes 196612
  34.9 21.0 %collective-permute-start.11 = (f32[4,32,128]{2,1,0:T(8,128)}, f32[4,32,128]{2,1,0:T(8,128)S(1)}, u32[]{:S(2)}, u32[]{:S(2)}) collective-permute-start(f32[4,32,128]{2,1,0:T(8,128)} %get-tuple-element.43), channel_id=1, source_target_pairs={{0,10},{1,11},{2,8},{3,9},{4,14},{5,15},{6,12},{7,13},{8,2},{9,3},... | collective-permute-start | bytes 196616 | tf_op jit(solution)/shard_map/ppermute | solution.py:402
  38.2 7.6 %copy-start.24 = (f32[4,32,128]{2,1,0:T(8,128)S(1)}, f32[4,32,128]{2,1,0:T(8,128)}, u32[]{:S(2)}) copy-start(f32[4,32,128]{2,1,0:T(8,128)} %get-tuple-element.44) | copy-start | bytes 196612
  38.2 10.2 %copy-start.23 = (f32[4,32,128]{2,1,0:T(8,128)S(1)}, f32[4,32,128]{2,1,0:T(8,128)}, u32[]{:S(2)}) copy-start(f32[4,32,128]{2,1,0:T(8,128)} %get-tuple-element.45) | copy-start | bytes 196612
  38.2 17.7 %copy-start.22 = (f32[4,32,128]{2,1,0:T(8,128)S(1)}, f32[4,32,128]{2,1,0:T(8,128)}, u32[]{:S(2)}) copy-start(f32[4,32,128]{2,1,0:T(8,128)} %get-tuple-element.46) | copy-start | bytes 196612
  38.2 17.8 %copy-start.21 = (f32[4,32,128]{2,1,0:T(8,128)S(1)}, f32[4,32,128]{2,1,0:T(8,128)}, u32[]{:S(2)}) copy-start(f32[4,32,128]{2,1,0:T(8,128)} %get-tuple-element.47) | copy-start | bytes 196612
  38.2 21.5 %copy-start.20 = (f32[4,32,128]{2,1,0:T(8,128)S(1)}, f32[4,32,128]{2,1,0:T(8,128)}, u32[]{:S(2)}) copy-start(f32[4,32,128]{2,1,0:T(8,128)} %get-tuple-element.48) | copy-start | bytes 196612
  38.2 1.0 %copy-start = (f32[64,32,128]{2,1,0:T(8,128)}, f32[64,32,128]{2,1,0:T(8,128)S(1)}, u32[]{:S(2)}) copy-start(f32[64,32,128]{2,1,0:T(8,128)S(1)} %all-to-all-done.refs_0_) | copy-start | bytes 3145732
  41.8 25.1 %copy-start.7 = (f32[4,32,128]{2,1,0:T(8,128)}, f32[4,32,128]{2,1,0:T(8,128)S(1)}, u32[]{:S(2)}) copy-start(f32[4,32,128]{2,1,0:T(8,128)S(1)} %collective-permute-done.7.refs_6_) | copy-start | bytes 196612
  41.8 14.2 %collective-permute-start = (f32[8,8,128]{2,1,0:T(8,128)}, f32[8,8,128]{2,1,0:T(8,128)S(1)}, u32[]{:S(2)}, u32[]{:S(2)}) collective-permute-start(f32[8,8,128]{2,1,0:T(8,128)} %get-tuple-element.29), channel_id=1, source_target_pairs={{0,1},{1,2},{2,3},{3,4},{4,5},{5,6},{6,7},{7,8},{8,9},{9,10},{10,1... | collective-permute-start | bytes 98312 | tf_op jit(solution)/shard_map/ppermute | solution.py:432
  44.4 22.5 %copy-start.8 = (f32[4,32,128]{2,1,0:T(8,128)}, f32[4,32,128]{2,1,0:T(8,128)S(1)}, u32[]{:S(2)}) copy-start(f32[4,32,128]{2,1,0:T(8,128)S(1)} %collective-permute-done.8.refs_7_) | copy-start | bytes 196612
  44.4 15.2 %collective-permute-start.1 = (f32[8,8,128]{2,1,0:T(8,128)}, f32[8,8,128]{2,1,0:T(8,128)S(1)}, u32[]{:S(2)}, u32[]{:S(2)}) collective-permute-start(f32[8,8,128]{2,1,0:T(8,128)} %get-tuple-element.30), channel_id=1, source_target_pairs={{1,0},{2,1},{3,2},{4,3},{5,4},{6,5},{7,6},{8,7},{9,8},{10,9},{11,1... | collective-permute-start | bytes 98312 | tf_op jit(solution)/shard_map/ppermute | solution.py:433
  45.7 21.2 %copy-start.9 = (f32[4,32,128]{2,1,0:T(8,128)}, f32[4,32,128]{2,1,0:T(8,128)S(1)}, u32[]{:S(2)}) copy-start(f32[4,32,128]{2,1,0:T(8,128)S(1)} %collective-permute-done.9.refs_8_) | copy-start | bytes 196612
  45.7 21.2 %collective-permute-start.12 = (f32[4,32,128]{2,1,0:T(8,128)S(1)}, f32[4,32,128]{2,1,0:T(8,128)S(1)}, u32[]{:S(2)}, u32[]{:S(2)}) collective-permute-start(f32[4,32,128]{2,1,0:T(8,128)S(1)} %copy-done.24), channel_id=1, source_target_pairs={{0,11},{1,10},{2,9},{3,8},{4,15},{5,14},{6,13},{7,12},{8,3},{9,2},... | collective-permute-start | bytes 196616 | tf_op jit(solution)/shard_map/ppermute | solution.py:402
  48.3 18.5 %copy-start.10 = (f32[4,32,128]{2,1,0:T(8,128)}, f32[4,32,128]{2,1,0:T(8,128)S(1)}, u32[]{:S(2)}) copy-start(f32[4,32,128]{2,1,0:T(8,128)S(1)} %collective-permute-done.10.refs_9_) | copy-start | bytes 196612
  48.4 18.6 %collective-permute-start.13 = (f32[4,32,128]{2,1,0:T(8,128)S(1)}, f32[4,32,128]{2,1,0:T(8,128)S(1)}, u32[]{:S(2)}, u32[]{:S(2)}) collective-permute-start(f32[4,32,128]{2,1,0:T(8,128)S(1)} %copy-done.23), channel_id=1, source_target_pairs={{0,12},{1,13},{2,14},{3,15},{4,8},{5,9},{6,10},{7,11},{8,4},{9,5},... | collective-permute-start | bytes 196616 | tf_op jit(solution)/shard_map/ppermute | solution.py:402
  55.9 11.0 %copy-start.11 = (f32[4,32,128]{2,1,0:T(8,128)}, f32[4,32,128]{2,1,0:T(8,128)S(1)}, u32[]{:S(2)}) copy-start(f32[4,32,128]{2,1,0:T(8,128)S(1)} %collective-permute-done.11.refs_10_) | copy-start | bytes 196612
  55.9 11.0 %collective-permute-start.14 = (f32[4,32,128]{2,1,0:T(8,128)S(1)}, f32[4,32,128]{2,1,0:T(8,128)S(1)}, u32[]{:S(2)}, u32[]{:S(2)}) collective-permute-start(f32[4,32,128]{2,1,0:T(8,128)S(1)} %copy-done.22), channel_id=1, source_target_pairs={{0,13},{1,12},{2,15},{3,14},{4,9},{5,8},{6,11},{7,10},{8,5},{9,4},... | collective-permute-start | bytes 196616 | tf_op jit(solution)/shard_map/ppermute | solution.py:402
  56.0 5.0 %copy-start.17 = (f32[8,8,128]{2,1,0:T(8,128)}, f32[8,8,128]{2,1,0:T(8,128)S(1)}, u32[]{:S(2)}) copy-start(f32[8,8,128]{2,1,0:T(8,128)S(1)} %collective-permute-done.above_ref) | copy-start | bytes 98308
  56.0 10.9 %collective-permute-start.15 = (f32[4,32,128]{2,1,0:T(8,128)S(1)}, f32[4,32,128]{2,1,0:T(8,128)S(1)}, u32[]{:S(2)}, u32[]{:S(2)}) collective-permute-start(f32[4,32,128]{2,1,0:T(8,128)S(1)} %copy-done.21), channel_id=1, source_target_pairs={{0,14},{1,15},{2,12},{3,13},{4,10},{5,11},{6,8},{7,9},{8,6},{9,7},... | collective-permute-start | bytes 196616 | tf_op jit(solution)/shard_map/ppermute | solution.py:402
  59.6 1.4 %copy-start.18 = (f32[8,8,128]{2,1,0:T(8,128)}, f32[8,8,128]{2,1,0:T(8,128)S(1)}, u32[]{:S(2)}) copy-start(f32[8,8,128]{2,1,0:T(8,128)S(1)} %collective-permute-done.1.below_ref) | copy-start | bytes 98308
  59.6 7.3 %collective-permute-start.16 = (f32[4,32,128]{2,1,0:T(8,128)S(1)}, f32[4,32,128]{2,1,0:T(8,128)S(1)}, u32[]{:S(2)}, u32[]{:S(2)}) collective-permute-start(f32[4,32,128]{2,1,0:T(8,128)S(1)} %copy-done.20), channel_id=1, source_target_pairs={{0,15},{1,14},{2,13},{3,12},{4,11},{5,10},{6,9},{7,8},{8,7},{9,6},... | collective-permute-start | bytes 196616 | tf_op jit(solution)/shard_map/ppermute | solution.py:402
  66.9 0.6 copy-start.12
  66.9 0.6 copy-start.13
  66.9 0.6 copy-start.14
  67.0 0.6 copy-start.15
  67.0 0.6 copy-start.16
where the time goes:
time: 90.8 us; the launch traced here: 90.3 us
  starting transfers between devices  40.1 us (44%)
  Pallas kernels  27.3 us (30%)
  blocking collectives  12.5 us (14%)
  waiting for transfers between devices  5.6 us (6%)
  local copies, waits for them, and re-layouts  3 us (3%)
  other arithmetic  1.42 us (2%)
    ppermute x15, starting transfers between devices, exchanged(): lax.ppermute(chunks[k], 'ccd', [(i, i ^ k) for i in range(devices)])  28.9 us
    all_to_all x1, blocking collectives, body(): fit = lax.all_to_all(fit, 'ccd', split_axis=0, concat_axis=0, tiled=True)  12.5 us
    pallas_call x2, Pallas kernels, warped(): call(functools.partial(warp_kernel, visit, devices, cap, paired), [f32(ca...  8.71 us
    all_to_all x1, starting transfers between devices, exchanged(): lax.all_to_all(chunks[0], 'ccd', split_axis=0, concat_axis=0, tiled=True)  7.39 us
    pallas_call x1, Pallas kernels, body(): call(difference_kernel, f32(rows, columns), [VMEM] * 3, [pltpu.VMEM((KSID...  6.06 us
    pallas_call x1, Pallas kernels, body(): call(gram_kernel, [f32(slabs, rows + 2 * SUB, LANES), f32(size, LANES)],...  5.89 us
    ppermute x15, waiting for transfers between devices, exchanged(): lax.ppermute(chunks[k], 'ccd', [(i, i ^ k) for i in range(devices)])  5.59 us
    pallas_call x1, Pallas kernels, body(): call(functools.partial(science_kernel, devices, cap, paired), [slab_shape...  4.08 us
  transfers between devices with their start and end apart: 18, of which 2 were waited for; matrix products, arithmetic and copies ran while one was open for 2% of the time, Pallas kernels for 14%

commit v1 on v0

--- a/solution.py
+++ b/solution.py
@@ -91,7 +91,7 @@
 
 
 def warp_kernel(
-    visit, devices, cap, paired, own_ref, tgt_ref, shift_ref, frac_ref, x_ref, *refs
+    visit, devices, cap, paired, strips, own_ref, tgt_ref, shift_ref, frac_ref, x_ref, *refs
 ):
     outs, (mid, blocks, inv, cnt) = refs[:-4], refs[-4:]
     rows, columns = x_ref.shape
@@ -146,9 +146,21 @@
                 outs[k][r] = blocks[inv[k * cap + r]]
     else:
 
-        @pl.loop(0, devices * cap)
-        def _(e):
-            outs[0][e] = blocks[inv[e]]
+        @pl.loop(0, devices)
+        def _(p):
+            for r in range(cap):
+                outs[0][p, r * BR : (r + 1) * BR, :] = blocks[inv[p * cap + r]]
+            if strips:
+                before = jnp.maximum(p - 1, 0)
+                after = jnp.minimum(p + 1, devices - 1)
+                outs[0][p, cap * BR :, :] = jnp.zeros((2 * SUB, LANES), jnp.float32)
+                for r in range(cap):
+                    at = cap * BR + REACH * r
+                    outs[0][p, at : at + REACH, :] = blocks[
+                        inv[before * cap + r], BR - REACH : BR, :
+                    ]
+                    at = at + SUB
+                    outs[0][p, at : at + REACH, :] = blocks[inv[after * cap + r], 0:REACH, :]
 
 
 def sum_blocks(devices, cap, paired, own, table_ref, ins, acc):
@@ -160,52 +172,59 @@
                 acc[slot] = acc[slot] + ins[k][r]
     else:
 
-        @pl.loop(0, devices * cap)
-        def _(e):
-            slot = table_ref[e]
-            acc[slot] = acc[slot] + ins[0][e]
-
-
-def template_kernel(devices, cap, paired, own_ref, table_ref, *refs):
-    ins, (out, top, bottom, acc) = refs[:-4], refs[-4:]
-    slabs, _, _ = out.shape
-    sum_blocks(devices, cap, paired, own_ref[0], table_ref, ins, acc)
-    for s in range(NB):
-        out[s % slabs, s // slabs * BR : (s // slabs + 1) * BR, :] = acc[s]
-    for j in range(slabs):
-        top[j] = acc[j, 0:SUB, :]
-        bottom[j] = acc[NB - slabs + j, BR - SUB : BR, :]
-
-
-def gram_kernel(
-    ends_ref, t_ref, above_ref, below_ref, coef_ref, ext_ref, gram_ref, lagged, gen, spec
+        @pl.loop(0, devices)
+        def _(c):
+            for r in range(cap):
+                slot = table_ref[c * cap + r]
+                acc[slot] = acc[slot] + ins[0][c, r * BR : (r + 1) * BR, :]
+
+
+def template_kernel(
+    devices, cap, own_ref, table_ref, ends_ref, in_ref, edges_ref, coef_ref,
+    ext_ref, gram_ref, acc, lagged, gen, spec,
 ):
-    slabs, rows, _ = t_ref.shape
+    slabs, rows = ext_ref.shape[0], ext_ref.shape[1] - 2 * SUB
     tiles = rows // SUB
     lane = lane_ids()
     sub = lax.broadcasted_iota(jnp.int32, (SUB, LANES), 0)
-
-    @pl.loop(0, tiles, unroll=UNROLL)
-    def _(t):
-        at = pl.ds(pl.multiple_of(t * SUB, SUB), SUB)
-        parts = [t_ref[j, at, :] for j in range(slabs)]
+    sum_blocks(devices, cap, False, own_ref[0], table_ref, [in_ref], acc)
+
+    for end in range(2):
+        at = cap * BR + end * SUB
+        strip = in_ref[:, at : at + SUB, :].reshape(devices * SUB, LANES)
+        edge = mm(edges_ref[end], strip)
+        first = SUB - REACH if end == 0 else SUB + rows
         for j in range(slabs):
-            ext_ref[j, pl.ds(pl.multiple_of(t * SUB + SUB, SUB), SUB), :] = parts[j]
+            whole = 0 if end == 0 else SUB + rows
+            ext_ref[j, whole : whole + SUB, :] = jnp.zeros((SUB, LANES), jnp.float32)
+            for i in range(REACH):
+                ext_ref[j, first + i : first + i + 1, :] = edge[i * slabs + j : i * slabs + j + 1]
+
+    def lag_tile(parts, at):
         for n, lag in enumerate(LAGS):
             for j, moved in enumerate(shifted(parts, lag, lane)):
                 lagged[n, j, at, :] = moved
 
-    for j in range(slabs):
-        ext_ref[j, 0:SUB, :] = above_ref[j]
-        ext_ref[j, SUB + rows :, :] = below_ref[j]
+    lag_tile([ext_ref[j, 0:SUB, :] for j in range(slabs)], slice(0, SUB))
+    for band in range(rows // BR):
+
+        @pl.loop(0, BR // SUB, unroll=UNROLL)
+        def _(t):
+            at = pl.ds(pl.multiple_of(t * SUB, SUB), SUB)
+            to = pl.ds(pl.multiple_of(SUB + band * BR + t * SUB, SUB), SUB)
+            parts = [acc[band * slabs + j, at, :] for j in range(slabs)]
+            for j in range(slabs):
+                ext_ref[j, to, :] = parts[j]
+            lag_tile(parts, to)
 
     gen[...] = jnp.zeros_like(gen)
     spec[...] = jnp.zeros_like(spec)
 
     @pl.loop(0, slabs)
     def _(j):
-        def firsts(t):
-            return [lagged[n, j, t * SUB : (t + 1) * SUB, :] for n in range(len(LAGS))]
+        def first(t, down, lag):
+            base = SUB + t * SUB - down // 2
+            return lagged[lag + KSIDE - 1, j, base : base + SUB, :]
 
         def second(t, down):
             base = SUB + t * SUB + down
@@ -213,10 +232,9 @@
 
         sums = [None] * len(PRODUCTS)
         for t in range(tiles):
-            first = firsts(t)
-            moved = [second(t, down) for down in range(KSIDE)]
+            moved = [second(t, down - down // 2) for down in range(KSIDE)]
             for n, (down, lag) in enumerate(PRODUCTS):
-                term = first[lag + KSIDE - 1] * moved[down]
+                term = first(t, down, lag) * moved[down]
                 sums[n] = term if sums[n] is None else sums[n] + term
         edge = ((j == 0) & (lane < REACH)) | ((j == slabs - 1) & (lane >= LANES - REACH))
         for n in range(len(PRODUCTS)):
@@ -226,7 +244,7 @@
             n = len(PRODUCTS) + m
             t = 0 if row >= 0 else tiles - 1
             here = (sub == row % SUB) & (ends_ref[0 if row >= 0 else 1] > 0)
-            term = lagged[lag + KSIDE - 1, j, t * SUB : (t + 1) * SUB, :] * second(t, down)
+            term = first(t, 0, lag) * second(t, down)
             term = jnp.where(here, term, 0.0)
             gen[n] = gen[n] + jnp.where(edge, 0.0, term)
             spec[n] = spec[n] + jnp.where(edge, term, 0.0)
@@ -378,8 +396,10 @@
 
     def warped(visit, paired):
         out = call(
-            functools.partial(warp_kernel, visit, devices, cap, paired),
-            [f32(cap, BR, BC)] * devices if paired else [f32(devices * cap, BR, BC)],
+            functools.partial(warp_kernel, visit, devices, cap, paired, visit == 0),
+            [f32(cap, BR, BC)] * devices
+            if paired
+            else [f32(devices, cap * BR + (2 * SUB if visit == 0 else 0), BC)],
             [SMEM, SMEM, SMEM, SMEM, pl.BlockSpec((None, rows, columns), lambda i: (visit, 0, 0))],
             [
                 pltpu.VMEM((slabs, rows + 2 * SUB, LANES), jnp.float32),
@@ -412,41 +432,43 @@
     earlier = block_ids[None, :] < block_ids[:, None]
     same = targets[:, :, None] == targets[:, None, :]
     order = jnp.sum(same & earlier[None], axis=2)
-    arrives = (targets == owner)[:, None, :] & (order[:, None, :] == jnp.arange(cap)[None, :, None])
-    table = jnp.where(
-        jnp.any(arrives, axis=2), jnp.sum(jnp.where(arrives, margin_slot[:, None, :], 0), axis=2), NB
-    ).reshape(-1).astype(jnp.int32)
+    in_place = order[:, None, :] == jnp.arange(cap)[None, :, None]
+
+    def slots_at(patch):
+        arrives = (targets == patch)[:, None, :] & in_place
+        slots = jnp.sum(jnp.where(arrives, margin_slot[:, None, :], 0), axis=2)
+        return jnp.where(jnp.any(arrives, axis=2), slots, NB).astype(jnp.int32)
+
+    table = slots_at(owner).reshape(-1)
+    wanted = jnp.arange(REACH * slabs)[:, None, None, None]
+    row_of = jnp.arange(SUB // REACH * REACH).reshape(1, 1, SUB // REACH, REACH) % REACH
+    spare = ((0, 0), (0, SUB // REACH - cap))
+
+    def edge_rows(patch, first_slot):
+        slots = jnp.pad(slots_at(patch), spare, constant_values=NB)[None, :, :, None]
+        hit = (slots - first_slot == wanted % slabs) & (row_of == wanted // slabs)
+        return hit.astype(jnp.float32).reshape(REACH * slabs, devices * SUB)
+
+    edges = jnp.stack([edge_rows(owner - 1, NB - slabs), edge_rows(owner + 1, 0)])
 
     slab_shape = f32(slabs, rows, LANES)
-    strip = f32(slabs, SUB, LANES)
     sums = pltpu.VMEM((NB + 1, BR, BC), jnp.float32)
-    template, top, bottom = call(
-        functools.partial(template_kernel, devices, cap, False),
-        [slab_shape, strip, strip],
-        [SMEM, SMEM, VMEM],
-        [sums],
-        pixels * 2,
-        pixels * 12,
-    )(own, table, *template_in)
-    ends = devices - 1
-    above = lax.ppermute(bottom, "ccd", [(i, i + 1) for i in range(ends)])
-    below = lax.ppermute(top, "ccd", [(i + 1, i) for i in range(ends)])
-
     size = NB
     count, coef = gram_table()
     at_ends = jnp.stack([owner == 0, owner == devices - 1]).astype(jnp.int32)
     extended, gram = call(
-        gram_kernel,
+        functools.partial(template_kernel, devices, cap),
         [f32(slabs, rows + 2 * SUB, LANES), f32(size, LANES)],
-        [SMEM] + [VMEM] * 4,
+        [SMEM, SMEM, SMEM] + [VMEM] * 3,
         [
-            pltpu.VMEM((len(LAGS), slabs, rows, LANES), jnp.float32),
+            sums,
+            pltpu.VMEM((len(LAGS), slabs, rows + SUB, LANES), jnp.float32),
             pltpu.VMEM((count, SUB, LANES), jnp.float32),
             pltpu.VMEM((count, SUB, LANES), jnp.float32),
         ],
         pixels * 2 * len(PRODUCTS),
         pixels * 8,
-    )(at_ends, template, above, below, jnp.asarray(coef))
+    )(own, table, at_ends, template_in[0], edges, jnp.asarray(coef))
 
     science, fit = call(
         functools.partial(science_kernel, devices, cap, paired),

time: 90.8 us -> 87.1 us (0.959)
  starting transfers between devices: 40.1 us -> 29.2 us
  waiting for transfers between devices: 5.6 us -> 14.9 us
  Pallas kernels: 27.3 us -> 25.4 us
  other arithmetic: 1.42 us -> 2.51 us
    ppermute x15, waiting for transfers between devices: 5.59 us -> 14.9 us  [exchanged(): lax.ppermute(chunks[k], 'ccd', [(i, i ^ k) for i in range(devices)])]
    ppermute x15, starting transfers between devices: 28.9 us -> 21.7 us  [exchanged(): lax.ppermute(chunks[k], 'ccd', [(i, i ^ k) for i in range(devices)])]
    ppermute x2 -> x0, starting transfers between devices: 3.88 us -> none  [the longest x1 2.59 us: body(): above = lax.ppermute(bottom, 'ccd', [(i, i + 1) for i in range(ends)])]
    pallas_call x4 -> x3, Pallas kernels: 17.1 us -> 15.2 us  [the longest x2 8.67 us: warped(): call(functools.partial(warp_kernel, visit, devices, cap, paired, visit ==...]
    unnamed x50 -> x36, local copies, waits for them, and re-layouts: 2.34 us -> 1.64 us
  transfers between devices with their start and end apart: 18 -> 16, of which waited for: 2 -> 5; matrix products, arithmetic and copies ran while one was open for 2% -> 4% of each run, Pallas kernels for 14% -> 12%
where the time goes in v1:
time: 87.1 us; the launch traced here: 86.7 us
  starting transfers between devices  29.2 us (34%)
  Pallas kernels  25.4 us (29%)
  waiting for transfers between devices  14.9 us (17%)
  blocking collectives  11.7 us (13%)
  local copies, waits for them, and re-layouts  2.74 us (3%)
  other arithmetic  2.51 us (3%)
    ppermute x15, starting transfers between devices, exchanged(): lax.ppermute(chunks[k], 'ccd', [(i, i ^ k) for i in range(devices)])  21.7 us
    ppermute x15, waiting for transfers between devices, exchanged(): lax.ppermute(chunks[k], 'ccd', [(i, i ^ k) for i in range(devices)])  14.9 us
    all_to_all x1, blocking collectives, body(): fit = lax.all_to_all(fit, 'ccd', split_axis=0, concat_axis=0, tiled=True)  11.7 us
    pallas_call x2, Pallas kernels, warped(): call(functools.partial(warp_kernel, visit, devices, cap, paired, visit ==...  8.67 us
    all_to_all x1, starting transfers between devices, exchanged(): lax.all_to_all(chunks[0], 'ccd', split_axis=0, concat_axis=0, tiled=True)  7.52 us
    pallas_call x1, Pallas kernels, body(): call(functools.partial(template_kernel, devices, cap), [f32(slabs, rows +...  6.56 us
    pallas_call x1, Pallas kernels, body(): call(difference_kernel, f32(rows, columns), [VMEM] * 3, [pltpu.VMEM((KSID...  6.06 us
    pallas_call x1, Pallas kernels, body(): call(functools.partial(science_kernel, devices, cap, paired), [slab_shape...  4.08 us
  transfers between devices with their start and end apart: 16, of which 5 were waited for; matrix products, arithmetic and copies ran while one was open for 4% of the time, Pallas kernels for 12%

profile of v1, /device:TPU:0, one launch (start us, length us, event | category | flops | bytes accessed | tf_op | source)
XLA Modules:
  0.0 86.7 jit_solution(1982454548151041300)
XLA Ops:
  0.0 4.5 %shard_map.64 = f32[16,144,128]{2,1,0:T(8,128)} custom-call(s32[1]{0:T(128)} %bitcast.own_ref, s32[16,32]{1,0:T(8,128)} %bitcast.8, s32[2,1,2]{2,1,0:T(1,128)} %shift_ref.3, f32[2,1,2]{2,1,0:T(1,128)} %frac_ref.3, f32[2,128,1024]{2,1,0:T(8,128)} %x_ref.3), custom_call_target="tpu_custom_call" | custom-call | flops 5242880 | bytes 1572864 | tf_op jit(solution)/shard_map/pallas_call | solution.py:398
  4.5 7.5 %all-to-all-start = ((f32[16,144,128]{2,1,0:T(8,128)}), f32[16,144,128]{2,1,0:T(8,128)S(1)}, u32[]{:S(2)}, u32[]{:S(2)}) async-start(f32[16,144,128]{2,1,0:T(8,128)} %shard_map.64), calls=%async_computation | async-start | bytes 2359296 | tf_op jit(solution)/shard_map/all_to_all | solution.py:418
  12.0 4.2 %shard_map.66 = (f32[4,32,128]{2,1,0:T(8,128)}, f32[4,32,128]{2,1,0:T(8,128)}, f32[4,32,128]{2,1,0:T(8,128)}, f32[4,32,128]{2,1,0:T(8,128)}, f32[4,32,128]{2,1,0...) custom-call(s32[1]{0:T(128)} %bitcast.own_ref, ...), custom_call_target="tpu_custom_call" | custom-call | flops 5242880 | bytes 1572864 | tf_op jit(solution)/shard_map/pallas_call | solution.py:398
  16.2 0.4 collective-permute-start
  16.6 1.6 %collective-permute-start.1 = (f32[4,32,128]{2,1,0:T(8,128)}, f32[4,32,128]{2,1,0:T(8,128)S(1)}, u32[]{:S(2)}, u32[]{:S(2)}) collective-permute-start(f32[4,32,128]{2,1,0:T(8,128)} %get-tuple-element.29), channel_id=1, source_target_pairs={{0,2},{1,3},{2,0},{3,1},{4,6},{5,7},{6,4},{7,5},{8,10},{9,11},{10,... | collective-permute-start | bytes 196616 | tf_op jit(solution)/shard_map/ppermute | solution.py:422
  18.2 0.0 collective-permute-start.2
  18.3 1.7 %collective-permute-start.3 = (f32[4,32,128]{2,1,0:T(8,128)}, f32[4,32,128]{2,1,0:T(8,128)S(1)}, u32[]{:S(2)}, u32[]{:S(2)}) collective-permute-start(f32[4,32,128]{2,1,0:T(8,128)} %get-tuple-element.31), channel_id=1, source_target_pairs={{0,4},{1,5},{2,6},{3,7},{4,0},{5,1},{6,2},{7,3},{8,12},{9,13},{10,... | collective-permute-start | bytes 196616 | tf_op jit(solution)/shard_map/ppermute | solution.py:422
  20.0 0.1 collective-permute-start.4
  20.1 0.0 copy-done.1
  20.1 0.5 convert_reduce_fusion
  20.6 0.3 fusion.4
  20.9 0.0 copy-done.17
  20.9 0.3 select_reduce_fusion.1
  21.2 0.1 copy.10
  21.3 0.1 copy.11
  21.4 0.1 broadcast_compare_fusion.5
  21.5 0.1 broadcast_compare_fusion.1
  21.6 0.1 broadcast_and_fusion.1
  21.7 0.1 copy.9
  21.8 0.6 select_n.76.table_ref
  22.4 0.1 copy.13
  22.5 0.1 convert_element_type.30
  22.6 0.1 copy.12
  22.6 0.0 collective-permute-done.refs_1_
  22.6 0.0 copy-start.2
  22.6 2.6 %collective-permute-start.5 = (f32[4,32,128]{2,1,0:T(8,128)}, f32[4,32,128]{2,1,0:T(8,128)S(1)}, u32[]{:S(2)}, u32[]{:S(2)}) collective-permute-start(f32[4,32,128]{2,1,0:T(8,128)} %get-tuple-element.33), channel_id=1, source_target_pairs={{0,6},{1,7},{2,4},{3,5},{4,2},{5,3},{6,0},{7,1},{8,14},{9,15},{10,... | collective-permute-start | bytes 196616 | tf_op jit(solution)/shard_map/ppermute | solution.py:422
  25.2 0.0 collective-permute-done.1.refs_2_
  25.3 0.1 collective-permute-start.6
  25.3 0.4 collective-permute-done.2.refs_3_
  25.7 2.2 %collective-permute-start.7 = (f32[4,32,128]{2,1,0:T(8,128)}, f32[4,32,128]{2,1,0:T(8,128)S(1)}, u32[]{:S(2)}, u32[]{:S(2)}) collective-permute-start(f32[4,32,128]{2,1,0:T(8,128)} %get-tuple-element.35), channel_id=1, source_target_pairs={{0,8},{1,9},{2,10},{3,11},{4,12},{5,13},{6,14},{7,15},{8,0},{9,1},... | collective-permute-start | bytes 196616 | tf_op jit(solution)/shard_map/ppermute | solution.py:422
  27.9 6.0 %collective-permute-done.3.refs_4_ = f32[4,32,128]{2,1,0:T(8,128)S(1)} collective-permute-done((f32[4,32,128]{2,1,0:T(8,128)}, f32[4,32,128]{2,1,0:T(8,128)S(1)}, u32[]{:S(2)}, u32[]{:S(2)}) %collective-permute-start.3) | collective-permute-done | bytes 65568 | tf_op jit(solution)/shard_map/ppermute | solution.py:422
  33.9 3.2 %collective-permute-start.8 = (f32[4,32,128]{2,1,0:T(8,128)}, f32[4,32,128]{2,1,0:T(8,128)S(1)}, u32[]{:S(2)}, u32[]{:S(2)}) collective-permute-start(f32[4,32,128]{2,1,0:T(8,128)} %get-tuple-element.36), channel_id=1, source_target_pairs={{0,9},{1,8},{2,11},{3,10},{4,13},{5,12},{6,15},{7,14},{8,1},{9,0},... | collective-permute-start | bytes 196616 | tf_op jit(solution)/shard_map/ppermute | solution.py:422
  37.1 0.0 collective-permute-done.4.refs_5_
  37.1 2.6 %collective-permute-start.9 = (f32[4,32,128]{2,1,0:T(8,128)}, f32[4,32,128]{2,1,0:T(8,128)S(1)}, u32[]{:S(2)}, u32[]{:S(2)}) collective-permute-start(f32[4,32,128]{2,1,0:T(8,128)} %get-tuple-element.37), channel_id=1, source_target_pairs={{0,10},{1,11},{2,8},{3,9},{4,14},{5,15},{6,12},{7,13},{8,2},{9,3},... | collective-permute-start | bytes 196616 | tf_op jit(solution)/shard_map/ppermute | solution.py:422
  39.7 0.6 add_convert_fusion.edges_ref
  40.4 0.0 collective-permute-done.5.refs_6_
  40.4 2.1 %collective-permute-start.10 = (f32[4,32,128]{2,1,0:T(8,128)}, f32[4,32,128]{2,1,0:T(8,128)S(1)}, u32[]{:S(2)}, u32[]{:S(2)}) collective-permute-start(f32[4,32,128]{2,1,0:T(8,128)} %get-tuple-element.38), channel_id=1, source_target_pairs={{0,11},{1,10},{2,9},{3,8},{4,15},{5,14},{6,13},{7,12},{8,3},{9,2},... | collective-permute-start | bytes 196616 | tf_op jit(solution)/shard_map/ppermute | solution.py:422
  42.4 0.0 collective-permute-done.6.refs_7_
  42.4 0.1 collective-permute-start.11
  42.5 7.9 %collective-permute-done.7.refs_8_ = f32[4,32,128]{2,1,0:T(8,128)S(1)} collective-permute-done((f32[4,32,128]{2,1,0:T(8,128)}, f32[4,32,128]{2,1,0:T(8,128)S(1)}, u32[]{:S(2)}, u32[]{:S(2)}) %collective-permute-start.7) | collective-permute-done | bytes 65568 | tf_op jit(solution)/shard_map/ppermute | solution.py:422
  50.4 0.0 collective-permute-start.12
  50.4 0.3 collective-permute-done.8.refs_9_
  50.7 3.0 %collective-permute-start.13 = (f32[4,32,128]{2,1,0:T(8,128)}, f32[4,32,128]{2,1,0:T(8,128)S(1)}, u32[]{:S(2)}, u32[]{:S(2)}) collective-permute-start(f32[4,32,128]{2,1,0:T(8,128)} %get-tuple-element.41), channel_id=1, source_target_pairs={{0,14},{1,15},{2,12},{3,13},{4,10},{5,11},{6,8},{7,9},{8,6},{9,7},... | collective-permute-start | bytes 196616 | tf_op jit(solution)/shard_map/ppermute | solution.py:422
  53.7 0.4 collective-permute-done.9.refs_10_
  54.1 1.9 %collective-permute-start.14 = (f32[4,32,128]{2,1,0:T(8,128)}, f32[4,32,128]{2,1,0:T(8,128)S(1)}, u32[]{:S(2)}, u32[]{:S(2)}) collective-permute-start(f32[4,32,128]{2,1,0:T(8,128)} %get-tuple-element.42), channel_id=1, source_target_pairs={{0,15},{1,14},{2,13},{3,12},{4,11},{5,10},{6,9},{7,8},{8,7},{9,6},... | collective-permute-start | bytes 196616 | tf_op jit(solution)/shard_map/ppermute | solution.py:422
  56.0 0.6 add_convert_fusion.1.ends_ref
  56.6 0.0 all-to-all-done.in_ref
  56.6 1.0 %copy-done = f32[16,144,128]{2,1,0:T(8,128)} copy-done((f32[16,144,128]{2,1,0:T(8,128)}, f32[16,144,128]{2,1,0:T(8,128)S(1)}, u32[]{:S(2)}) %copy-start) | copy-done | bytes 1179672
  57.6 6.6 %shard_map.65 = (f32[8,144,128]{2,1,0:T(8,128)}, f32[32,128]{1,0:T(8,128)}) custom-call(s32[1]{0:T(128)} %bitcast.own_ref, s32[64]{0:T(128)} %select_n.76.table_ref, s32[2]{0:T(128)} %add_convert_fusion.1.ends_ref, f32[16,144,128]{2,1,0:T(8,128)} %copy-done, f32[2,16,128]{2,1,0:T(8,128)} %add_convert_fusion.edges_ref, f32[25,80,128]{2,1,0:T(8,128)} %constant.68.clone.coef_ref), custom_call_target="tpu_custom_call" | custom-call | flops 10747904 | bytes 1048576 | tf_op jit(solution)/shard_map/pallas_call | solution.py:459
  64.1 0.0 collective-permute-done.10.refs_11_
  64.2 0.0 collective-permute-done.11.refs_12_
  64.2 0.0 copy-start.13
  64.2 0.0 collective-permute-done.12.refs_13_
  64.2 0.0 collective-permute-done.13.refs_14_
  64.2 0.0 copy-start.15
  64.2 0.0 collective-permute-done.14.refs_15_
  64.3 0.4 copy-done.12
  64.8 0.0 copy-done.13
  64.8 0.0 copy-done.14
  64.8 0.0 copy-done.15
  64.8 0.0 copy-done.16
  64.9 4.1 %shard_map.67 = (f32[8,128,128]{2,1,0:T(8,128)}, f32[16,8,128]{2,1,0:T(8,128)}) custom-call(s32[1]{0:T(128)} %bitcast.own_ref, s32[64]{0:T(128)} %select_n.76.table_ref, f32[8,144,128]{2,1,0:T(8,128)} %get-tuple-element.25.ext_ref, f32[32,128]{1,0:T(8,128)} %get-tuple-element.26.gram_ref, f32[4,32,128]{2,1,0:T(8,128)} %get-tuple-element.27.refs_0_, ...), custom_call_target="tpu_custom_call" | custom-call | flops 6553600 | bytes 2097152 | tf_op jit(solution)/shard_map/pallas_call | solution.py:473
  69.0 11.7 %all_to_all.10.fit_ref = f32[16,8,128]{2,1,0:T(8,128)} all-to-all(f32[16,8,128]{2,1,0:T(8,128)} %get-tuple-element.43), channel_id=1, replica_groups=mesh['field'=2,'ccd'=16] {'ccd'}, dimensions={0} | all-to-all | bytes 131072 | tf_op jit(solution)/shard_map/all_to_all | solution.py:485
  80.7 6.1 %shard_map.68 = f32[128,1024]{1,0:T(8,128)} custom-call(f32[16,8,128]{2,1,0:T(8,128)} %all_to_all.10.fit_ref, f32[8,144,128]{2,1,0:T(8,128)} %get-tuple-element.25.ext_ref, f32[8,128,128]{2,1,0:T(8,128)} %get-tuple-element.44.sci_ref), custom_call_target="tpu_custom_call" | custom-call | flops 6553600 | bytes 1572864 | tf_op jit(solution)/shard_map/pallas_call | solution.py:487
  (33 shorter events, 0.1 us)
Async XLA Ops:
  4.5 15.6 %copy-start.1 = (s32[16,32,1]{1,2,0:T(1,128)S(1)}, s32[16,32,1]{1,2,0:T(1,128)}, u32[]{:S(2)}) copy-start(s32[16,32,1]{1,2,0:T(1,128)} %param.9) | copy-start | bytes 6148
  4.5 16.4 %copy-start.17 = (s32[16,32]{1,0:T(8,128)S(1)}, s32[16,32]{1,0:T(8,128)}, u32[]{:S(2)}) copy-start(s32[16,32]{1,0:T(8,128)} %param.10) | copy-start | bytes 6148
  4.5 52.1 %all-to-all-start = ((f32[16,144,128]{2,1,0:T(8,128)}), f32[16,144,128]{2,1,0:T(8,128)S(1)}, u32[]{:S(2)}, u32[]{:S(2)}) async-start(f32[16,144,128]{2,1,0:T(8,128)} %shard_map.64), calls=%async_computation | async-start | bytes 2359296 | tf_op jit(solution)/shard_map/all_to_all | solution.py:418
  16.2 6.4 %collective-permute-start = (f32[4,32,128]{2,1,0:T(8,128)}, f32[4,32,128]{2,1,0:T(8,128)S(1)}, u32[]{:S(2)}, u32[]{:S(2)}) collective-permute-start(f32[4,32,128]{2,1,0:T(8,128)} %get-tuple-element.28), channel_id=1, source_target_pairs={{0,1},{1,0},{2,3},{3,2},{4,5},{5,4},{6,7},{7,6},{8,9},{9,8},{10,11... | collective-permute-start | bytes 196616 | tf_op jit(solution)/shard_map/ppermute | solution.py:422
  16.6 8.6 %collective-permute-start.1 = (f32[4,32,128]{2,1,0:T(8,128)}, f32[4,32,128]{2,1,0:T(8,128)S(1)}, u32[]{:S(2)}, u32[]{:S(2)}) collective-permute-start(f32[4,32,128]{2,1,0:T(8,128)} %get-tuple-element.29), channel_id=1, source_target_pairs={{0,2},{1,3},{2,0},{3,1},{4,6},{5,7},{6,4},{7,5},{8,10},{9,11},{10,... | collective-permute-start | bytes 196616 | tf_op jit(solution)/shard_map/ppermute | solution.py:422
  18.2 7.5 %collective-permute-start.2 = (f32[4,32,128]{2,1,0:T(8,128)}, f32[4,32,128]{2,1,0:T(8,128)S(1)}, u32[]{:S(2)}, u32[]{:S(2)}) collective-permute-start(f32[4,32,128]{2,1,0:T(8,128)} %get-tuple-element.30), channel_id=1, source_target_pairs={{0,3},{1,2},{2,1},{3,0},{4,7},{5,6},{6,5},{7,4},{8,11},{9,10},{10,... | collective-permute-start | bytes 196616 | tf_op jit(solution)/shard_map/ppermute | solution.py:422
  18.3 15.6 %collective-permute-start.3 = (f32[4,32,128]{2,1,0:T(8,128)}, f32[4,32,128]{2,1,0:T(8,128)S(1)}, u32[]{:S(2)}, u32[]{:S(2)}) collective-permute-start(f32[4,32,128]{2,1,0:T(8,128)} %get-tuple-element.31), channel_id=1, source_target_pairs={{0,4},{1,5},{2,6},{3,7},{4,0},{5,1},{6,2},{7,3},{8,12},{9,13},{10,... | collective-permute-start | bytes 196616 | tf_op jit(solution)/shard_map/ppermute | solution.py:422
  20.0 17.1 %collective-permute-start.4 = (f32[4,32,128]{2,1,0:T(8,128)}, f32[4,32,128]{2,1,0:T(8,128)S(1)}, u32[]{:S(2)}, u32[]{:S(2)}) collective-permute-start(f32[4,32,128]{2,1,0:T(8,128)} %get-tuple-element.32), channel_id=1, source_target_pairs={{0,5},{1,4},{2,7},{3,6},{4,1},{5,0},{6,3},{7,2},{8,13},{9,12},{10,... | collective-permute-start | bytes 196616 | tf_op jit(solution)/shard_map/ppermute | solution.py:422
  22.6 41.6 %copy-start.2 = (f32[4,32,128]{2,1,0:T(8,128)}, f32[4,32,128]{2,1,0:T(8,128)S(1)}, u32[]{:S(2)}) copy-start(f32[4,32,128]{2,1,0:T(8,128)S(1)} %collective-permute-done.refs_1_) | copy-start | bytes 196612
  22.6 17.7 %collective-permute-start.5 = (f32[4,32,128]{2,1,0:T(8,128)}, f32[4,32,128]{2,1,0:T(8,128)S(1)}, u32[]{:S(2)}, u32[]{:S(2)}) collective-permute-start(f32[4,32,128]{2,1,0:T(8,128)} %get-tuple-element.33), channel_id=1, source_target_pairs={{0,6},{1,7},{2,4},{3,5},{4,2},{5,3},{6,0},{7,1},{8,14},{9,15},{10,... | collective-permute-start | bytes 196616 | tf_op jit(solution)/shard_map/ppermute | solution.py:422
  25.2 39.0 %copy-start.3 = (f32[4,32,128]{2,1,0:T(8,128)}, f32[4,32,128]{2,1,0:T(8,128)S(1)}, u32[]{:S(2)}) copy-start(f32[4,32,128]{2,1,0:T(8,128)S(1)} %collective-permute-done.1.refs_2_) | copy-start | bytes 196612
  25.3 17.2 %collective-permute-start.6 = (f32[4,32,128]{2,1,0:T(8,128)}, f32[4,32,128]{2,1,0:T(8,128)S(1)}, u32[]{:S(2)}, u32[]{:S(2)}) collective-permute-start(f32[4,32,128]{2,1,0:T(8,128)} %get-tuple-element.34), channel_id=1, source_target_pairs={{0,7},{1,6},{2,5},{3,4},{4,3},{5,2},{6,1},{7,0},{8,15},{9,14},{10,... | collective-permute-start | bytes 196616 | tf_op jit(solution)/shard_map/ppermute | solution.py:422
  25.7 38.5 %copy-start.4 = (f32[4,32,128]{2,1,0:T(8,128)}, f32[4,32,128]{2,1,0:T(8,128)S(1)}, u32[]{:S(2)}) copy-start(f32[4,32,128]{2,1,0:T(8,128)S(1)} %collective-permute-done.2.refs_3_) | copy-start | bytes 196612
  25.7 24.7 %collective-permute-start.7 = (f32[4,32,128]{2,1,0:T(8,128)}, f32[4,32,128]{2,1,0:T(8,128)S(1)}, u32[]{:S(2)}, u32[]{:S(2)}) collective-permute-start(f32[4,32,128]{2,1,0:T(8,128)} %get-tuple-element.35), channel_id=1, source_target_pairs={{0,8},{1,9},{2,10},{3,11},{4,12},{5,13},{6,14},{7,15},{8,0},{9,1},... | collective-permute-start | bytes 196616 | tf_op jit(solution)/shard_map/ppermute | solution.py:422
  33.9 30.4 %copy-start.5 = (f32[4,32,128]{2,1,0:T(8,128)}, f32[4,32,128]{2,1,0:T(8,128)S(1)}, u32[]{:S(2)}) copy-start(f32[4,32,128]{2,1,0:T(8,128)S(1)} %collective-permute-done.3.refs_4_) | copy-start | bytes 196612
  33.9 16.8 %collective-permute-start.8 = (f32[4,32,128]{2,1,0:T(8,128)}, f32[4,32,128]{2,1,0:T(8,128)S(1)}, u32[]{:S(2)}, u32[]{:S(2)}) collective-permute-start(f32[4,32,128]{2,1,0:T(8,128)} %get-tuple-element.36), channel_id=1, source_target_pairs={{0,9},{1,8},{2,11},{3,10},{4,13},{5,12},{6,15},{7,14},{8,1},{9,0},... | collective-permute-start | bytes 196616 | tf_op jit(solution)/shard_map/ppermute | solution.py:422
  37.1 27.2 %copy-start.6 = (f32[4,32,128]{2,1,0:T(8,128)}, f32[4,32,128]{2,1,0:T(8,128)S(1)}, u32[]{:S(2)}) copy-start(f32[4,32,128]{2,1,0:T(8,128)S(1)} %collective-permute-done.4.refs_5_) | copy-start | bytes 196612
  37.1 17.0 %collective-permute-start.9 = (f32[4,32,128]{2,1,0:T(8,128)}, f32[4,32,128]{2,1,0:T(8,128)S(1)}, u32[]{:S(2)}, u32[]{:S(2)}) collective-permute-start(f32[4,32,128]{2,1,0:T(8,128)} %get-tuple-element.37), channel_id=1, source_target_pairs={{0,10},{1,11},{2,8},{3,9},{4,14},{5,15},{6,12},{7,13},{8,2},{9,3},... | collective-permute-start | bytes 196616 | tf_op jit(solution)/shard_map/ppermute | solution.py:422
  40.4 23.9 %copy-start.7 = (f32[4,32,128]{2,1,0:T(8,128)}, f32[4,32,128]{2,1,0:T(8,128)S(1)}, u32[]{:S(2)}) copy-start(f32[4,32,128]{2,1,0:T(8,128)S(1)} %collective-permute-done.5.refs_6_) | copy-start | bytes 196612
  40.4 23.8 %collective-permute-start.10 = (f32[4,32,128]{2,1,0:T(8,128)}, f32[4,32,128]{2,1,0:T(8,128)S(1)}, u32[]{:S(2)}, u32[]{:S(2)}) collective-permute-start(f32[4,32,128]{2,1,0:T(8,128)} %get-tuple-element.38), channel_id=1, source_target_pairs={{0,11},{1,10},{2,9},{3,8},{4,15},{5,14},{6,13},{7,12},{8,3},{9,2},... | collective-permute-start | bytes 196616 | tf_op jit(solution)/shard_map/ppermute | solution.py:422
  42.4 21.9 %copy-start.8 = (f32[4,32,128]{2,1,0:T(8,128)}, f32[4,32,128]{2,1,0:T(8,128)S(1)}, u32[]{:S(2)}) copy-start(f32[4,32,128]{2,1,0:T(8,128)S(1)} %collective-permute-done.6.refs_7_) | copy-start | bytes 196612
  42.4 21.7 %collective-permute-start.11 = (f32[4,32,128]{2,1,0:T(8,128)}, f32[4,32,128]{2,1,0:T(8,128)S(1)}, u32[]{:S(2)}, u32[]{:S(2)}) collective-permute-start(f32[4,32,128]{2,1,0:T(8,128)} %get-tuple-element.39), channel_id=1, source_target_pairs={{0,12},{1,13},{2,14},{3,15},{4,8},{5,9},{6,10},{7,11},{8,4},{9,5},... | collective-permute-start | bytes 196616 | tf_op jit(solution)/shard_map/ppermute | solution.py:422
  50.4 13.9 %copy-start.9 = (f32[4,32,128]{2,1,0:T(8,128)}, f32[4,32,128]{2,1,0:T(8,128)S(1)}, u32[]{:S(2)}) copy-start(f32[4,32,128]{2,1,0:T(8,128)S(1)} %collective-permute-done.7.refs_8_) | copy-start | bytes 196612
  50.4 13.8 %collective-permute-start.12 = (f32[4,32,128]{2,1,0:T(8,128)}, f32[4,32,128]{2,1,0:T(8,128)S(1)}, u32[]{:S(2)}, u32[]{:S(2)}) collective-permute-start(f32[4,32,128]{2,1,0:T(8,128)} %get-tuple-element.40), channel_id=1, source_target_pairs={{0,13},{1,12},{2,15},{3,14},{4,9},{5,8},{6,11},{7,10},{8,5},{9,4},... | collective-permute-start | bytes 196616 | tf_op jit(solution)/shard_map/ppermute | solution.py:422
  50.7 13.6 %copy-start.10 = (f32[4,32,128]{2,1,0:T(8,128)}, f32[4,32,128]{2,1,0:T(8,128)S(1)}, u32[]{:S(2)}) copy-start(f32[4,32,128]{2,1,0:T(8,128)S(1)} %collective-permute-done.8.refs_9_) | copy-start | bytes 196612
  50.7 13.5 %collective-permute-start.13 = (f32[4,32,128]{2,1,0:T(8,128)}, f32[4,32,128]{2,1,0:T(8,128)S(1)}, u32[]{:S(2)}, u32[]{:S(2)}) collective-permute-start(f32[4,32,128]{2,1,0:T(8,128)} %get-tuple-element.41), channel_id=1, source_target_pairs={{0,14},{1,15},{2,12},{3,13},{4,10},{5,11},{6,8},{7,9},{8,6},{9,7},... | collective-permute-start | bytes 196616 | tf_op jit(solution)/shard_map/ppermute | solution.py:422
  54.1 10.2 %copy-start.11 = (f32[4,32,128]{2,1,0:T(8,128)}, f32[4,32,128]{2,1,0:T(8,128)S(1)}, u32[]{:S(2)}) copy-start(f32[4,32,128]{2,1,0:T(8,128)S(1)} %collective-permute-done.9.refs_10_) | copy-start | bytes 196612
  54.1 10.1 %collective-permute-start.14 = (f32[4,32,128]{2,1,0:T(8,128)}, f32[4,32,128]{2,1,0:T(8,128)S(1)}, u32[]{:S(2)}, u32[]{:S(2)}) collective-permute-start(f32[4,32,128]{2,1,0:T(8,128)} %get-tuple-element.42), channel_id=1, source_target_pairs={{0,15},{1,14},{2,13},{3,12},{4,11},{5,10},{6,9},{7,8},{8,7},{9,6},... | collective-permute-start | bytes 196616 | tf_op jit(solution)/shard_map/ppermute | solution.py:422
  56.6 1.0 %copy-start = (f32[16,144,128]{2,1,0:T(8,128)}, f32[16,144,128]{2,1,0:T(8,128)S(1)}, u32[]{:S(2)}) copy-start(f32[16,144,128]{2,1,0:T(8,128)S(1)} %all-to-all-done.in_ref) | copy-start | bytes 3538948
  64.1 0.6 copy-start.12
  64.2 0.6 copy-start.13
  64.2 0.6 copy-start.14
  64.2 0.6 copy-start.15
  64.2 0.7 copy-start.16

commit v2 on v1

--- a/solution.py
+++ b/solution.py
@@ -29,6 +29,8 @@
 )
 MAX_PERMUTES = 32
 UNROLL = 4
+STEP = 4
+GROUP = 5
 RHS_LANE = KB
 
 
@@ -43,16 +45,17 @@
     )
 
 
-def call(kernel, out_shape, in_specs, scratch, flops, moved, grid=()):
+def call(kernel, out_shape, in_specs, scratch, flops, moved, grid=(), room=16, out=VMEM):
     many = isinstance(out_shape, (list, tuple))
     return pl.pallas_call(
         kernel,
         out_shape=out_shape,
         grid=grid,
         in_specs=in_specs,
-        out_specs=[VMEM] * len(out_shape) if many else VMEM,
+        out_specs=[out] * len(out_shape) if many else out,
         scratch_shapes=scratch,
         cost_estimate=pl.CostEstimate(flops=flops, bytes_accessed=moved, transcendentals=0),
+        compiler_params=pltpu.CompilerParams(vmem_limit_bytes=room << 20 if room else None),
     )
 
 
@@ -91,9 +94,9 @@
 
 
 def warp_kernel(
-    visit, devices, cap, paired, strips, own_ref, tgt_ref, shift_ref, frac_ref, x_ref, *refs
+    visit, devices, cap, paired, own_ref, tgt_ref, shift_ref, frac_ref, x_ref, *refs
 ):
-    outs, (mid, blocks, inv, cnt) = refs[:-4], refs[-4:]
+    outs, (mid, blocks, edges, inv, cnt, where, sems) = refs[:-7], refs[-7:]
     rows, columns = x_ref.shape
     slabs, tiles = columns // LANES, rows // SUB
     own = own_ref[0]
@@ -109,7 +112,9 @@
         c = cnt[p]
         cnt[p] = c + 1
         k = jnp.bitwise_xor(p, own) if paired else p
-        inv[k * cap + jnp.minimum(c, cap - 1)] = b
+        at = k * cap + jnp.minimum(c, cap - 1)
+        inv[at] = b
+        where[b] = at
 
     col_w = tap_weights(shift_ref[visit, 0, 1], frac_ref[visit, 0, 1], lane)
     row_w = tap_weights(shift_ref[visit, 0, 0], frac_ref[visit, 0, 0], lane)
@@ -117,18 +122,33 @@
         mid[j, 0:SUB, :] = jnp.zeros((SUB, LANES), jnp.float32)
         mid[j, SUB + rows :, :] = jnp.zeros((SUB, LANES), jnp.float32)
 
-    @pl.loop(0, tiles, unroll=UNROLL)
-    def _(t):
+    def column_pass(t):
         for b in range(NB // tiles):
             book(t * (NB // tiles) + b)
         at = pl.multiple_of(t * SUB, SUB)
         parts = [x_ref[pl.ds(at, SUB), j * LANES : (j + 1) * LANES] for j in range(slabs)]
-        total = [jnp.zeros((SUB, LANES), jnp.float32)] * slabs
-        for n, d in enumerate(TAPS):
-            moved = shifted(parts, -d, lane)
-            total = [a + col_w[n] * m for a, m in zip(total, moved)]
+        zero = jnp.zeros((SUB, LANES), jnp.float32)
+        ahead = [shifted([zero] + parts, -b, lane) for b in range(STEP)]
+        total = [zero] * slabs
+        for a in sorted({d // STEP for d in TAPS}):
+            group = [zero] * (slabs + 1)
+            for n, d in enumerate(TAPS):
+                if d // STEP == a:
+                    group = [g + col_w[n] * m for g, m in zip(group, ahead[d - STEP * a])]
+            moved = shifted(group, -STEP * a, lane)[1:]
+            total = [x + m for x, m in zip(total, moved)]
         for j in range(slabs):
             mid[j, pl.ds(at + SUB, SUB), :] = total[j]
+
+    @pl.loop(0, rows // BR)
+    def _(band):
+        for t in range(BR // SUB):
+            column_pass(band * (BR // SUB) + t)
+
+    def send(b):
+        p, r = lax.div(where[b], cap), lax.rem(where[b], cap)
+        to = outs[0].at[p, pl.ds(pl.multiple_of(r * BR, BR), BR), :]
+        return pltpu.make_async_copy(blocks.at[b], to, sems.at[b])
 
     @pl.loop(0, slabs)
     def _(j):
@@ -139,59 +159,76 @@
                 total = total + row_w[n] * mid[j, first + d : first + d + SUB, :]
             inner = (t * SUB) % BR
             blocks[(t * SUB) // BR * slabs + j, inner : inner + SUB, :] = total
+        if not paired:
+            for band in range(rows // BR):
+                send(band * slabs + j).start()
 
     if paired:
         for k in range(devices):
             for r in range(cap):
-                outs[k][r] = blocks[inv[k * cap + r]]
-    else:
-
-        @pl.loop(0, devices)
-        def _(p):
-            for r in range(cap):
-                outs[0][p, r * BR : (r + 1) * BR, :] = blocks[inv[p * cap + r]]
-            if strips:
-                before = jnp.maximum(p - 1, 0)
-                after = jnp.minimum(p + 1, devices - 1)
-                outs[0][p, cap * BR :, :] = jnp.zeros((2 * SUB, LANES), jnp.float32)
-                for r in range(cap):
-                    at = cap * BR + REACH * r
-                    outs[0][p, at : at + REACH, :] = blocks[
-                        inv[before * cap + r], BR - REACH : BR, :
-                    ]
-                    at = at + SUB
-                    outs[0][p, at : at + REACH, :] = blocks[inv[after * cap + r], 0:REACH, :]
+                outs[k][r * BR : (r + 1) * BR, :] = blocks[inv[k * cap + r]]
+        return
+
+    @pl.loop(0, devices)
+    def _(p):
+        before, after = jnp.maximum(p - 1, 0), jnp.minimum(p + 1, devices - 1)
+        edges[p] = jnp.zeros((2 * SUB, LANES), jnp.float32)
+        for r in range(cap):
+            at = REACH * r
+            edges[p, at : at + REACH, :] = blocks[inv[before * cap + r], BR - REACH : BR, :]
+            at = SUB + REACH * r
+            edges[p, at : at + REACH, :] = blocks[inv[after * cap + r], 0:REACH, :]
+
+    last = pltpu.make_async_copy(edges, outs[0].at[:, cap * BR :, :], sems.at[NB])
+    last.start()
+    last.wait()
+
+    @pl.loop(0, NB)
+    def _(b):
+        send(b).wait()
 
 
 def sum_blocks(devices, cap, paired, own, table_ref, ins, acc):
     acc[...] = jnp.zeros_like(acc)
+
+    def add(chunk, c):
+        for r in range(cap):
+            slot = table_ref[c * cap + r]
+            acc[slot] = acc[slot] + chunk[r * BR : (r + 1) * BR, :]
+
     if paired:
         for k in range(devices):
-            for r in range(cap):
-                slot = table_ref[jnp.bitwise_xor(own, k) * cap + r]
-                acc[slot] = acc[slot] + ins[k][r]
+            add(ins[k], jnp.bitwise_xor(own, k))
     else:
 
         @pl.loop(0, devices)
         def _(c):
-            for r in range(cap):
-                slot = table_ref[c * cap + r]
-                acc[slot] = acc[slot] + ins[0][c, r * BR : (r + 1) * BR, :]
+            add(ins[0].at[c], c)
 
 
 def template_kernel(
-    devices, cap, own_ref, table_ref, ends_ref, in_ref, edges_ref, coef_ref,
-    ext_ref, gram_ref, acc, lagged, gen, spec,
+    devices, cap, paired, own_ref, table_ref, ends_ref, edges_ref, coef_ref, *refs
 ):
-    slabs, rows = ext_ref.shape[0], ext_ref.shape[1] - 2 * SUB
+    ins, (cols_ref, gram_ref, acc, far, gen, spec) = refs[:-6], refs[-6:]
+    slabs, rows = cols_ref.shape[1], cols_ref.shape[2] - 2 * SUB
+    ext_ref = cols_ref.at[REACH]
+
+    def lagged(lag):
+        if abs(lag) <= REACH:
+            return cols_ref.at[REACH - lag]
+        return far.at[lag + KSIDE - 1 if lag < 0 else lag + KSIDE - 1 - KSIDE]
+
     tiles = rows // SUB
     lane = lane_ids()
     sub = lax.broadcasted_iota(jnp.int32, (SUB, LANES), 0)
-    sum_blocks(devices, cap, False, own_ref[0], table_ref, [in_ref], acc)
+    sum_blocks(devices, cap, paired, own_ref[0], table_ref, ins, acc)
 
     for end in range(2):
         at = cap * BR + end * SUB
-        strip = in_ref[:, at : at + SUB, :].reshape(devices * SUB, LANES)
+        if paired:
+            strip = jnp.concatenate([chunk[at : at + SUB, :] for chunk in ins], axis=0)
+        else:
+            strip = ins[0][:, at : at + SUB, :].reshape(devices * SUB, LANES)
         edge = mm(edges_ref[end], strip)
         first = SUB - REACH if end == 0 else SUB + rows
         for j in range(slabs):
@@ -201,11 +238,12 @@
                 ext_ref[j, first + i : first + i + 1, :] = edge[i * slabs + j : i * slabs + j + 1]
 
     def lag_tile(parts, at):
-        for n, lag in enumerate(LAGS):
+        for lag in LAGS:
             for j, moved in enumerate(shifted(parts, lag, lane)):
-                lagged[n, j, at, :] = moved
-
-    lag_tile([ext_ref[j, 0:SUB, :] for j in range(slabs)], slice(0, SUB))
+                lagged(lag)[j, at, :] = moved
+
+    for at in (slice(0, SUB), slice(SUB + rows, 2 * SUB + rows)):
+        lag_tile([ext_ref[j, at, :] for j in range(slabs)], at)
     for band in range(rows // BR):
 
         @pl.loop(0, BR // SUB, unroll=UNROLL)
@@ -213,8 +251,6 @@
             at = pl.ds(pl.multiple_of(t * SUB, SUB), SUB)
             to = pl.ds(pl.multiple_of(SUB + band * BR + t * SUB, SUB), SUB)
             parts = [acc[band * slabs + j, at, :] for j in range(slabs)]
-            for j in range(slabs):
-                ext_ref[j, to, :] = parts[j]
             lag_tile(parts, to)
 
     gen[...] = jnp.zeros_like(gen)
@@ -224,7 +260,7 @@
     def _(j):
         def first(t, down, lag):
             base = SUB + t * SUB - down // 2
-            return lagged[lag + KSIDE - 1, j, base : base + SUB, :]
+            return lagged(lag)[j, base : base + SUB, :]
 
         def second(t, down):
             base = SUB + t * SUB + down
@@ -267,41 +303,29 @@
     gram_ref[...] = total + jnp.where(row == column, 0.0, flipped)
 
 
-def science_kernel(devices, cap, paired, own_ref, table_ref, ext_ref, gram_ref, *refs):
-    ins, (out, fit_ref, acc, moved, sums_ref) = refs[:-5], refs[-5:]
-    slabs, rows, _ = out.shape
-    lane = lane_ids()
-    sum_blocks(devices, cap, paired, own_ref[0], table_ref, ins, acc)
-
-    for band in range(rows // BR):
-
-        @pl.loop(0, BR // SUB, unroll=UNROLL)
-        def _(t):
-            at = pl.ds(pl.multiple_of(t * SUB, SUB), SUB)
-            to = pl.ds(pl.multiple_of(band * BR + t * SUB, SUB), SUB)
-            parts = [acc[band * slabs + j, at, :] for j in range(slabs)]
-            for j in range(slabs):
-                out[j, to, :] = parts[j]
-            for q in range(KSIDE):
-                for j, part in enumerate(shifted(parts, q - REACH, lane)):
-                    moved[q, j, to, :] = part
-
-    def slab(j, sums):
-        sums = list(sums)
+def science_kernel(devices, cap, paired, own_ref, table_ref, cols_ref, gram_ref, *refs):
+    ins, (out, fit_ref, sums_ref) = refs[:-3], refs[-3:]
+    slabs, rows = cols_ref.shape[1], cols_ref.shape[2] - 2 * SUB
+    sum_blocks(devices, cap, paired, own_ref[0], table_ref, ins, out)
+
+    sums_ref[...] = jnp.zeros_like(sums_ref)
+
+    @pl.loop(0, slabs)
+    def _(j):
+        sums = [None] * KB
         for t in range(rows // SUB):
             base = SUB + t * SUB - REACH
-            seconds = [moved[q, j, t * SUB : (t + 1) * SUB, :] for q in range(KSIDE)]
+            inner = (t * SUB) % BR
+            target = out[(t * SUB) // BR * slabs + j, inner : inner + SUB, :]
             for r in range(KSIDE):
-                first = ext_ref[j, base + r : base + r + SUB, :]
                 for q in range(KSIDE):
-                    sums[r * KSIDE + q] = sums[r * KSIDE + q] + first * seconds[q]
-        return tuple(sums)
-
-    sums = lax.fori_loop(0, slabs, slab, (jnp.zeros((SUB, LANES), jnp.float32),) * KB)
-    sums_ref[...] = jnp.zeros_like(sums_ref)
-    for i in range(KB):
-        sums_ref[i : i + 1, :] = jnp.sum(sums[i], axis=0, keepdims=True)
-    rhs = jnp.sum(sums_ref[...], axis=1, keepdims=True)
+                    i = r * KSIDE + q
+                    term = cols_ref[q, j, base + r : base + r + SUB, :] * target
+                    sums[i] = term if sums[i] is None else sums[i] + term
+        for i in range(KB):
+            sums_ref[i] = sums_ref[i] + sums[i]
+
+    rhs = jnp.sum(jnp.sum(sums_ref[...], axis=1), axis=1, keepdims=True)
     size = gram_ref.shape[0]
     column = lax.broadcasted_iota(jnp.int32, (size, LANES), 1)
     joined = jnp.where(column == RHS_LANE, rhs, gram_ref[...])
@@ -323,43 +347,44 @@
     trace = jnp.sum(jnp.where(diagonal, work, 0.0), axis=(0, 1), keepdims=True)
     ridge = 0.001 * trace / KB + 1.0
     work = jnp.where(lane < size, jnp.where(diagonal, work + ridge, work), 0.0)
-    for i in range(KB):
-        pivot = work[i : i + 1, :] / work[i : i + 1, i : i + 1]
-        work = jnp.where(row == i, pivot, work - work[:, i : i + 1] * pivot)
+    for base in range(0, KB, GROUP):
+        group = [
+            jnp.broadcast_to(work[:, i : i + 1], (size, LANES)) for i in range(base, base + GROUP)
+        ]
+        for k, column in enumerate(group):
+            i = base + k
+            inverse = 1.0 / column[i : i + 1]
+
+            def eliminated(values):
+                pivot = values[i : i + 1] * inverse
+                return jnp.where(row == i, pivot, values - column * pivot)
+
+            group[k + 1 :] = [eliminated(c) for c in group[k + 1 :]]
+            work = eliminated(work)
     return work[:, RHS_LANE : RHS_LANE + 1]
 
 
-def difference_kernel(fit_ref, ext_ref, sci_ref, out_ref, rowed):
-    slabs, rows, _ = sci_ref.shape
-    lane = lane_ids()
+def difference_kernel(fit_ref, cols_ref, sci_ref, out_ref):
+    slabs, rows = cols_ref.shape[1], cols_ref.shape[2] - 2 * SUB
     shared = fit_ref[0]
     for k in range(1, fit_ref.shape[0]):
         shared = shared + fit_ref[k]
     kernel = solved(shared, NB)
     taps = [jnp.broadcast_to(kernel[i : i + 1, :], (SUB, LANES)) for i in range(KB)]
 
-    @pl.loop(0, slabs)
-    def _(j):
-        for t in range(rows // SUB):
-            base = SUB + t * SUB - REACH
-            sums = [None] * KSIDE
-            for r in range(KSIDE):
-                part = ext_ref[j, base + r : base + r + SUB, :]
-                for q in range(KSIDE):
-                    term = taps[r * KSIDE + q] * part
-                    sums[q] = term if sums[q] is None else sums[q] + term
-            for q in range(KSIDE):
-                rowed[q, j, t * SUB : (t + 1) * SUB, :] = sums[q]
-
-    @pl.loop(0, rows // SUB, unroll=UNROLL)
-    def _(t):
-        at = pl.ds(pl.multiple_of(t * SUB, SUB), SUB)
-        total = [jnp.zeros((SUB, LANES), jnp.float32)] * slabs
-        for q in range(KSIDE):
-            parts = [rowed[q, j, at, :] for j in range(slabs)]
-            total = [a + m for a, m in zip(total, shifted(parts, REACH - q, lane))]
+    @pl.loop(0, rows // BR)
+    def _(band):
         for j in range(slabs):
-            out_ref[at, j * LANES : (j + 1) * LANES] = sci_ref[j, at, :] - total[j]
+            for t in range(BR // SUB):
+                total = None
+                for r in range(KSIDE):
+                    for q in range(KSIDE):
+                        at = pl.ds(band * BR + SUB + t * SUB + r - REACH, SUB)
+                        term = taps[r * KSIDE + q] * cols_ref[q, j, at, :]
+                        total = term if total is None else total + term
+                science = sci_ref[band * slabs + j, t * SUB : (t + 1) * SUB, :]
+                at = pl.ds(pl.multiple_of(band * BR + t * SUB, SUB), SUB)
+                out_ref[at, j * LANES : (j + 1) * LANES] = science - total
 
 
 def by_permutes(devices):
@@ -395,23 +420,26 @@
     pixels = rows * columns
 
     def warped(visit, paired):
-        out = call(
-            functools.partial(warp_kernel, visit, devices, cap, paired, visit == 0),
-            [f32(cap, BR, BC)] * devices
-            if paired
-            else [f32(devices, cap * BR + (2 * SUB if visit == 0 else 0), BC)],
+        packed = [f32(cap * BR, BC)] * devices if paired else [f32(devices, cap * BR + 2 * SUB, BC)]
+        return call(
+            functools.partial(warp_kernel, visit, devices, cap, paired),
+            packed,
             [SMEM, SMEM, SMEM, SMEM, pl.BlockSpec((None, rows, columns), lambda i: (visit, 0, 0))],
             [
                 pltpu.VMEM((slabs, rows + 2 * SUB, LANES), jnp.float32),
                 pltpu.VMEM((NB, BR, BC), jnp.float32),
+                pltpu.VMEM((devices, 2 * SUB, LANES), jnp.float32),
                 pltpu.SMEM((devices * cap,), jnp.int32),
                 pltpu.SMEM((devices,), jnp.int32),
+                pltpu.SMEM((NB,), jnp.int32),
+                pltpu.SemaphoreType.DMA((NB + 1,)),
             ],
             40 * pixels,
             4 * pixels * 3,
-            (1,),
+            grid=(1,),
+            room=0 if visit == 0 else 16,
+            out=VMEM if paired else pl.BlockSpec(memory_space=pltpu.HBM),
         )(own, targets, lanczos_shift, lanczos_frac, exposures)
-        return out
 
     def exchanged(chunks):
         if len(chunks) == 1:
@@ -445,53 +473,44 @@
     spare = ((0, 0), (0, SUB // REACH - cap))
 
     def edge_rows(patch, first_slot):
-        slots = jnp.pad(slots_at(patch), spare, constant_values=NB)[None, :, :, None]
+        slots = jnp.pad(slots_at(patch), spare, constant_values=NB)
+        slots = slots[None, :, :, None]
         hit = (slots - first_slot == wanted % slabs) & (row_of == wanted // slabs)
         return hit.astype(jnp.float32).reshape(REACH * slabs, devices * SUB)
 
     edges = jnp.stack([edge_rows(owner - 1, NB - slabs), edge_rows(owner + 1, 0)])
 
-    slab_shape = f32(slabs, rows, LANES)
     sums = pltpu.VMEM((NB + 1, BR, BC), jnp.float32)
     size = NB
     count, coef = gram_table()
     at_ends = jnp.stack([owner == 0, owner == devices - 1]).astype(jnp.int32)
-    extended, gram = call(
-        functools.partial(template_kernel, devices, cap),
-        [f32(slabs, rows + 2 * SUB, LANES), f32(size, LANES)],
-        [SMEM, SMEM, SMEM] + [VMEM] * 3,
+    shifts, gram = call(
+        functools.partial(template_kernel, devices, cap, False),
+        [f32(KSIDE, slabs, rows + 2 * SUB, LANES), f32(size, LANES)],
+        [SMEM, SMEM, SMEM] + [VMEM] * (2 + len(template_in)),
         [
             sums,
-            pltpu.VMEM((len(LAGS), slabs, rows + SUB, LANES), jnp.float32),
+            pltpu.VMEM((len(LAGS) - KSIDE, slabs, rows + 2 * SUB, LANES), jnp.float32),
             pltpu.VMEM((count, SUB, LANES), jnp.float32),
             pltpu.VMEM((count, SUB, LANES), jnp.float32),
         ],
         pixels * 2 * len(PRODUCTS),
         pixels * 8,
-    )(own, table, at_ends, template_in[0], edges, jnp.asarray(coef))
+    )(own, table, at_ends, edges, jnp.asarray(coef), *template_in)
 
     science, fit = call(
         functools.partial(science_kernel, devices, cap, paired),
-        [slab_shape, f32(devices, SUB, LANES)],
+        [f32(NB + 1, BR, BC), f32(devices, SUB, LANES)],
         [SMEM, SMEM, VMEM, VMEM] + [VMEM] * len(science_in),
-        [
-            sums,
-            pltpu.VMEM((KSIDE, slabs, rows, LANES), jnp.float32),
-            pltpu.VMEM((size, LANES), jnp.float32),
-        ],
+        [pltpu.VMEM((size, SUB, LANES), jnp.float32)],
         pixels * 2 * KB,
         pixels * 16,
-    )(own, table, extended, gram, *science_in)
+    )(own, table, shifts, gram, *science_in)
     fit = lax.all_to_all(fit, "ccd", split_axis=0, concat_axis=0, tiled=True)
 
     return call(
-        difference_kernel,
-        f32(rows, columns),
-        [VMEM] * 3,
-        [pltpu.VMEM((KSIDE, slabs, rows, LANES), jnp.float32)],
-        pixels * 2 * KB,
-        pixels * 12,
-    )(fit, extended, science)
+        difference_kernel, f32(rows, columns), [VMEM] * 3, [], pixels * 2 * KB, pixels * 12
+    )(fit, shifts, science)
 
 
 def solution(mesh):

time: 87.1 us -> 84.9 us (0.975)
  Pallas kernels: 25.4 us -> 18.1 us
  waiting for transfers between devices: 14.9 us -> 18.7 us
  local copies, waits for them, and re-layouts: 2.74 us -> 5.02 us
  starting transfers between devices: 29.2 us -> 30.9 us
  blocking collectives: 11.7 us -> 10.2 us
  other arithmetic: 2.51 us -> 1.42 us
    pallas_call x5, Pallas kernels: 25.4 us -> 18.1 us  [the longest x2 8.2 us: warped(): call(functools.partial(warp_kernel, visit, devices, cap, paired), packed,...]
    ppermute x15, waiting for transfers between devices: 14.9 us -> 18.7 us  [exchanged(): lax.ppermute(chunks[k], 'ccd', [(i, i ^ k) for i in range(devices)])]
    unnamed x36 -> x26, local copies, waits for them, and re-layouts: 1.64 us -> 4.42 us
    ppermute x15, starting transfers between devices: 21.7 us -> 23.4 us  [exchanged(): lax.ppermute(chunks[k], 'ccd', [(i, i ^ k) for i in range(devices)])]
    all_to_all x1, blocking collectives: 11.7 us -> 10.2 us  [body(): fit = lax.all_to_all(fit, 'ccd', split_axis=0, concat_axis=0, tiled=True)]
  transfers between devices with their start and end apart: 16 -> 16, of which waited for: 5 -> 3; matrix products, arithmetic and copies ran while one was open for 4% -> 2% of each run, Pallas kernels for 12% -> 10%
where the time goes in v2:
time: 84.9 us; the launch traced here: 84.7 us
  starting transfers between devices  30.9 us (36%)
  waiting for transfers between devices  18.7 us (22%)
  Pallas kernels  18.1 us (21%)
  blocking collectives  10.2 us (12%)
  local copies, waits for them, and re-layouts  5.02 us (6%)
  other arithmetic  1.42 us (2%)
    ppermute x15, starting transfers between devices, exchanged(): lax.ppermute(chunks[k], 'ccd', [(i, i ^ k) for i in range(devices)])  23.4 us
    ppermute x15, waiting for transfers between devices, exchanged(): lax.ppermute(chunks[k], 'ccd', [(i, i ^ k) for i in range(devices)])  18.7 us
    all_to_all x1, blocking collectives, body(): fit = lax.all_to_all(fit, 'ccd', split_axis=0, concat_axis=0, tiled=True)  10.2 us
    pallas_call x2, Pallas kernels, warped(): call(functools.partial(warp_kernel, visit, devices, cap, paired), packed,...  8.2 us
    all_to_all x1, starting transfers between devices, exchanged(): lax.all_to_all(chunks[0], 'ccd', split_axis=0, concat_axis=0, tiled=True)  7.53 us
    pallas_call x1, Pallas kernels, body(): call(functools.partial(template_kernel, devices, cap, False), [f32(KSIDE,...  4.95 us
    unnamed x26, local copies, waits for them, and re-layouts  4.42 us
    pallas_call x1, Pallas kernels, body(): call(difference_kernel, f32(rows, columns), [VMEM] * 3, [], pixels * 2 *...  2.9 us
  transfers between devices with their start and end apart: 16, of which 3 were waited for; matrix products, arithmetic and copies ran while one was open for 2% of the time, Pallas kernels for 10%

profile of v2, /device:TPU:0, one launch (start us, length us, event | category | flops | bytes accessed | tf_op | source)
XLA Modules:
  0.0 84.7 jit_solution(15196981100252210561)
XLA Ops:
  0.0 4.4 %shard_map.64 = f32[16,144,128]{2,1,0:T(8,128)} custom-call(s32[1]{0:T(128)} %bitcast.own_ref, s32[16,32]{1,0:T(8,128)} %bitcast.8, s32[2,1,2]{2,1,0:T(1,128)} %shift_ref.3, f32[2,1,2]{2,1,0:T(1,128)} %frac_ref.3, f32[2,128,1024]{2,1,0:T(8,128)} %x_ref.3), custom_call_target="tpu_custom_call" | custom-call | flops 5242880 | bytes 1572864 | tf_op jit(solution)/shard_map/pallas_call | solution.py:424
  4.4 0.0 copy-start
  4.5 0.0 copy-start.2
  4.5 0.0 copy-start.3
  4.5 0.0 copy-start.4
  4.5 0.0 copy-start.12
  4.5 7.5 %all-to-all-start = ((f32[16,144,128]{2,1,0:T(8,128)}), f32[16,144,128]{2,1,0:T(8,128)S(1)}, u32[]{:S(2)}, u32[]{:S(2)}) async-start(f32[16,144,128]{2,1,0:T(8,128)} %shard_map.64), calls=%async_computation | async-start | bytes 2359296 | tf_op jit(solution)/shard_map/all_to_all | solution.py:446
  12.1 0.0 copy-start.1
  12.1 3.8 %shard_map.66 = (f32[128,128]{1,0:T(8,128)S(1)}, f32[128,128]{1,0:T(8,128)}, f32[128,128]{1,0:T(8,128)}, f32[128,128]{1,0:T(8,128)S(1)}, f32[128,128]{1,0:T(8,12...) custom-call(s32[1]{0:T(128)} %bitcast.own_ref, ...), custom_call_target="tpu_custom_call" | custom-call | flops 5242880 | bytes 1572864 | tf_op jit(solution)/shard_map/pallas_call | solution.py:424
  15.9 0.6 copy-done.5
  16.5 0.6 copy-done.6
  17.1 0.6 copy-done.7
  17.8 0.6 copy-done.8
  18.4 0.6 copy-done.9
  19.0 0.6 copy-done.10
  19.6 0.6 copy-done.11
  20.3 0.4 collective-permute-start
  20.7 1.6 %collective-permute-start.1 = (f32[128,128]{1,0:T(8,128)}, f32[128,128]{1,0:T(8,128)S(1)}, u32[]{:S(2)}, u32[]{:S(2)}) collective-permute-start(f32[128,128]{1,0:T(8,128)} %get-tuple-element.29), channel_id=1, source_target_pairs={{0,2},{1,3},{2,0},{3,1},{4,6},{5,7},{6,4},{7,5},{8,10},{9,11},{10,... | collective-permute-start | bytes 196616 | tf_op jit(solution)/shard_map/ppermute | solution.py:450
  22.3 2.1 %collective-permute-start.10 = (f32[128,128]{1,0:T(8,128)}, f32[128,128]{1,0:T(8,128)S(1)}, u32[]{:S(2)}, u32[]{:S(2)}) collective-permute-start(f32[128,128]{1,0:T(8,128)} %get-tuple-element.38), channel_id=1, source_target_pairs={{0,11},{1,10},{2,9},{3,8},{4,15},{5,14},{6,13},{7,12},{8,3},{9,2},... | collective-permute-start | bytes 196616 | tf_op jit(solution)/shard_map/ppermute | solution.py:450
  24.4 1.5 %collective-permute-start.11 = (f32[128,128]{1,0:T(8,128)}, f32[128,128]{1,0:T(8,128)S(1)}, u32[]{:S(2)}, u32[]{:S(2)}) collective-permute-start(f32[128,128]{1,0:T(8,128)} %get-tuple-element.39), channel_id=1, source_target_pairs={{0,12},{1,13},{2,14},{3,15},{4,8},{5,9},{6,10},{7,11},{8,4},{9,5},... | collective-permute-start | bytes 196616 | tf_op jit(solution)/shard_map/ppermute | solution.py:450
  25.9 2.1 %collective-permute-start.12 = (f32[128,128]{1,0:T(8,128)}, f32[128,128]{1,0:T(8,128)S(1)}, u32[]{:S(2)}, u32[]{:S(2)}) collective-permute-start(f32[128,128]{1,0:T(8,128)} %get-tuple-element.40), channel_id=1, source_target_pairs={{0,13},{1,12},{2,15},{3,14},{4,9},{5,8},{6,11},{7,10},{8,5},{9,4},... | collective-permute-start | bytes 196616 | tf_op jit(solution)/shard_map/ppermute | solution.py:450
  27.9 0.5 convert_reduce_fusion
  28.4 0.3 fusion.4
  28.7 0.3 select_reduce_fusion.1
  29.0 0.1 copy.10
  29.1 0.1 copy.11
  29.2 0.1 broadcast_compare_fusion.5
  29.3 0.1 broadcast_compare_fusion.1
  29.4 0.1 broadcast_and_fusion.1
  29.6 0.1 copy.12
  29.6 0.1 convert_element_type.31
  29.7 0.1 copy.13
  29.8 0.1 copy.9
  29.8 0.1 select_n.76.table_ref
  30.0 0.0 collective-permute-done.refs_1_
  30.0 2.4 %collective-permute-start.13 = (f32[128,128]{1,0:T(8,128)}, f32[128,128]{1,0:T(8,128)S(1)}, u32[]{:S(2)}, u32[]{:S(2)}) collective-permute-start(f32[128,128]{1,0:T(8,128)} %copy-done.11), channel_id=1, source_target_pairs={{0,14},{1,15},{2,12},{3,13},{4,10},{5,11},{6,8},{7,9},{8,6},{9,7},... | collective-permute-start | bytes 196616 | tf_op jit(solution)/shard_map/ppermute | solution.py:450
  32.4 0.0 collective-permute-done.1.refs_2_
  32.4 2.1 %collective-permute-start.14 = (f32[128,128]{1,0:T(8,128)}, f32[128,128]{1,0:T(8,128)S(1)}, u32[]{:S(2)}, u32[]{:S(2)}) collective-permute-start(f32[128,128]{1,0:T(8,128)} %copy-done.10), channel_id=1, source_target_pairs={{0,15},{1,14},{2,13},{3,12},{4,11},{5,10},{6,9},{7,8},{8,7},{9,6},... | collective-permute-start | bytes 196616 | tf_op jit(solution)/shard_map/ppermute | solution.py:450
  34.5 15.7 %collective-permute-done.10.refs_11_ = f32[128,128]{1,0:T(8,128)S(1)} collective-permute-done((f32[128,128]{1,0:T(8,128)}, f32[128,128]{1,0:T(8,128)S(1)}, u32[]{:S(2)}, u32[]{:S(2)}) %collective-permute-start.10) | collective-permute-done | bytes 65568 | tf_op jit(solution)/shard_map/ppermute | solution.py:450
  50.2 1.1 %collective-permute-start.2 = (f32[128,128]{1,0:T(8,128)}, f32[128,128]{1,0:T(8,128)S(1)}, u32[]{:S(2)}, u32[]{:S(2)}) collective-permute-start(f32[128,128]{1,0:T(8,128)} %copy-done.9), channel_id=1, source_target_pairs={{0,3},{1,2},{2,1},{3,0},{4,7},{5,6},{6,5},{7,4},{8,11},{9,10},{10,... | collective-permute-start | bytes 196616 | tf_op jit(solution)/shard_map/ppermute | solution.py:450
  51.3 0.0 collective-permute-done.11.refs_12_
  51.3 1.1 %collective-permute-start.3 = (f32[128,128]{1,0:T(8,128)}, f32[128,128]{1,0:T(8,128)S(1)}, u32[]{:S(2)}, u32[]{:S(2)}) collective-permute-start(f32[128,128]{1,0:T(8,128)} %copy-done.8), channel_id=1, source_target_pairs={{0,4},{1,5},{2,6},{3,7},{4,0},{5,1},{6,2},{7,3},{8,12},{9,13},{10,... | collective-permute-start | bytes 196616 | tf_op jit(solution)/shard_map/ppermute | solution.py:450
  52.4 0.0 collective-permute-done.12.refs_13_
  52.4 1.1 %collective-permute-start.4 = (f32[128,128]{1,0:T(8,128)}, f32[128,128]{1,0:T(8,128)S(1)}, u32[]{:S(2)}, u32[]{:S(2)}) collective-permute-start(f32[128,128]{1,0:T(8,128)} %copy-done.7), channel_id=1, source_target_pairs={{0,5},{1,4},{2,7},{3,6},{4,1},{5,0},{6,3},{7,2},{8,13},{9,12},{10,... | collective-permute-start | bytes 196616 | tf_op jit(solution)/shard_map/ppermute | solution.py:450
  53.5 0.0 collective-permute-done.13.refs_14_
  53.5 2.6 %collective-permute-start.5 = (f32[128,128]{1,0:T(8,128)}, f32[128,128]{1,0:T(8,128)S(1)}, u32[]{:S(2)}, u32[]{:S(2)}) collective-permute-start(f32[128,128]{1,0:T(8,128)} %copy-done.6), channel_id=1, source_target_pairs={{0,6},{1,7},{2,4},{3,5},{4,2},{5,3},{6,0},{7,1},{8,14},{9,15},{10,... | collective-permute-start | bytes 196616 | tf_op jit(solution)/shard_map/ppermute | solution.py:450
  56.1 0.0 collective-permute-done.14.refs_15_
  56.1 0.3 collective-permute-start.6
  56.3 0.0 collective-permute-done.2.refs_3_
  56.3 1.1 %collective-permute-start.7 = (f32[128,128]{1,0:T(8,128)S(1)}, f32[128,128]{1,0:T(8,128)S(1)}, u32[]{:S(2)}, u32[]{:S(2)}) collective-permute-start(f32[128,128]{1,0:T(8,128)S(1)} %get-tuple-element.35), channel_id=1, source_target_pairs={{0,8},{1,9},{2,10},{3,11},{4,12},{5,13},{6,14},{7,15},{8,0},{9,1},... | collective-permute-start | bytes 196616 | tf_op jit(solution)/shard_map/ppermute | solution.py:450
  57.4 0.0 collective-permute-done.3.refs_4_
  57.4 1.5 %collective-permute-start.8 = (f32[128,128]{1,0:T(8,128)S(1)}, f32[128,128]{1,0:T(8,128)S(1)}, u32[]{:S(2)}, u32[]{:S(2)}) collective-permute-start(f32[128,128]{1,0:T(8,128)S(1)} %get-tuple-element.36), channel_id=1, source_target_pairs={{0,9},{1,8},{2,11},{3,10},{4,13},{5,12},{6,15},{7,14},{8,1},{9,0},... | collective-permute-start | bytes 196616 | tf_op jit(solution)/shard_map/ppermute | solution.py:450
  58.9 0.0 collective-permute-done.4.refs_5_
  58.9 2.6 %collective-permute-start.9 = (f32[128,128]{1,0:T(8,128)S(1)}, f32[128,128]{1,0:T(8,128)S(1)}, u32[]{:S(2)}, u32[]{:S(2)}) collective-permute-start(f32[128,128]{1,0:T(8,128)S(1)} %get-tuple-element.37), channel_id=1, source_target_pairs={{0,10},{1,11},{2,8},{3,9},{4,14},{5,15},{6,12},{7,13},{8,2},{9,3},... | collective-permute-start | bytes 196616 | tf_op jit(solution)/shard_map/ppermute | solution.py:450
  61.4 0.1 add_convert_fusion.1.ends_ref
  61.5 0.0 all-to-all-done.refs_0_
  61.5 5.0 %shard_map.65 = (f32[5,8,144,128]{3,2,1,0:T(8,128)S(1)}, f32[32,128]{1,0:T(8,128)S(1)}) custom-call(s32[1]{0:T(128)} %bitcast.own_ref, s32[64]{0:T(128)S(1)} %select_n.76.table_ref, s32[2]{0:T(128)S(1)} %add_convert_fusion.1.ends_ref, f32[2,16,128]{2,1,0:T(8,128)S(1)} %add_convert_fusion.edges_ref, f32[25,80,128]{2,1,0:T(8,128)S(1)} %copy-done.1, ...), custom_call_target="tpu_custom_call" | custom-call | flops 10747904 | bytes 1048576 | tf_op jit(solution)/shard_map/pallas_call | solution.py:487
  66.5 0.0 collective-permute-done.5.refs_6_
  66.5 0.0 collective-permute-done.6.refs_7_
  66.5 0.4 collective-permute-done.8.refs_9_
  66.9 2.6 %collective-permute-done.9.refs_10_ = f32[128,128]{1,0:T(8,128)S(1)} collective-permute-done((f32[128,128]{1,0:T(8,128)S(1)}, f32[128,128]{1,0:T(8,128)S(1)}, u32[]{:S(2)}, u32[]{:S(2)}) %collective-permute-start.9) | collective-permute-done | bytes 65568 | tf_op jit(solution)/shard_map/ppermute | solution.py:450
  69.5 2.1 %shard_map.67 = (f32[33,32,128]{2,1,0:T(8,128)S(1)}, f32[16,8,128]{2,1,0:T(8,128)S(1)}) custom-call(s32[1]{0:T(128)} %bitcast.own_ref, s32[64]{0:T(128)S(1)} %select_n.76.table_ref, f32[5,8,144,128]{3,2,1,0:T(8,128)S(1)} %get-tuple-element.25.cols_ref, f32[32,128]{1,0:T(8,128)S(1)} %get-tuple-element.26.gram_ref, f32[128,128]{1,0:T(8,128)S(1)} %get-tuple-element.27.refs_0_, ...), custom_call_target="tpu_custom_call" | custom-call | flops 6553600 | bytes 2097152 | tf_op jit(solution)/shard_map/pallas_call | solution.py:501
  71.6 10.2 %all_to_all.10.fit_ref = f32[16,8,128]{2,1,0:T(8,128)S(1)} all-to-all(f32[16,8,128]{2,1,0:T(8,128)S(1)} %get-tuple-element.43), channel_id=1, replica_groups=mesh['field'=2,'ccd'=16] {'ccd'}, dimensions={0} | all-to-all | bytes 131072 | tf_op jit(solution)/shard_map/all_to_all | solution.py:509
  81.8 2.9 %shard_map.68 = f32[128,1024]{1,0:T(8,128)} custom-call(f32[16,8,128]{2,1,0:T(8,128)S(1)} %all_to_all.10.fit_ref, f32[5,8,144,128]{3,2,1,0:T(8,128)S(1)} %get-tuple-element.25.cols_ref, f32[33,32,128]{2,1,0:T(8,128)S(1)} %get-tuple-element.44.sci_ref), custom_call_target="tpu_custom_call" | custom-call | flops 6553600 | bytes 1572864 | tf_op jit(solution)/shard_map/pallas_call | solution.py:511
  (23 shorter events, 0.1 us)
Async XLA Ops:
  4.4 7.6 %copy-start = (f32[2,128,1024]{2,1,0:T(8,128)S(1)}, f32[2,128,1024]{2,1,0:T(8,128)}, u32[]{:S(2)}) copy-start(f32[2,128,1024]{2,1,0:T(8,128)} %x_ref.3) | copy-start | bytes 3145732
  4.5 7.6 %copy-start.2 = (s32[16,32,1]{1,2,0:T(1,128)S(1)}, s32[16,32,1]{1,2,0:T(1,128)}, u32[]{:S(2)}) copy-start(s32[16,32,1]{1,2,0:T(1,128)} %param.9) | copy-start | bytes 6148
  4.5 7.6 %copy-start.3 = (s32[2,1,2]{2,1,0:T(1,128)S(1)}, s32[2,1,2]{2,1,0:T(1,128)}, u32[]{:S(2)}) copy-start(s32[2,1,2]{2,1,0:T(1,128)} %shift_ref.3) | copy-start | bytes 52
  4.5 7.6 %copy-start.4 = (f32[2,1,2]{2,1,0:T(1,128)S(1)}, f32[2,1,2]{2,1,0:T(1,128)}, u32[]{:S(2)}) copy-start(f32[2,1,2]{2,1,0:T(1,128)} %frac_ref.3) | copy-start | bytes 52
  4.5 24.2 %copy-start.12 = (s32[16,32]{1,0:T(8,128)S(1)}, s32[16,32]{1,0:T(8,128)}, u32[]{:S(2)}) copy-start(s32[16,32]{1,0:T(8,128)} %param.10) | copy-start | bytes 6148
  4.5 57.0 %all-to-all-start = ((f32[16,144,128]{2,1,0:T(8,128)}), f32[16,144,128]{2,1,0:T(8,128)S(1)}, u32[]{:S(2)}, u32[]{:S(2)}) async-start(f32[16,144,128]{2,1,0:T(8,128)} %shard_map.64), calls=%async_computation | async-start | bytes 2359296 | tf_op jit(solution)/shard_map/all_to_all | solution.py:446
  12.1 49.4 %copy-start.1 = (f32[25,80,128]{2,1,0:T(8,128)S(1)}, f32[25,80,128]{2,1,0:T(8,128)}, u32[]{:S(2)}) copy-start(f32[25,80,128]{2,1,0:T(8,128)} %constant.68.clone.coef_ref) | copy-start | bytes 3072004
  15.9 0.6 copy-start.5
  16.5 0.6 copy-start.6
  17.1 0.6 copy-start.7
  17.7 0.6 copy-start.8
  18.4 0.6 copy-start.9
  19.0 0.6 copy-start.10
  19.6 0.6 copy-start.11
  20.3 9.7 %collective-permute-start = (f32[128,128]{1,0:T(8,128)}, f32[128,128]{1,0:T(8,128)S(1)}, u32[]{:S(2)}, u32[]{:S(2)}) collective-permute-start(f32[128,128]{1,0:T(8,128)} %get-tuple-element.28), channel_id=1, source_target_pairs={{0,1},{1,0},{2,3},{3,2},{4,5},{5,4},{6,7},{7,6},{8,9},{9,8},{10,11... | collective-permute-start | bytes 196616 | tf_op jit(solution)/shard_map/ppermute | solution.py:450
  20.7 11.7 %collective-permute-start.1 = (f32[128,128]{1,0:T(8,128)}, f32[128,128]{1,0:T(8,128)S(1)}, u32[]{:S(2)}, u32[]{:S(2)}) collective-permute-start(f32[128,128]{1,0:T(8,128)} %get-tuple-element.29), channel_id=1, source_target_pairs={{0,2},{1,3},{2,0},{3,1},{4,6},{5,7},{6,4},{7,5},{8,10},{9,11},{10,... | collective-permute-start | bytes 196616 | tf_op jit(solution)/shard_map/ppermute | solution.py:450
  22.3 27.9 %collective-permute-start.10 = (f32[128,128]{1,0:T(8,128)}, f32[128,128]{1,0:T(8,128)S(1)}, u32[]{:S(2)}, u32[]{:S(2)}) collective-permute-start(f32[128,128]{1,0:T(8,128)} %get-tuple-element.38), channel_id=1, source_target_pairs={{0,11},{1,10},{2,9},{3,8},{4,15},{5,14},{6,13},{7,12},{8,3},{9,2},... | collective-permute-start | bytes 196616 | tf_op jit(solution)/shard_map/ppermute | solution.py:450
  24.4 26.9 %collective-permute-start.11 = (f32[128,128]{1,0:T(8,128)}, f32[128,128]{1,0:T(8,128)S(1)}, u32[]{:S(2)}, u32[]{:S(2)}) collective-permute-start(f32[128,128]{1,0:T(8,128)} %get-tuple-element.39), channel_id=1, source_target_pairs={{0,12},{1,13},{2,14},{3,15},{4,8},{5,9},{6,10},{7,11},{8,4},{9,5},... | collective-permute-start | bytes 196616 | tf_op jit(solution)/shard_map/ppermute | solution.py:450
  25.9 26.5 %collective-permute-start.12 = (f32[128,128]{1,0:T(8,128)}, f32[128,128]{1,0:T(8,128)S(1)}, u32[]{:S(2)}, u32[]{:S(2)}) collective-permute-start(f32[128,128]{1,0:T(8,128)} %get-tuple-element.40), channel_id=1, source_target_pairs={{0,13},{1,12},{2,15},{3,14},{4,9},{5,8},{6,11},{7,10},{8,5},{9,4},... | collective-permute-start | bytes 196616 | tf_op jit(solution)/shard_map/ppermute | solution.py:450
  30.0 23.5 %collective-permute-start.13 = (f32[128,128]{1,0:T(8,128)}, f32[128,128]{1,0:T(8,128)S(1)}, u32[]{:S(2)}, u32[]{:S(2)}) collective-permute-start(f32[128,128]{1,0:T(8,128)} %copy-done.11), channel_id=1, source_target_pairs={{0,14},{1,15},{2,12},{3,13},{4,10},{5,11},{6,8},{7,9},{8,6},{9,7},... | collective-permute-start | bytes 196616 | tf_op jit(solution)/shard_map/ppermute | solution.py:450
  32.4 23.7 %collective-permute-start.14 = (f32[128,128]{1,0:T(8,128)}, f32[128,128]{1,0:T(8,128)S(1)}, u32[]{:S(2)}, u32[]{:S(2)}) collective-permute-start(f32[128,128]{1,0:T(8,128)} %copy-done.10), channel_id=1, source_target_pairs={{0,15},{1,14},{2,13},{3,12},{4,11},{5,10},{6,9},{7,8},{8,7},{9,6},... | collective-permute-start | bytes 196616 | tf_op jit(solution)/shard_map/ppermute | solution.py:450
  50.2 6.1 %collective-permute-start.2 = (f32[128,128]{1,0:T(8,128)}, f32[128,128]{1,0:T(8,128)S(1)}, u32[]{:S(2)}, u32[]{:S(2)}) collective-permute-start(f32[128,128]{1,0:T(8,128)} %copy-done.9), channel_id=1, source_target_pairs={{0,3},{1,2},{2,1},{3,0},{4,7},{5,6},{6,5},{7,4},{8,11},{9,10},{10,... | collective-permute-start | bytes 196616 | tf_op jit(solution)/shard_map/ppermute | solution.py:450
  51.3 6.1 %collective-permute-start.3 = (f32[128,128]{1,0:T(8,128)}, f32[128,128]{1,0:T(8,128)S(1)}, u32[]{:S(2)}, u32[]{:S(2)}) collective-permute-start(f32[128,128]{1,0:T(8,128)} %copy-done.8), channel_id=1, source_target_pairs={{0,4},{1,5},{2,6},{3,7},{4,0},{5,1},{6,2},{7,3},{8,12},{9,13},{10,... | collective-permute-start | bytes 196616 | tf_op jit(solution)/shard_map/ppermute | solution.py:450
  52.4 6.5 %collective-permute-start.4 = (f32[128,128]{1,0:T(8,128)}, f32[128,128]{1,0:T(8,128)S(1)}, u32[]{:S(2)}, u32[]{:S(2)}) collective-permute-start(f32[128,128]{1,0:T(8,128)} %copy-done.7), channel_id=1, source_target_pairs={{0,5},{1,4},{2,7},{3,6},{4,1},{5,0},{6,3},{7,2},{8,13},{9,12},{10,... | collective-permute-start | bytes 196616 | tf_op jit(solution)/shard_map/ppermute | solution.py:450
  53.5 13.0 %collective-permute-start.5 = (f32[128,128]{1,0:T(8,128)}, f32[128,128]{1,0:T(8,128)S(1)}, u32[]{:S(2)}, u32[]{:S(2)}) collective-permute-start(f32[128,128]{1,0:T(8,128)} %copy-done.6), channel_id=1, source_target_pairs={{0,6},{1,7},{2,4},{3,5},{4,2},{5,3},{6,0},{7,1},{8,14},{9,15},{10,... | collective-permute-start | bytes 196616 | tf_op jit(solution)/shard_map/ppermute | solution.py:450
  56.1 10.4 %collective-permute-start.6 = (f32[128,128]{1,0:T(8,128)}, f32[128,128]{1,0:T(8,128)S(1)}, u32[]{:S(2)}, u32[]{:S(2)}) collective-permute-start(f32[128,128]{1,0:T(8,128)} %copy-done.5), channel_id=1, source_target_pairs={{0,7},{1,6},{2,5},{3,4},{4,3},{5,2},{6,1},{7,0},{8,15},{9,14},{10,... | collective-permute-start | bytes 196616 | tf_op jit(solution)/shard_map/ppermute | solution.py:450
  56.3 10.2 %collective-permute-start.7 = (f32[128,128]{1,0:T(8,128)S(1)}, f32[128,128]{1,0:T(8,128)S(1)}, u32[]{:S(2)}, u32[]{:S(2)}) collective-permute-start(f32[128,128]{1,0:T(8,128)S(1)} %get-tuple-element.35), channel_id=1, source_target_pairs={{0,8},{1,9},{2,10},{3,11},{4,12},{5,13},{6,14},{7,15},{8,0},{9,1},... | collective-permute-start | bytes 196616 | tf_op jit(solution)/shard_map/ppermute | solution.py:450
  57.4 9.5 %collective-permute-start.8 = (f32[128,128]{1,0:T(8,128)S(1)}, f32[128,128]{1,0:T(8,128)S(1)}, u32[]{:S(2)}, u32[]{:S(2)}) collective-permute-start(f32[128,128]{1,0:T(8,128)S(1)} %get-tuple-element.36), channel_id=1, source_target_pairs={{0,9},{1,8},{2,11},{3,10},{4,13},{5,12},{6,15},{7,14},{8,1},{9,0},... | collective-permute-start | bytes 196616 | tf_op jit(solution)/shard_map/ppermute | solution.py:450
  58.9 10.6 %collective-permute-start.9 = (f32[128,128]{1,0:T(8,128)S(1)}, f32[128,128]{1,0:T(8,128)S(1)}, u32[]{:S(2)}, u32[]{:S(2)}) collective-permute-start(f32[128,128]{1,0:T(8,128)S(1)} %get-tuple-element.37), channel_id=1, source_target_pairs={{0,10},{1,11},{2,8},{3,9},{4,14},{5,15},{6,12},{7,13},{8,2},{9,3},... | collective-permute-start | bytes 196616 | tf_op jit(solution)/shard_map/ppermute | solution.py:450

commit v3 on v2

--- a/solution.py
+++ b/solution.py
@@ -31,6 +31,7 @@
 UNROLL = 4
 STEP = 4
 GROUP = 5
+LATE = 2
 RHS_LANE = KB
 
 
@@ -197,8 +198,8 @@
             acc[slot] = acc[slot] + chunk[r * BR : (r + 1) * BR, :]
 
     if paired:
-        for k in range(devices):
-            add(ins[k], jnp.bitwise_xor(own, k))
+        for k, chunk in enumerate(ins):
+            add(chunk, jnp.bitwise_xor(own, k))
     else:
 
         @pl.loop(0, devices)
@@ -303,11 +304,21 @@
     gram_ref[...] = total + jnp.where(row == column, 0.0, flipped)
 
 
-def science_kernel(devices, cap, paired, own_ref, table_ref, cols_ref, gram_ref, *refs):
-    ins, (out, fit_ref, sums_ref) = refs[:-3], refs[-3:]
+def joined_fit(gram, sums):
+    rhs = jnp.sum(jnp.sum(sums, axis=1), axis=1, keepdims=True)
+    size = gram.shape[0]
+    column = lax.broadcasted_iota(jnp.int32, (size, LANES), 1)
+    joined = jnp.where(column == RHS_LANE, rhs, gram)
+    packed = joined[0:SUB]
+    for a in range(1, size // SUB):
+        packed = packed + pltpu.roll(joined[a * SUB : (a + 1) * SUB], a * size, 1)
+    return packed
+
+
+def science_kernel(devices, cap, paired, own_ref, table_ref, cols_ref, *refs):
+    ins, (out, sums_ref) = refs[:-2], refs[-2:]
     slabs, rows = cols_ref.shape[1], cols_ref.shape[2] - 2 * SUB
     sum_blocks(devices, cap, paired, own_ref[0], table_ref, ins, out)
-
     sums_ref[...] = jnp.zeros_like(sums_ref)
 
     @pl.loop(0, slabs)
@@ -325,14 +336,39 @@
         for i in range(KB):
             sums_ref[i] = sums_ref[i] + sums[i]
 
-    rhs = jnp.sum(jnp.sum(sums_ref[...], axis=1), axis=1, keepdims=True)
-    size = gram_ref.shape[0]
-    column = lax.broadcasted_iota(jnp.int32, (size, LANES), 1)
-    joined = jnp.where(column == RHS_LANE, rhs, gram_ref[...])
-    packed = joined[0:SUB]
-    for a in range(1, size // SUB):
-        packed = packed + pltpu.roll(joined[a * SUB : (a + 1) * SUB], a * size, 1)
-    for k in range(devices):
+
+def late_kernel(
+    first, cap, own_ref, table_ref, cols_ref, gram_ref, early_ref, sums_ref, *refs
+):
+    ins, (out, fit_ref, all_sums) = refs[:-3], refs[-3:]
+    slabs = cols_ref.shape[1]
+    out[...] = early_ref[...]
+    sums = [sums_ref[i] for i in range(KB)]
+    for n, chunk in enumerate(ins):
+        for r in range(cap):
+            slot = table_ref[jnp.bitwise_xor(own_ref[0], first + n) * cap + r]
+            out[slot] = out[slot] + chunk[r * BR : (r + 1) * BR, :]
+            share = (slot < NB).astype(jnp.float32)
+            inside = jnp.minimum(slot, NB - 1)
+            j, band = lax.rem(inside, slabs), lax.div(inside, slabs)
+            for t in range(BR // SUB):
+                at = r * BR + t * SUB
+                target = chunk[at : at + SUB, :] * share
+                base = band * BR + SUB + t * SUB - REACH
+                for i in range(KB):
+                    part = cols_ref[i % KSIDE, j, pl.ds(base + i // KSIDE, SUB), :]
+                    sums[i] = sums[i] + part * target
+    all_sums[...] = jnp.zeros_like(all_sums)
+    for i in range(KB):
+        all_sums[i] = sums[i]
+    packed = joined_fit(gram_ref[...], all_sums[...])
+    for k in range(fit_ref.shape[0]):
+        fit_ref[k] = packed
+
+
+def fit_kernel(gram_ref, sums_ref, fit_ref):
+    packed = joined_fit(gram_ref[...], sums_ref[...])
+    for k in range(fit_ref.shape[0]):
         fit_ref[k] = packed
 
 
@@ -364,13 +400,17 @@
     return work[:, RHS_LANE : RHS_LANE + 1]
 
 
-def difference_kernel(fit_ref, cols_ref, sci_ref, out_ref):
+def difference_kernel(fit_ref, cols_ref, sci_ref, out_ref, whole, sems):
     slabs, rows = cols_ref.shape[1], cols_ref.shape[2] - 2 * SUB
     shared = fit_ref[0]
     for k in range(1, fit_ref.shape[0]):
         shared = shared + fit_ref[k]
     kernel = solved(shared, NB)
     taps = [jnp.broadcast_to(kernel[i : i + 1, :], (SUB, LANES)) for i in range(KB)]
+
+    def store(band):
+        at = pl.ds(pl.multiple_of(band * BR, BR), BR)
+        return pltpu.make_async_copy(whole.at[at, :], out_ref.at[at, :], sems.at[band])
 
     @pl.loop(0, rows // BR)
     def _(band):
@@ -384,7 +424,11 @@
                         total = term if total is None else total + term
                 science = sci_ref[band * slabs + j, t * SUB : (t + 1) * SUB, :]
                 at = pl.ds(pl.multiple_of(band * BR + t * SUB, SUB), SUB)
-                out_ref[at, j * LANES : (j + 1) * LANES] = science - total
+                whole[at, j * LANES : (j + 1) * LANES] = science - total
+        store(band).start()
+
+    for band in range(rows // BR):
+        store(band).wait()
 
 
 def by_permutes(devices):
@@ -498,18 +542,36 @@
         pixels * 8,
     )(own, table, at_ends, edges, jnp.asarray(coef), *template_in)
 
-    science, fit = call(
+    first = devices - LATE if paired else len(science_in)
+    science, sums = call(
         functools.partial(science_kernel, devices, cap, paired),
-        [f32(NB + 1, BR, BC), f32(devices, SUB, LANES)],
-        [SMEM, SMEM, VMEM, VMEM] + [VMEM] * len(science_in),
-        [pltpu.VMEM((size, SUB, LANES), jnp.float32)],
+        [f32(NB + 1, BR, BC), f32(size, SUB, LANES)],
+        [SMEM, SMEM, VMEM] + [VMEM] * first,
+        [],
         pixels * 2 * KB,
         pixels * 16,
-    )(own, table, shifts, gram, *science_in)
+    )(own, table, shifts, *science_in[:first])
+    if paired:
+        science, fit = call(
+            functools.partial(late_kernel, first, cap),
+            [f32(NB + 1, BR, BC), f32(devices, SUB, LANES)],
+            [SMEM, SMEM] + [VMEM] * (4 + LATE),
+            [pltpu.VMEM((size, SUB, LANES), jnp.float32)],
+            pixels * KB // 2,
+            pixels * 8,
+        )(own, table, shifts, gram, science, sums, *science_in[first:])
+    else:
+        fit = call(fit_kernel, f32(devices, SUB, LANES), [VMEM] * 2, [], 10**5, 10**5)(gram, sums)
     fit = lax.all_to_all(fit, "ccd", split_axis=0, concat_axis=0, tiled=True)
 
     return call(
-        difference_kernel, f32(rows, columns), [VMEM] * 3, [], pixels * 2 * KB, pixels * 12
+        difference_kernel,
+        f32(rows, columns),
+        [VMEM] * 3,
+        [pltpu.VMEM((rows, columns), jnp.float32), pltpu.SemaphoreType.DMA((rows // BR,))],
+        pixels * 2 * KB,
+        pixels * 12,
+        out=pl.BlockSpec(memory_space=pltpu.HBM),
     )(fit, shifts, science)
 
 

time: 84.9 us -> 78.4 us (0.923)
  waiting for transfers between devices: 18.7 us -> 12.9 us
  starting transfers between devices: 30.9 us -> 28.5 us
  blocking collectives: 10.2 us -> 11.4 us
    ppermute x15, waiting for transfers between devices: 18.7 us -> 12.9 us  [exchanged(): lax.ppermute(chunks[k], 'ccd', [(i, i ^ k) for i in range(devices)])]
    ppermute x15, starting transfers between devices: 23.4 us -> 20.9 us  [exchanged(): lax.ppermute(chunks[k], 'ccd', [(i, i ^ k) for i in range(devices)])]
    all_to_all x1, blocking collectives: 10.2 us -> 11.4 us  [body(): fit = lax.all_to_all(fit, 'ccd', split_axis=0, concat_axis=0, tiled=True)]
    pallas_call x1 -> x2, Pallas kernels: 2.9 us -> 3.72 us  [the longest x1 2.79 us: body(): call(difference_kernel, f32(rows, columns), [VMEM] * 3, [pltpu.VMEM((rows...]
  transfers between devices with their start and end apart: 16 -> 16, of which waited for: 3 -> 5; matrix products, arithmetic and copies ran while one was open for 2% -> 3% of each run, Pallas kernels for 10% -> 14%
where the time goes in v3:
time: 78.4 us; the launch traced here: 78.1 us
  starting transfers between devices  28.5 us (36%)
  Pallas kernels  18.7 us (24%)
  waiting for transfers between devices  12.9 us (16%)
  blocking collectives  11.4 us (15%)
  local copies, waits for them, and re-layouts  4.92 us (6%)
  other arithmetic  1.42 us (2%)
    ppermute x15, starting transfers between devices, exchanged(): lax.ppermute(chunks[k], 'ccd', [(i, i ^ k) for i in range(devices)])  20.9 us
    ppermute x15, waiting for transfers between devices, exchanged(): lax.ppermute(chunks[k], 'ccd', [(i, i ^ k) for i in range(devices)])  12.9 us
    all_to_all x1, blocking collectives, body(): fit = lax.all_to_all(fit, 'ccd', split_axis=0, concat_axis=0, tiled=True)  11.4 us
    pallas_call x2, Pallas kernels, warped(): call(functools.partial(warp_kernel, visit, devices, cap, paired), packed,...  8.16 us
    all_to_all x1, starting transfers between devices, exchanged(): lax.all_to_all(chunks[0], 'ccd', split_axis=0, concat_axis=0, tiled=True)  7.53 us
    pallas_call x1, Pallas kernels, body(): call(functools.partial(template_kernel, devices, cap, False), [f32(KSIDE,...  4.95 us
    unnamed x26, local copies, waits for them, and re-layouts  4.35 us
    pallas_call x1, Pallas kernels, body(): call(difference_kernel, f32(rows, columns), [VMEM] * 3, [pltpu.VMEM((rows...  2.79 us
  transfers between devices with their start and end apart: 16, of which 5 were waited for; matrix products, arithmetic and copies ran while one was open for 3% of the time, Pallas kernels for 14%

profile of v3, /device:TPU:0, one launch (start us, length us, event | category | flops | bytes accessed | tf_op | source)
XLA Modules:
  0.0 78.1 jit_solution(8015597217561817099)
XLA Ops:
  0.0 4.4 %shard_map.64 = f32[16,144,128]{2,1,0:T(8,128)} custom-call(s32[1]{0:T(128)} %bitcast.own_ref, s32[16,32]{1,0:T(8,128)} %bitcast.8, s32[2,1,2]{2,1,0:T(1,128)} %shift_ref.3, f32[2,1,2]{2,1,0:T(1,128)} %frac_ref.3, f32[2,128,1024]{2,1,0:T(8,128)} %x_ref.3), custom_call_target="tpu_custom_call" | custom-call | flops 5242880 | bytes 1572864 | tf_op jit(solution)/shard_map/pallas_call | solution.py:468
  4.4 0.0 copy-start
  4.4 0.0 copy-start.2
  4.4 0.0 copy-start.3
  4.5 0.0 copy-start.4
  4.5 0.0 copy-start.12
  4.5 7.5 %all-to-all-start = ((f32[16,144,128]{2,1,0:T(8,128)}), f32[16,144,128]{2,1,0:T(8,128)S(1)}, u32[]{:S(2)}, u32[]{:S(2)}) async-start(f32[16,144,128]{2,1,0:T(8,128)} %shard_map.64), calls=%async_computation | async-start | bytes 2359296 | tf_op jit(solution)/shard_map/all_to_all | solution.py:490
  12.1 0.0 copy-start.1
  12.1 3.8 %shard_map.66 = (f32[128,128]{1,0:T(8,128)S(1)}, f32[128,128]{1,0:T(8,128)}, f32[128,128]{1,0:T(8,128)}, f32[128,128]{1,0:T(8,128)}, f32[128,128]{1,0:T(8,128)},...) custom-call(s32[1]{0:T(128)} %bitcast.own_ref, ...), custom_call_target="tpu_custom_call" | custom-call | flops 5242880 | bytes 1572864 | tf_op jit(solution)/shard_map/pallas_call | solution.py:468
  15.8 0.6 copy-done.5
  16.5 0.6 copy-done.6
  17.1 0.6 copy-done.7
  17.7 0.6 copy-done.8
  18.3 0.6 copy-done.9
  18.9 0.6 copy-done.10
  19.5 0.6 copy-done.11
  20.2 0.4 collective-permute-start
  20.6 1.6 %collective-permute-start.1 = (f32[128,128]{1,0:T(8,128)}, f32[128,128]{1,0:T(8,128)S(1)}, u32[]{:S(2)}, u32[]{:S(2)}) collective-permute-start(f32[128,128]{1,0:T(8,128)} %get-tuple-element.31), channel_id=1, source_target_pairs={{0,2},{1,3},{2,0},{3,1},{4,6},{5,7},{6,4},{7,5},{8,10},{9,11},{10,... | collective-permute-start | bytes 196616 | tf_op jit(solution)/shard_map/ppermute | solution.py:494
  22.2 0.0 collective-permute-start.2
  22.2 1.7 %collective-permute-start.3 = (f32[128,128]{1,0:T(8,128)}, f32[128,128]{1,0:T(8,128)S(1)}, u32[]{:S(2)}, u32[]{:S(2)}) collective-permute-start(f32[128,128]{1,0:T(8,128)} %get-tuple-element.33), channel_id=1, source_target_pairs={{0,4},{1,5},{2,6},{3,7},{4,0},{5,1},{6,2},{7,3},{8,12},{9,13},{10,... | collective-permute-start | bytes 196616 | tf_op jit(solution)/shard_map/ppermute | solution.py:494
  23.9 0.1 collective-permute-start.4
  24.1 0.5 convert_reduce_fusion
  24.5 0.3 fusion.4
  24.8 0.3 select_reduce_fusion.1
  25.1 0.1 copy.10
  25.2 0.1 copy.11
  25.3 0.1 broadcast_compare_fusion.5
  25.4 0.1 broadcast_compare_fusion.1
  25.5 0.1 broadcast_and_fusion.1
  25.6 0.1 copy.9
  25.7 0.1 select_n.76.table_ref
  25.9 0.1 copy.13
  25.9 0.1 convert_element_type.30
  26.0 0.1 copy.12
  26.1 0.0 collective-permute-done.refs_1_
  26.1 2.6 %collective-permute-start.5 = (f32[128,128]{1,0:T(8,128)}, f32[128,128]{1,0:T(8,128)S(1)}, u32[]{:S(2)}, u32[]{:S(2)}) collective-permute-start(f32[128,128]{1,0:T(8,128)} %copy-done.11), channel_id=1, source_target_pairs={{0,6},{1,7},{2,4},{3,5},{4,2},{5,3},{6,0},{7,1},{8,14},{9,15},{10,... | collective-permute-start | bytes 196616 | tf_op jit(solution)/shard_map/ppermute | solution.py:494
  28.7 0.0 collective-permute-done.1.refs_2_
  28.7 0.1 collective-permute-start.6
  28.7 1.1 %collective-permute-done.2.refs_3_ = f32[128,128]{1,0:T(8,128)S(1)} collective-permute-done((f32[128,128]{1,0:T(8,128)}, f32[128,128]{1,0:T(8,128)S(1)}, u32[]{:S(2)}, u32[]{:S(2)}) %collective-permute-start.2) | collective-permute-done | bytes 65568 | tf_op jit(solution)/shard_map/ppermute | solution.py:494
  29.9 1.4 %collective-permute-start.7 = (f32[128,128]{1,0:T(8,128)}, f32[128,128]{1,0:T(8,128)S(1)}, u32[]{:S(2)}, u32[]{:S(2)}) collective-permute-start(f32[128,128]{1,0:T(8,128)} %copy-done.9), channel_id=1, source_target_pairs={{0,8},{1,9},{2,10},{3,11},{4,12},{5,13},{6,14},{7,15},{8,0},{9,1},... | collective-permute-start | bytes 196616 | tf_op jit(solution)/shard_map/ppermute | solution.py:494
  31.3 2.6 %collective-permute-done.3.refs_4_ = f32[128,128]{1,0:T(8,128)S(1)} collective-permute-done((f32[128,128]{1,0:T(8,128)}, f32[128,128]{1,0:T(8,128)S(1)}, u32[]{:S(2)}, u32[]{:S(2)}) %collective-permute-start.3) | collective-permute-done | bytes 65568 | tf_op jit(solution)/shard_map/ppermute | solution.py:494
  33.9 3.2 %collective-permute-start.8 = (f32[128,128]{1,0:T(8,128)}, f32[128,128]{1,0:T(8,128)S(1)}, u32[]{:S(2)}, u32[]{:S(2)}) collective-permute-start(f32[128,128]{1,0:T(8,128)} %copy-done.8), channel_id=1, source_target_pairs={{0,9},{1,8},{2,11},{3,10},{4,13},{5,12},{6,15},{7,14},{8,1},{9,0},... | collective-permute-start | bytes 196616 | tf_op jit(solution)/shard_map/ppermute | solution.py:494
  37.1 0.0 collective-permute-done.4.refs_5_
  37.1 2.6 %collective-permute-start.9 = (f32[128,128]{1,0:T(8,128)}, f32[128,128]{1,0:T(8,128)S(1)}, u32[]{:S(2)}, u32[]{:S(2)}) collective-permute-start(f32[128,128]{1,0:T(8,128)} %copy-done.7), channel_id=1, source_target_pairs={{0,10},{1,11},{2,8},{3,9},{4,14},{5,15},{6,12},{7,13},{8,2},{9,3},... | collective-permute-start | bytes 196616 | tf_op jit(solution)/shard_map/ppermute | solution.py:494
  39.8 0.0 collective-permute-done.5.refs_6_
  39.8 2.1 %collective-permute-start.10 = (f32[128,128]{1,0:T(8,128)}, f32[128,128]{1,0:T(8,128)S(1)}, u32[]{:S(2)}, u32[]{:S(2)}) collective-permute-start(f32[128,128]{1,0:T(8,128)} %copy-done.6), channel_id=1, source_target_pairs={{0,11},{1,10},{2,9},{3,8},{4,15},{5,14},{6,13},{7,12},{8,3},{9,2},... | collective-permute-start | bytes 196616 | tf_op jit(solution)/shard_map/ppermute | solution.py:494
  41.9 0.0 collective-permute-done.6.refs_7_
  41.9 0.1 collective-permute-start.11
  42.0 8.4 %collective-permute-done.7.refs_8_ = f32[128,128]{1,0:T(8,128)S(1)} collective-permute-done((f32[128,128]{1,0:T(8,128)}, f32[128,128]{1,0:T(8,128)S(1)}, u32[]{:S(2)}, u32[]{:S(2)}) %collective-permute-start.7) | collective-permute-done | bytes 65568 | tf_op jit(solution)/shard_map/ppermute | solution.py:494
  50.4 0.0 collective-permute-start.12
  50.4 0.3 collective-permute-done.8.refs_9_
  50.7 3.0 %collective-permute-start.13 = (f32[128,128]{1,0:T(8,128)S(1)}, f32[128,128]{1,0:T(8,128)S(1)}, u32[]{:S(2)}, u32[]{:S(2)}) collective-permute-start(f32[128,128]{1,0:T(8,128)S(1)} %get-tuple-element.45), channel_id=1, source_target_pairs={{0,14},{1,15},{2,12},{3,13},{4,10},{5,11},{6,8},{7,9},{8,6},{9,7},... | collective-permute-start | bytes 196616 | tf_op jit(solution)/shard_map/ppermute | solution.py:494
  53.7 0.4 collective-permute-done.9.refs_10_
  54.1 1.9 %collective-permute-start.14 = (f32[128,128]{1,0:T(8,128)S(1)}, f32[128,128]{1,0:T(8,128)S(1)}, u32[]{:S(2)}, u32[]{:S(2)}) collective-permute-start(f32[128,128]{1,0:T(8,128)S(1)} %get-tuple-element.46), channel_id=1, source_target_pairs={{0,15},{1,14},{2,13},{3,12},{4,11},{5,10},{6,9},{7,8},{8,7},{9,6},... | collective-permute-start | bytes 196616 | tf_op jit(solution)/shard_map/ppermute | solution.py:494
  56.0 0.1 add_convert_fusion.1.ends_ref
  56.1 0.0 all-to-all-done.refs_0_
  56.1 5.0 %shard_map.65 = (f32[5,8,144,128]{3,2,1,0:T(8,128)S(1)}, f32[32,128]{1,0:T(8,128)S(1)}) custom-call(s32[1]{0:T(128)} %bitcast.own_ref, s32[64]{0:T(128)S(1)} %select_n.76.table_ref, s32[2]{0:T(128)S(1)} %add_convert_fusion.1.ends_ref, f32[2,16,128]{2,1,0:T(8,128)S(1)} %add_convert_fusion.edges_ref, f32[25,80,128]{2,1,0:T(8,128)S(1)} %copy-done.1, ...), custom_call_target="tpu_custom_call" | custom-call | flops 10747904 | bytes 1048576 | tf_op jit(solution)/shard_map/pallas_call | solution.py:531
  61.0 0.0 collective-permute-done.11.refs_12_
  61.1 0.0 collective-permute-done.12.refs_13_
  61.1 1.9 %shard_map.67 = (f32[33,32,128]{2,1,0:T(8,128)S(1)}, f32[32,8,128]{2,1,0:T(8,128)S(1)}) custom-call(s32[1]{0:T(128)} %bitcast.own_ref, s32[64]{0:T(128)S(1)} %select_n.76.table_ref, f32[5,8,144,128]{3,2,1,0:T(8,128)S(1)} %get-tuple-element.27.cols_ref, f32[128,128]{1,0:T(8,128)S(1)} %get-tuple-element.29.refs_0_, ...), custom_call_target="tpu_custom_call" | custom-call | flops 6553600 | bytes 2097152 | tf_op jit(solution)/shard_map/pallas_call | solution.py:546
  63.0 0.0 collective-permute-done.13.refs_0_
  63.0 0.9 %shard_map.68 = (f32[33,32,128]{2,1,0:T(8,128)S(1)}, f32[16,8,128]{2,1,0:T(8,128)S(1)}) custom-call(s32[1]{0:T(128)} %bitcast.own_ref, s32[64]{0:T(128)S(1)} %select_n.76.table_ref, f32[5,8,144,128]{3,2,1,0:T(8,128)S(1)} %get-tuple-element.27.cols_ref, f32[32,128]{1,0:T(8,128)S(1)} %get-tuple-element.28.gram_ref, ...), custom_call_target="tpu_custom_call" | custom-call | flops 1638400 | bytes 1048576 | tf_op jit(solution)/shard_map/pallas_call | solution.py:555
  63.9 11.4 %all_to_all.10.fit_ref = f32[16,8,128]{2,1,0:T(8,128)S(1)} all-to-all(f32[16,8,128]{2,1,0:T(8,128)S(1)} %get-tuple-element.47), channel_id=1, replica_groups=mesh['field'=2,'ccd'=16] {'ccd'}, dimensions={0} | all-to-all | bytes 131072 | tf_op jit(solution)/shard_map/all_to_all | solution.py:565
  75.3 2.8 %shard_map.69 = f32[128,1024]{1,0:T(8,128)} custom-call(f32[16,8,128]{2,1,0:T(8,128)S(1)} %all_to_all.10.fit_ref, f32[5,8,144,128]{3,2,1,0:T(8,128)S(1)} %get-tuple-element.27.cols_ref, f32[33,32,128]{2,1,0:T(8,128)S(1)} %get-tuple-element.48.sci_ref), custom_call_target="tpu_custom_call" | custom-call | flops 6553600 | bytes 1572864 | tf_op jit(solution)/shard_map/pallas_call | solution.py:567
  (24 shorter events, 0.1 us)
Async XLA Ops:
  4.4 7.6 %copy-start = (f32[2,128,1024]{2,1,0:T(8,128)S(1)}, f32[2,128,1024]{2,1,0:T(8,128)}, u32[]{:S(2)}) copy-start(f32[2,128,1024]{2,1,0:T(8,128)} %x_ref.3) | copy-start | bytes 3145732
  4.4 7.6 %copy-start.2 = (s32[16,32,1]{1,2,0:T(1,128)S(1)}, s32[16,32,1]{1,2,0:T(1,128)}, u32[]{:S(2)}) copy-start(s32[16,32,1]{1,2,0:T(1,128)} %param.9) | copy-start | bytes 6148
  4.4 7.6 %copy-start.3 = (s32[2,1,2]{2,1,0:T(1,128)S(1)}, s32[2,1,2]{2,1,0:T(1,128)}, u32[]{:S(2)}) copy-start(s32[2,1,2]{2,1,0:T(1,128)} %shift_ref.3) | copy-start | bytes 52
  4.5 7.6 %copy-start.4 = (f32[2,1,2]{2,1,0:T(1,128)S(1)}, f32[2,1,2]{2,1,0:T(1,128)}, u32[]{:S(2)}) copy-start(f32[2,1,2]{2,1,0:T(1,128)} %frac_ref.3) | copy-start | bytes 52
  4.5 20.4 %copy-start.12 = (s32[16,32]{1,0:T(8,128)S(1)}, s32[16,32]{1,0:T(8,128)}, u32[]{:S(2)}) copy-start(s32[16,32]{1,0:T(8,128)} %param.10) | copy-start | bytes 6148
  4.5 51.6 %all-to-all-start = ((f32[16,144,128]{2,1,0:T(8,128)}), f32[16,144,128]{2,1,0:T(8,128)S(1)}, u32[]{:S(2)}, u32[]{:S(2)}) async-start(f32[16,144,128]{2,1,0:T(8,128)} %shard_map.64), calls=%async_computation | async-start | bytes 2359296 | tf_op jit(solution)/shard_map/all_to_all | solution.py:490
  12.1 44.0 %copy-start.1 = (f32[25,80,128]{2,1,0:T(8,128)S(1)}, f32[25,80,128]{2,1,0:T(8,128)}, u32[]{:S(2)}) copy-start(f32[25,80,128]{2,1,0:T(8,128)} %constant.68.clone.coef_ref) | copy-start | bytes 3072004
  15.8 0.6 copy-start.5
  16.4 0.6 copy-start.6
  17.1 0.6 copy-start.7
  17.7 0.6 copy-start.8
  18.3 0.6 copy-start.9
  18.9 0.6 copy-start.10
  19.5 0.6 copy-start.11
  20.2 5.9 %collective-permute-start = (f32[128,128]{1,0:T(8,128)}, f32[128,128]{1,0:T(8,128)S(1)}, u32[]{:S(2)}, u32[]{:S(2)}) collective-permute-start(f32[128,128]{1,0:T(8,128)} %get-tuple-element.30), channel_id=1, source_target_pairs={{0,1},{1,0},{2,3},{3,2},{4,5},{5,4},{6,7},{7,6},{8,9},{9,8},{10,11... | collective-permute-start | bytes 196616 | tf_op jit(solution)/shard_map/ppermute | solution.py:494
  20.6 8.1 %collective-permute-start.1 = (f32[128,128]{1,0:T(8,128)}, f32[128,128]{1,0:T(8,128)S(1)}, u32[]{:S(2)}, u32[]{:S(2)}) collective-permute-start(f32[128,128]{1,0:T(8,128)} %get-tuple-element.31), channel_id=1, source_target_pairs={{0,2},{1,3},{2,0},{3,1},{4,6},{5,7},{6,4},{7,5},{8,10},{9,11},{10,... | collective-permute-start | bytes 196616 | tf_op jit(solution)/shard_map/ppermute | solution.py:494
  22.2 7.7 %collective-permute-start.2 = (f32[128,128]{1,0:T(8,128)}, f32[128,128]{1,0:T(8,128)S(1)}, u32[]{:S(2)}, u32[]{:S(2)}) collective-permute-start(f32[128,128]{1,0:T(8,128)} %get-tuple-element.32), channel_id=1, source_target_pairs={{0,3},{1,2},{2,1},{3,0},{4,7},{5,6},{6,5},{7,4},{8,11},{9,10},{10,... | collective-permute-start | bytes 196616 | tf_op jit(solution)/shard_map/ppermute | solution.py:494
  22.2 11.7 %collective-permute-start.3 = (f32[128,128]{1,0:T(8,128)}, f32[128,128]{1,0:T(8,128)S(1)}, u32[]{:S(2)}, u32[]{:S(2)}) collective-permute-start(f32[128,128]{1,0:T(8,128)} %get-tuple-element.33), channel_id=1, source_target_pairs={{0,4},{1,5},{2,6},{3,7},{4,0},{5,1},{6,2},{7,3},{8,12},{9,13},{10,... | collective-permute-start | bytes 196616 | tf_op jit(solution)/shard_map/ppermute | solution.py:494
  23.9 13.2 %collective-permute-start.4 = (f32[128,128]{1,0:T(8,128)}, f32[128,128]{1,0:T(8,128)S(1)}, u32[]{:S(2)}, u32[]{:S(2)}) collective-permute-start(f32[128,128]{1,0:T(8,128)} %get-tuple-element.34), channel_id=1, source_target_pairs={{0,5},{1,4},{2,7},{3,6},{4,1},{5,0},{6,3},{7,2},{8,13},{9,12},{10,... | collective-permute-start | bytes 196616 | tf_op jit(solution)/shard_map/ppermute | solution.py:494
  26.1 13.7 %collective-permute-start.5 = (f32[128,128]{1,0:T(8,128)}, f32[128,128]{1,0:T(8,128)S(1)}, u32[]{:S(2)}, u32[]{:S(2)}) collective-permute-start(f32[128,128]{1,0:T(8,128)} %copy-done.11), channel_id=1, source_target_pairs={{0,6},{1,7},{2,4},{3,5},{4,2},{5,3},{6,0},{7,1},{8,14},{9,15},{10,... | collective-permute-start | bytes 196616 | tf_op jit(solution)/shard_map/ppermute | solution.py:494
  28.7 13.2 %collective-permute-start.6 = (f32[128,128]{1,0:T(8,128)}, f32[128,128]{1,0:T(8,128)S(1)}, u32[]{:S(2)}, u32[]{:S(2)}) collective-permute-start(f32[128,128]{1,0:T(8,128)} %copy-done.10), channel_id=1, source_target_pairs={{0,7},{1,6},{2,5},{3,4},{4,3},{5,2},{6,1},{7,0},{8,15},{9,14},{10,... | collective-permute-start | bytes 196616 | tf_op jit(solution)/shard_map/ppermute | solution.py:494
  29.9 20.5 %collective-permute-start.7 = (f32[128,128]{1,0:T(8,128)}, f32[128,128]{1,0:T(8,128)S(1)}, u32[]{:S(2)}, u32[]{:S(2)}) collective-permute-start(f32[128,128]{1,0:T(8,128)} %copy-done.9), channel_id=1, source_target_pairs={{0,8},{1,9},{2,10},{3,11},{4,12},{5,13},{6,14},{7,15},{8,0},{9,1},... | collective-permute-start | bytes 196616 | tf_op jit(solution)/shard_map/ppermute | solution.py:494
  33.9 16.7 %collective-permute-start.8 = (f32[128,128]{1,0:T(8,128)}, f32[128,128]{1,0:T(8,128)S(1)}, u32[]{:S(2)}, u32[]{:S(2)}) collective-permute-start(f32[128,128]{1,0:T(8,128)} %copy-done.8), channel_id=1, source_target_pairs={{0,9},{1,8},{2,11},{3,10},{4,13},{5,12},{6,15},{7,14},{8,1},{9,0},... | collective-permute-start | bytes 196616 | tf_op jit(solution)/shard_map/ppermute | solution.py:494
  37.1 17.0 %collective-permute-start.9 = (f32[128,128]{1,0:T(8,128)}, f32[128,128]{1,0:T(8,128)S(1)}, u32[]{:S(2)}, u32[]{:S(2)}) collective-permute-start(f32[128,128]{1,0:T(8,128)} %copy-done.7), channel_id=1, source_target_pairs={{0,10},{1,11},{2,8},{3,9},{4,14},{5,15},{6,12},{7,13},{8,2},{9,3},... | collective-permute-start | bytes 196616 | tf_op jit(solution)/shard_map/ppermute | solution.py:494
  39.8 21.2 %collective-permute-start.10 = (f32[128,128]{1,0:T(8,128)}, f32[128,128]{1,0:T(8,128)S(1)}, u32[]{:S(2)}, u32[]{:S(2)}) collective-permute-start(f32[128,128]{1,0:T(8,128)} %copy-done.6), channel_id=1, source_target_pairs={{0,11},{1,10},{2,9},{3,8},{4,15},{5,14},{6,13},{7,12},{8,3},{9,2},... | collective-permute-start | bytes 196616 | tf_op jit(solution)/shard_map/ppermute | solution.py:494
  41.9 19.2 %collective-permute-start.11 = (f32[128,128]{1,0:T(8,128)}, f32[128,128]{1,0:T(8,128)S(1)}, u32[]{:S(2)}, u32[]{:S(2)}) collective-permute-start(f32[128,128]{1,0:T(8,128)} %copy-done.5), channel_id=1, source_target_pairs={{0,12},{1,13},{2,14},{3,15},{4,8},{5,9},{6,10},{7,11},{8,4},{9,5},... | collective-permute-start | bytes 196616 | tf_op jit(solution)/shard_map/ppermute | solution.py:494
  50.4 10.6 %collective-permute-start.12 = (f32[128,128]{1,0:T(8,128)S(1)}, f32[128,128]{1,0:T(8,128)S(1)}, u32[]{:S(2)}, u32[]{:S(2)}) collective-permute-start(f32[128,128]{1,0:T(8,128)S(1)} %get-tuple-element.42), channel_id=1, source_target_pairs={{0,13},{1,12},{2,15},{3,14},{4,9},{5,8},{6,11},{7,10},{8,5},{9,4},... | collective-permute-start | bytes 196616 | tf_op jit(solution)/shard_map/ppermute | solution.py:494
  50.7 12.3 %collective-permute-start.13 = (f32[128,128]{1,0:T(8,128)S(1)}, f32[128,128]{1,0:T(8,128)S(1)}, u32[]{:S(2)}, u32[]{:S(2)}) collective-permute-start(f32[128,128]{1,0:T(8,128)S(1)} %get-tuple-element.45), channel_id=1, source_target_pairs={{0,14},{1,15},{2,12},{3,13},{4,10},{5,11},{6,8},{7,9},{8,6},{9,7},... | collective-permute-start | bytes 196616 | tf_op jit(solution)/shard_map/ppermute | solution.py:494
  54.1 8.9 %collective-permute-start.14 = (f32[128,128]{1,0:T(8,128)S(1)}, f32[128,128]{1,0:T(8,128)S(1)}, u32[]{:S(2)}, u32[]{:S(2)}) collective-permute-start(f32[128,128]{1,0:T(8,128)S(1)} %get-tuple-element.46), channel_id=1, source_target_pairs={{0,15},{1,14},{2,13},{3,12},{4,11},{5,10},{6,9},{7,8},{8,7},{9,6},... | collective-permute-start | bytes 196616 | tf_op jit(solution)/shard_map/ppermute | solution.py:494

commit v4 on v3

--- a/solution.py
+++ b/solution.py
@@ -30,7 +30,7 @@
 MAX_PERMUTES = 32
 UNROLL = 4
 STEP = 4
-GROUP = 5
+GROUP = 13
 LATE = 2
 RHS_LANE = KB
 
@@ -170,7 +170,7 @@
                 outs[k][r * BR : (r + 1) * BR, :] = blocks[inv[k * cap + r]]
         return
 
-    @pl.loop(0, devices)
+    @pl.loop(0, devices, unroll=UNROLL)
     def _(p):
         before, after = jnp.maximum(p - 1, 0), jnp.minimum(p + 1, devices - 1)
         edges[p] = jnp.zeros((2 * SUB, LANES), jnp.float32)
@@ -189,7 +189,7 @@
         send(b).wait()
 
 
-def sum_blocks(devices, cap, paired, own, table_ref, ins, acc):
+def sum_blocks(devices, cap, partners, own, table_ref, ins, acc):
     acc[...] = jnp.zeros_like(acc)
 
     def add(chunk, c):
@@ -197,8 +197,8 @@
             slot = table_ref[c * cap + r]
             acc[slot] = acc[slot] + chunk[r * BR : (r + 1) * BR, :]
 
-    if paired:
-        for k, chunk in enumerate(ins):
+    if partners:
+        for k, chunk in zip(partners, ins):
             add(chunk, jnp.bitwise_xor(own, k))
     else:
 
@@ -208,7 +208,7 @@
 
 
 def template_kernel(
-    devices, cap, paired, own_ref, table_ref, ends_ref, edges_ref, coef_ref, *refs
+    devices, cap, own_ref, table_ref, ends_ref, edges_ref, coef_ref, *refs
 ):
     ins, (cols_ref, gram_ref, acc, far, gen, spec) = refs[:-6], refs[-6:]
     slabs, rows = cols_ref.shape[1], cols_ref.shape[2] - 2 * SUB
@@ -222,14 +222,11 @@
     tiles = rows // SUB
     lane = lane_ids()
     sub = lax.broadcasted_iota(jnp.int32, (SUB, LANES), 0)
-    sum_blocks(devices, cap, paired, own_ref[0], table_ref, ins, acc)
+    sum_blocks(devices, cap, (), own_ref[0], table_ref, ins, acc)
 
     for end in range(2):
         at = cap * BR + end * SUB
-        if paired:
-            strip = jnp.concatenate([chunk[at : at + SUB, :] for chunk in ins], axis=0)
-        else:
-            strip = ins[0][:, at : at + SUB, :].reshape(devices * SUB, LANES)
+        strip = ins[0][:, at : at + SUB, :].reshape(devices * SUB, LANES)
         edge = mm(edges_ref[end], strip)
         first = SUB - REACH if end == 0 else SUB + rows
         for j in range(slabs):
@@ -315,10 +312,10 @@
     return packed
 
 
-def science_kernel(devices, cap, paired, own_ref, table_ref, cols_ref, *refs):
+def science_kernel(devices, cap, partners, own_ref, table_ref, cols_ref, *refs):
     ins, (out, sums_ref) = refs[:-2], refs[-2:]
     slabs, rows = cols_ref.shape[1], cols_ref.shape[2] - 2 * SUB
-    sum_blocks(devices, cap, paired, own_ref[0], table_ref, ins, out)
+    sum_blocks(devices, cap, partners, own_ref[0], table_ref, ins, out)
     sums_ref[...] = jnp.zeros_like(sums_ref)
 
     @pl.loop(0, slabs)
@@ -338,15 +335,15 @@
 
 
 def late_kernel(
-    first, cap, own_ref, table_ref, cols_ref, gram_ref, early_ref, sums_ref, *refs
+    partners, cap, own_ref, table_ref, cols_ref, gram_ref, early_ref, sums_ref, *refs
 ):
     ins, (out, fit_ref, all_sums) = refs[:-3], refs[-3:]
     slabs = cols_ref.shape[1]
     out[...] = early_ref[...]
     sums = [sums_ref[i] for i in range(KB)]
-    for n, chunk in enumerate(ins):
+    for k, chunk in zip(partners, ins):
         for r in range(cap):
-            slot = table_ref[jnp.bitwise_xor(own_ref[0], first + n) * cap + r]
+            slot = table_ref[jnp.bitwise_xor(own_ref[0], k) * cap + r]
             out[slot] = out[slot] + chunk[r * BR : (r + 1) * BR, :]
             share = (slot < NB).astype(jnp.float32)
             inside = jnp.minimum(slot, NB - 1)
@@ -385,7 +382,8 @@
     work = jnp.where(lane < size, jnp.where(diagonal, work + ridge, work), 0.0)
     for base in range(0, KB, GROUP):
         group = [
-            jnp.broadcast_to(work[:, i : i + 1], (size, LANES)) for i in range(base, base + GROUP)
+            jnp.broadcast_to(work[:, i : i + 1], (size, LANES))
+            for i in range(base, min(base + GROUP, KB))
         ]
         for k, column in enumerate(group):
             i = base + k
@@ -433,6 +431,10 @@
 
 def by_permutes(devices):
     return devices <= MAX_PERMUTES and devices & (devices - 1) == 0
+
+
+def exchange_order(devices):
+    return tuple(range(1, devices))
 
 
 def gram_table():
@@ -529,7 +531,7 @@
     count, coef = gram_table()
     at_ends = jnp.stack([owner == 0, owner == devices - 1]).astype(jnp.int32)
     shifts, gram = call(
-        functools.partial(template_kernel, devices, cap, False),
+        functools.partial(template_kernel, devices, cap),
         [f32(KSIDE, slabs, rows + 2 * SUB, LANES), f32(size, LANES)],
         [SMEM, SMEM, SMEM] + [VMEM] * (2 + len(template_in)),
         [
@@ -542,24 +544,26 @@
         pixels * 8,
     )(own, table, at_ends, edges, jnp.asarray(coef), *template_in)
 
-    first = devices - LATE if paired else len(science_in)
+    order = (0, *exchange_order(devices)) if paired else ()
+    early, late = (order[:-LATE], order[-LATE:]) if paired else ((), ())
+    early_in = [science_in[k] for k in early] if paired else science_in
     science, sums = call(
-        functools.partial(science_kernel, devices, cap, paired),
+        functools.partial(science_kernel, devices, cap, early),
         [f32(NB + 1, BR, BC), f32(size, SUB, LANES)],
-        [SMEM, SMEM, VMEM] + [VMEM] * first,
+        [SMEM, SMEM, VMEM] + [VMEM] * len(early_in),
         [],
         pixels * 2 * KB,
         pixels * 16,
-    )(own, table, shifts, *science_in[:first])
+    )(own, table, shifts, *early_in)
     if paired:
         science, fit = call(
-            functools.partial(late_kernel, first, cap),
+            functools.partial(late_kernel, late, cap),
             [f32(NB + 1, BR, BC), f32(devices, SUB, LANES)],
             [SMEM, SMEM] + [VMEM] * (4 + LATE),
             [pltpu.VMEM((size, SUB, LANES), jnp.float32)],
             pixels * KB // 2,
             pixels * 8,
-        )(own, table, shifts, gram, science, sums, *science_in[first:])
+        )(own, table, shifts, gram, science, sums, *[science_in[k] for k in late])
     else:
         fit = call(fit_kernel, f32(devices, SUB, LANES), [VMEM] * 2, [], 10**5, 10**5)(gram, sums)
     fit = lax.all_to_all(fit, "ccd", split_axis=0, concat_axis=0, tiled=True)

time: 78.4 us -> 78.1 us (level)
  no operation moved by 1% of the time
where the time goes in v4:
time: 78.1 us; the launch traced here: 77.9 us
  starting transfers between devices  28.5 us (36%)
  Pallas kernels  18.5 us (24%)
  waiting for transfers between devices  12.9 us (17%)
  blocking collectives  11.4 us (15%)
  local copies, waits for them, and re-layouts  4.92 us (6%)
  other arithmetic  1.42 us (2%)
    ppermute x15, starting transfers between devices, exchanged(): lax.ppermute(chunks[k], 'ccd', [(i, i ^ k) for i in range(devices)])  20.9 us
    ppermute x15, waiting for transfers between devices, exchanged(): lax.ppermute(chunks[k], 'ccd', [(i, i ^ k) for i in range(devices)])  12.9 us
    all_to_all x1, blocking collectives, body(): fit = lax.all_to_all(fit, 'ccd', split_axis=0, concat_axis=0, tiled=True)  11.4 us
    pallas_call x2, Pallas kernels, warped(): call(functools.partial(warp_kernel, visit, devices, cap, paired), packed,...  8.1 us
    all_to_all x1, starting transfers between devices, exchanged(): lax.all_to_all(chunks[0], 'ccd', split_axis=0, concat_axis=0, tiled=True)  7.53 us
    pallas_call x1, Pallas kernels, body(): call(functools.partial(template_kernel, devices, cap), [f32(KSIDE, slabs,...  4.95 us
    unnamed x26, local copies, waits for them, and re-layouts  4.35 us
    pallas_call x1, Pallas kernels, body(): call(difference_kernel, f32(rows, columns), [VMEM] * 3, [pltpu.VMEM((rows...  2.6 us
  transfers between devices with their start and end apart: 16, of which 5 were waited for; matrix products, arithmetic and copies ran while one was open for 3% of the time, Pallas kernels for 14%

profile of v4, /device:TPU:0, one launch (start us, length us, event | category | flops | bytes accessed | tf_op | source)
XLA Modules:
  0.0 77.9 jit_solution(2718107842984842974)
XLA Ops:
  0.0 4.3 %shard_map.64 = f32[16,144,128]{2,1,0:T(8,128)} custom-call(s32[1]{0:T(128)} %bitcast.own_ref, s32[16,32]{1,0:T(8,128)} %bitcast.8, s32[2,1,2]{2,1,0:T(1,128)} %shift_ref.3, f32[2,1,2]{2,1,0:T(1,128)} %frac_ref.3, f32[2,128,1024]{2,1,0:T(8,128)} %x_ref.3), custom_call_target="tpu_custom_call" | custom-call | flops 5242880 | bytes 1572864 | tf_op jit(solution)/shard_map/pallas_call | solution.py:470
  4.4 0.0 copy-start
  4.4 0.0 copy-start.2
  4.4 0.0 copy-start.3
  4.4 0.0 copy-start.4
  4.4 0.0 copy-start.12
  4.4 7.5 %all-to-all-start = ((f32[16,144,128]{2,1,0:T(8,128)}), f32[16,144,128]{2,1,0:T(8,128)S(1)}, u32[]{:S(2)}, u32[]{:S(2)}) async-start(f32[16,144,128]{2,1,0:T(8,128)} %shard_map.64), calls=%async_computation | async-start | bytes 2359296 | tf_op jit(solution)/shard_map/all_to_all | solution.py:492
  12.0 0.0 copy-start.1
  12.0 3.8 %shard_map.66 = (f32[128,128]{1,0:T(8,128)S(1)}, f32[128,128]{1,0:T(8,128)}, f32[128,128]{1,0:T(8,128)}, f32[128,128]{1,0:T(8,128)}, f32[128,128]{1,0:T(8,128)},...) custom-call(s32[1]{0:T(128)} %bitcast.own_ref, ...), custom_call_target="tpu_custom_call" | custom-call | flops 5242880 | bytes 1572864 | tf_op jit(solution)/shard_map/pallas_call | solution.py:470
  15.8 0.6 copy-done.5
  16.4 0.6 copy-done.6
  17.0 0.6 copy-done.7
  17.6 0.6 copy-done.8
  18.2 0.6 copy-done.9
  18.9 0.6 copy-done.10
  19.5 0.6 copy-done.11
  20.1 0.4 collective-permute-start
  20.5 1.6 %collective-permute-start.1 = (f32[128,128]{1,0:T(8,128)}, f32[128,128]{1,0:T(8,128)S(1)}, u32[]{:S(2)}, u32[]{:S(2)}) collective-permute-start(f32[128,128]{1,0:T(8,128)} %get-tuple-element.31), channel_id=1, source_target_pairs={{0,2},{1,3},{2,0},{3,1},{4,6},{5,7},{6,4},{7,5},{8,10},{9,11},{10,... | collective-permute-start | bytes 196616 | tf_op jit(solution)/shard_map/ppermute | solution.py:496
  22.1 0.0 collective-permute-start.2
  22.1 1.7 %collective-permute-start.3 = (f32[128,128]{1,0:T(8,128)}, f32[128,128]{1,0:T(8,128)S(1)}, u32[]{:S(2)}, u32[]{:S(2)}) collective-permute-start(f32[128,128]{1,0:T(8,128)} %get-tuple-element.33), channel_id=1, source_target_pairs={{0,4},{1,5},{2,6},{3,7},{4,0},{5,1},{6,2},{7,3},{8,12},{9,13},{10,... | collective-permute-start | bytes 196616 | tf_op jit(solution)/shard_map/ppermute | solution.py:496
  23.9 0.1 collective-permute-start.4
  24.0 0.5 convert_reduce_fusion
  24.5 0.3 fusion.4
  24.8 0.3 select_reduce_fusion.1
  25.1 0.1 copy.10
  25.2 0.1 copy.11
  25.3 0.1 broadcast_compare_fusion.5
  25.3 0.1 broadcast_compare_fusion.1
  25.5 0.1 broadcast_and_fusion.1
  25.6 0.1 copy.9
  25.6 0.1 select_n.76.table_ref
  25.8 0.1 copy.13
  25.9 0.1 convert_element_type.30
  25.9 0.1 copy.12
  26.0 0.0 collective-permute-done.refs_1_
  26.0 2.6 %collective-permute-start.5 = (f32[128,128]{1,0:T(8,128)}, f32[128,128]{1,0:T(8,128)S(1)}, u32[]{:S(2)}, u32[]{:S(2)}) collective-permute-start(f32[128,128]{1,0:T(8,128)} %copy-done.11), channel_id=1, source_target_pairs={{0,6},{1,7},{2,4},{3,5},{4,2},{5,3},{6,0},{7,1},{8,14},{9,15},{10,... | collective-permute-start | bytes 196616 | tf_op jit(solution)/shard_map/ppermute | solution.py:496
  28.6 0.0 collective-permute-done.1.refs_2_
  28.6 0.1 collective-permute-start.6
  28.7 1.1 %collective-permute-done.2.refs_3_ = f32[128,128]{1,0:T(8,128)S(1)} collective-permute-done((f32[128,128]{1,0:T(8,128)}, f32[128,128]{1,0:T(8,128)S(1)}, u32[]{:S(2)}, u32[]{:S(2)}) %collective-permute-start.2) | collective-permute-done | bytes 65568 | tf_op jit(solution)/shard_map/ppermute | solution.py:496
  29.8 1.4 %collective-permute-start.7 = (f32[128,128]{1,0:T(8,128)}, f32[128,128]{1,0:T(8,128)S(1)}, u32[]{:S(2)}, u32[]{:S(2)}) collective-permute-start(f32[128,128]{1,0:T(8,128)} %copy-done.9), channel_id=1, source_target_pairs={{0,8},{1,9},{2,10},{3,11},{4,12},{5,13},{6,14},{7,15},{8,0},{9,1},... | collective-permute-start | bytes 196616 | tf_op jit(solution)/shard_map/ppermute | solution.py:496
  31.3 2.6 %collective-permute-done.3.refs_4_ = f32[128,128]{1,0:T(8,128)S(1)} collective-permute-done((f32[128,128]{1,0:T(8,128)}, f32[128,128]{1,0:T(8,128)S(1)}, u32[]{:S(2)}, u32[]{:S(2)}) %collective-permute-start.3) | collective-permute-done | bytes 65568 | tf_op jit(solution)/shard_map/ppermute | solution.py:496
  33.9 3.2 %collective-permute-start.8 = (f32[128,128]{1,0:T(8,128)}, f32[128,128]{1,0:T(8,128)S(1)}, u32[]{:S(2)}, u32[]{:S(2)}) collective-permute-start(f32[128,128]{1,0:T(8,128)} %copy-done.8), channel_id=1, source_target_pairs={{0,9},{1,8},{2,11},{3,10},{4,13},{5,12},{6,15},{7,14},{8,1},{9,0},... | collective-permute-start | bytes 196616 | tf_op jit(solution)/shard_map/ppermute | solution.py:496
  37.1 0.0 collective-permute-done.4.refs_5_
  37.1 2.6 %collective-permute-start.9 = (f32[128,128]{1,0:T(8,128)}, f32[128,128]{1,0:T(8,128)S(1)}, u32[]{:S(2)}, u32[]{:S(2)}) collective-permute-start(f32[128,128]{1,0:T(8,128)} %copy-done.7), channel_id=1, source_target_pairs={{0,10},{1,11},{2,8},{3,9},{4,14},{5,15},{6,12},{7,13},{8,2},{9,3},... | collective-permute-start | bytes 196616 | tf_op jit(solution)/shard_map/ppermute | solution.py:496
  39.7 0.0 collective-permute-done.5.refs_6_
  39.7 2.1 %collective-permute-start.10 = (f32[128,128]{1,0:T(8,128)}, f32[128,128]{1,0:T(8,128)S(1)}, u32[]{:S(2)}, u32[]{:S(2)}) collective-permute-start(f32[128,128]{1,0:T(8,128)} %copy-done.6), channel_id=1, source_target_pairs={{0,11},{1,10},{2,9},{3,8},{4,15},{5,14},{6,13},{7,12},{8,3},{9,2},... | collective-permute-start | bytes 196616 | tf_op jit(solution)/shard_map/ppermute | solution.py:496
  41.8 0.0 collective-permute-done.6.refs_7_
  41.8 0.1 collective-permute-start.11
  41.9 8.4 %collective-permute-done.7.refs_8_ = f32[128,128]{1,0:T(8,128)S(1)} collective-permute-done((f32[128,128]{1,0:T(8,128)}, f32[128,128]{1,0:T(8,128)S(1)}, u32[]{:S(2)}, u32[]{:S(2)}) %collective-permute-start.7) | collective-permute-done | bytes 65568 | tf_op jit(solution)/shard_map/ppermute | solution.py:496
  50.4 0.0 collective-permute-start.12
  50.4 0.3 collective-permute-done.8.refs_9_
  50.6 3.0 %collective-permute-start.13 = (f32[128,128]{1,0:T(8,128)S(1)}, f32[128,128]{1,0:T(8,128)S(1)}, u32[]{:S(2)}, u32[]{:S(2)}) collective-permute-start(f32[128,128]{1,0:T(8,128)S(1)} %get-tuple-element.45), channel_id=1, source_target_pairs={{0,14},{1,15},{2,12},{3,13},{4,10},{5,11},{6,8},{7,9},{8,6},{9,7},... | collective-permute-start | bytes 196616 | tf_op jit(solution)/shard_map/ppermute | solution.py:496
  53.7 0.4 collective-permute-done.9.refs_10_
  54.1 1.9 %collective-permute-start.14 = (f32[128,128]{1,0:T(8,128)S(1)}, f32[128,128]{1,0:T(8,128)S(1)}, u32[]{:S(2)}, u32[]{:S(2)}) collective-permute-start(f32[128,128]{1,0:T(8,128)S(1)} %get-tuple-element.46), channel_id=1, source_target_pairs={{0,15},{1,14},{2,13},{3,12},{4,11},{5,10},{6,9},{7,8},{8,7},{9,6},... | collective-permute-start | bytes 196616 | tf_op jit(solution)/shard_map/ppermute | solution.py:496
  55.9 0.1 add_convert_fusion.1.ends_ref
  56.0 0.0 all-to-all-done.refs_0_
  56.0 5.0 %shard_map.65 = (f32[5,8,144,128]{3,2,1,0:T(8,128)S(1)}, f32[32,128]{1,0:T(8,128)S(1)}) custom-call(s32[1]{0:T(128)} %bitcast.own_ref, s32[64]{0:T(128)S(1)} %select_n.76.table_ref, s32[2]{0:T(128)S(1)} %add_convert_fusion.1.ends_ref, f32[2,16,128]{2,1,0:T(8,128)S(1)} %add_convert_fusion.edges_ref, f32[25,80,128]{2,1,0:T(8,128)S(1)} %copy-done.1, ...), custom_call_target="tpu_custom_call" | custom-call | flops 10747904 | bytes 1048576 | tf_op jit(solution)/shard_map/pallas_call | solution.py:533
  61.0 0.0 collective-permute-done.10.refs_11_
  61.0 0.0 collective-permute-done.11.refs_12_
  61.0 0.0 collective-permute-done.12.refs_13_
  61.0 1.9 %shard_map.67 = (f32[33,32,128]{2,1,0:T(8,128)S(1)}, f32[32,8,128]{2,1,0:T(8,128)S(1)}) custom-call(s32[1]{0:T(128)} %bitcast.own_ref, s32[64]{0:T(128)S(1)} %select_n.76.table_ref, f32[5,8,144,128]{3,2,1,0:T(8,128)S(1)} %get-tuple-element.27.cols_ref, f32[128,128]{1,0:T(8,128)S(1)} %get-tuple-element.29.refs_0_, ...), custom_call_target="tpu_custom_call" | custom-call | flops 6553600 | bytes 2097152 | tf_op jit(solution)/shard_map/pallas_call | solution.py:550
  62.9 0.9 %shard_map.68 = (f32[33,32,128]{2,1,0:T(8,128)S(1)}, f32[16,8,128]{2,1,0:T(8,128)S(1)}) custom-call(s32[1]{0:T(128)} %bitcast.own_ref, s32[64]{0:T(128)S(1)} %select_n.76.table_ref, f32[5,8,144,128]{3,2,1,0:T(8,128)S(1)} %get-tuple-element.27.cols_ref, f32[32,128]{1,0:T(8,128)S(1)} %get-tuple-element.28.gram_ref, ...), custom_call_target="tpu_custom_call" | custom-call | flops 1638400 | bytes 1048576 | tf_op jit(solution)/shard_map/pallas_call | solution.py:559
  63.9 11.4 %all_to_all.10.fit_ref = f32[16,8,128]{2,1,0:T(8,128)S(1)} all-to-all(f32[16,8,128]{2,1,0:T(8,128)S(1)} %get-tuple-element.47), channel_id=1, replica_groups=mesh['field'=2,'ccd'=16] {'ccd'}, dimensions={0} | all-to-all | bytes 131072 | tf_op jit(solution)/shard_map/all_to_all | solution.py:569
  75.3 2.6 %shard_map.69 = f32[128,1024]{1,0:T(8,128)} custom-call(f32[16,8,128]{2,1,0:T(8,128)S(1)} %all_to_all.10.fit_ref, f32[5,8,144,128]{3,2,1,0:T(8,128)S(1)} %get-tuple-element.27.cols_ref, f32[33,32,128]{2,1,0:T(8,128)S(1)} %get-tuple-element.48.sci_ref), custom_call_target="tpu_custom_call" | custom-call | flops 6553600 | bytes 1572864 | tf_op jit(solution)/shard_map/pallas_call | solution.py:571
  (24 shorter events, 0.1 us)
Async XLA Ops:
  4.4 7.6 %copy-start = (f32[2,128,1024]{2,1,0:T(8,128)S(1)}, f32[2,128,1024]{2,1,0:T(8,128)}, u32[]{:S(2)}) copy-start(f32[2,128,1024]{2,1,0:T(8,128)} %x_ref.3) | copy-start | bytes 3145732
  4.4 7.6 %copy-start.2 = (s32[16,32,1]{1,2,0:T(1,128)S(1)}, s32[16,32,1]{1,2,0:T(1,128)}, u32[]{:S(2)}) copy-start(s32[16,32,1]{1,2,0:T(1,128)} %param.9) | copy-start | bytes 6148
  4.4 7.6 %copy-start.3 = (s32[2,1,2]{2,1,0:T(1,128)S(1)}, s32[2,1,2]{2,1,0:T(1,128)}, u32[]{:S(2)}) copy-start(s32[2,1,2]{2,1,0:T(1,128)} %shift_ref.3) | copy-start | bytes 52
  4.4 7.6 %copy-start.4 = (f32[2,1,2]{2,1,0:T(1,128)S(1)}, f32[2,1,2]{2,1,0:T(1,128)}, u32[]{:S(2)}) copy-start(f32[2,1,2]{2,1,0:T(1,128)} %frac_ref.3) | copy-start | bytes 52
  4.4 20.4 %copy-start.12 = (s32[16,32]{1,0:T(8,128)S(1)}, s32[16,32]{1,0:T(8,128)}, u32[]{:S(2)}) copy-start(s32[16,32]{1,0:T(8,128)} %param.10) | copy-start | bytes 6148
  4.4 51.6 %all-to-all-start = ((f32[16,144,128]{2,1,0:T(8,128)}), f32[16,144,128]{2,1,0:T(8,128)S(1)}, u32[]{:S(2)}, u32[]{:S(2)}) async-start(f32[16,144,128]{2,1,0:T(8,128)} %shard_map.64), calls=%async_computation | async-start | bytes 2359296 | tf_op jit(solution)/shard_map/all_to_all | solution.py:492
  12.0 44.0 %copy-start.1 = (f32[25,80,128]{2,1,0:T(8,128)S(1)}, f32[25,80,128]{2,1,0:T(8,128)}, u32[]{:S(2)}) copy-start(f32[25,80,128]{2,1,0:T(8,128)} %constant.68.clone.coef_ref) | copy-start | bytes 3072004
  15.8 0.6 copy-start.5
  16.4 0.6 copy-start.6
  17.0 0.6 copy-start.7
  17.6 0.6 copy-start.8
  18.2 0.6 copy-start.9
  18.9 0.6 copy-start.10
  19.5 0.6 copy-start.11
  20.1 5.9 %collective-permute-start = (f32[128,128]{1,0:T(8,128)}, f32[128,128]{1,0:T(8,128)S(1)}, u32[]{:S(2)}, u32[]{:S(2)}) collective-permute-start(f32[128,128]{1,0:T(8,128)} %get-tuple-element.30), channel_id=1, source_target_pairs={{0,1},{1,0},{2,3},{3,2},{4,5},{5,4},{6,7},{7,6},{8,9},{9,8},{10,11... | collective-permute-start | bytes 196616 | tf_op jit(solution)/shard_map/ppermute | solution.py:496
  20.5 8.1 %collective-permute-start.1 = (f32[128,128]{1,0:T(8,128)}, f32[128,128]{1,0:T(8,128)S(1)}, u32[]{:S(2)}, u32[]{:S(2)}) collective-permute-start(f32[128,128]{1,0:T(8,128)} %get-tuple-element.31), channel_id=1, source_target_pairs={{0,2},{1,3},{2,0},{3,1},{4,6},{5,7},{6,4},{7,5},{8,10},{9,11},{10,... | collective-permute-start | bytes 196616 | tf_op jit(solution)/shard_map/ppermute | solution.py:496
  22.1 7.7 %collective-permute-start.2 = (f32[128,128]{1,0:T(8,128)}, f32[128,128]{1,0:T(8,128)S(1)}, u32[]{:S(2)}, u32[]{:S(2)}) collective-permute-start(f32[128,128]{1,0:T(8,128)} %get-tuple-element.32), channel_id=1, source_target_pairs={{0,3},{1,2},{2,1},{3,0},{4,7},{5,6},{6,5},{7,4},{8,11},{9,10},{10,... | collective-permute-start | bytes 196616 | tf_op jit(solution)/shard_map/ppermute | solution.py:496
  22.1 11.7 %collective-permute-start.3 = (f32[128,128]{1,0:T(8,128)}, f32[128,128]{1,0:T(8,128)S(1)}, u32[]{:S(2)}, u32[]{:S(2)}) collective-permute-start(f32[128,128]{1,0:T(8,128)} %get-tuple-element.33), channel_id=1, source_target_pairs={{0,4},{1,5},{2,6},{3,7},{4,0},{5,1},{6,2},{7,3},{8,12},{9,13},{10,... | collective-permute-start | bytes 196616 | tf_op jit(solution)/shard_map/ppermute | solution.py:496
  23.9 13.2 %collective-permute-start.4 = (f32[128,128]{1,0:T(8,128)}, f32[128,128]{1,0:T(8,128)S(1)}, u32[]{:S(2)}, u32[]{:S(2)}) collective-permute-start(f32[128,128]{1,0:T(8,128)} %get-tuple-element.34), channel_id=1, source_target_pairs={{0,5},{1,4},{2,7},{3,6},{4,1},{5,0},{6,3},{7,2},{8,13},{9,12},{10,... | collective-permute-start | bytes 196616 | tf_op jit(solution)/shard_map/ppermute | solution.py:496
  26.0 13.7 %collective-permute-start.5 = (f32[128,128]{1,0:T(8,128)}, f32[128,128]{1,0:T(8,128)S(1)}, u32[]{:S(2)}, u32[]{:S(2)}) collective-permute-start(f32[128,128]{1,0:T(8,128)} %copy-done.11), channel_id=1, source_target_pairs={{0,6},{1,7},{2,4},{3,5},{4,2},{5,3},{6,0},{7,1},{8,14},{9,15},{10,... | collective-permute-start | bytes 196616 | tf_op jit(solution)/shard_map/ppermute | solution.py:496
  28.6 13.2 %collective-permute-start.6 = (f32[128,128]{1,0:T(8,128)}, f32[128,128]{1,0:T(8,128)S(1)}, u32[]{:S(2)}, u32[]{:S(2)}) collective-permute-start(f32[128,128]{1,0:T(8,128)} %copy-done.10), channel_id=1, source_target_pairs={{0,7},{1,6},{2,5},{3,4},{4,3},{5,2},{6,1},{7,0},{8,15},{9,14},{10,... | collective-permute-start | bytes 196616 | tf_op jit(solution)/shard_map/ppermute | solution.py:496
  29.8 20.5 %collective-permute-start.7 = (f32[128,128]{1,0:T(8,128)}, f32[128,128]{1,0:T(8,128)S(1)}, u32[]{:S(2)}, u32[]{:S(2)}) collective-permute-start(f32[128,128]{1,0:T(8,128)} %copy-done.9), channel_id=1, source_target_pairs={{0,8},{1,9},{2,10},{3,11},{4,12},{5,13},{6,14},{7,15},{8,0},{9,1},... | collective-permute-start | bytes 196616 | tf_op jit(solution)/shard_map/ppermute | solution.py:496
  33.9 16.7 %collective-permute-start.8 = (f32[128,128]{1,0:T(8,128)}, f32[128,128]{1,0:T(8,128)S(1)}, u32[]{:S(2)}, u32[]{:S(2)}) collective-permute-start(f32[128,128]{1,0:T(8,128)} %copy-done.8), channel_id=1, source_target_pairs={{0,9},{1,8},{2,11},{3,10},{4,13},{5,12},{6,15},{7,14},{8,1},{9,0},... | collective-permute-start | bytes 196616 | tf_op jit(solution)/shard_map/ppermute | solution.py:496
  37.1 17.0 %collective-permute-start.9 = (f32[128,128]{1,0:T(8,128)}, f32[128,128]{1,0:T(8,128)S(1)}, u32[]{:S(2)}, u32[]{:S(2)}) collective-permute-start(f32[128,128]{1,0:T(8,128)} %copy-done.7), channel_id=1, source_target_pairs={{0,10},{1,11},{2,8},{3,9},{4,14},{5,15},{6,12},{7,13},{8,2},{9,3},... | collective-permute-start | bytes 196616 | tf_op jit(solution)/shard_map/ppermute | solution.py:496
  39.7 21.2 %collective-permute-start.10 = (f32[128,128]{1,0:T(8,128)}, f32[128,128]{1,0:T(8,128)S(1)}, u32[]{:S(2)}, u32[]{:S(2)}) collective-permute-start(f32[128,128]{1,0:T(8,128)} %copy-done.6), channel_id=1, source_target_pairs={{0,11},{1,10},{2,9},{3,8},{4,15},{5,14},{6,13},{7,12},{8,3},{9,2},... | collective-permute-start | bytes 196616 | tf_op jit(solution)/shard_map/ppermute | solution.py:496
  41.8 19.2 %collective-permute-start.11 = (f32[128,128]{1,0:T(8,128)}, f32[128,128]{1,0:T(8,128)S(1)}, u32[]{:S(2)}, u32[]{:S(2)}) collective-permute-start(f32[128,128]{1,0:T(8,128)} %copy-done.5), channel_id=1, source_target_pairs={{0,12},{1,13},{2,14},{3,15},{4,8},{5,9},{6,10},{7,11},{8,4},{9,5},... | collective-permute-start | bytes 196616 | tf_op jit(solution)/shard_map/ppermute | solution.py:496
  50.4 10.6 %collective-permute-start.12 = (f32[128,128]{1,0:T(8,128)S(1)}, f32[128,128]{1,0:T(8,128)S(1)}, u32[]{:S(2)}, u32[]{:S(2)}) collective-permute-start(f32[128,128]{1,0:T(8,128)S(1)} %get-tuple-element.42), channel_id=1, source_target_pairs={{0,13},{1,12},{2,15},{3,14},{4,9},{5,8},{6,11},{7,10},{8,5},{9,4},... | collective-permute-start | bytes 196616 | tf_op jit(solution)/shard_map/ppermute | solution.py:496
  50.6 12.3 %collective-permute-start.13 = (f32[128,128]{1,0:T(8,128)S(1)}, f32[128,128]{1,0:T(8,128)S(1)}, u32[]{:S(2)}, u32[]{:S(2)}) collective-permute-start(f32[128,128]{1,0:T(8,128)S(1)} %get-tuple-element.45), channel_id=1, source_target_pairs={{0,14},{1,15},{2,12},{3,13},{4,10},{5,11},{6,8},{7,9},{8,6},{9,7},... | collective-permute-start | bytes 196616 | tf_op jit(solution)/shard_map/ppermute | solution.py:496
  54.1 8.9 %collective-permute-start.14 = (f32[128,128]{1,0:T(8,128)S(1)}, f32[128,128]{1,0:T(8,128)S(1)}, u32[]{:S(2)}, u32[]{:S(2)}) collective-permute-start(f32[128,128]{1,0:T(8,128)S(1)} %get-tuple-element.46), channel_id=1, source_target_pairs={{0,15},{1,14},{2,13},{3,12},{4,11},{5,10},{6,9},{7,8},{8,7},{9,6},... | collective-permute-start | bytes 196616 | tf_op jit(solution)/shard_map/ppermute | solution.py:496
